TPU v7x, 128 devices: a whole 4x4x4 slice. The times are simulated.
128 devices in a mesh: gx: 16 (over x, z), gy: 8 (over y, core).
Axes of the slice: x: 4, y: 4, z: 4, core: 2. Of those that a mesh axis runs over, the one named last changes fastest.
Arguments:
- states: bfloat16 [2, 64, 8, 128, 1024], P(None, None, None, 'gx', 'gy'), may hold values from -6 to 6, as said below
- class_map: int32 [8, 128, 1024], P(None, 'gx', 'gy'), may hold values from 0 to 7
- perm_table: float32 [8], replicated, may hold values from 0.05 to 1
- candidates: int32 [16, 8, 64], replicated, may hold values from 0 to 8191, as said below
- merge_order: int32 [127, 128], replicated, may hold values from 0 to 127, each once within a row
Outputs:
- flux: bfloat16 [64, 8, 128, 1024], P(None, None, 'gx', 'gy')
- kept_rows: float32 [127, 64, 64], replicated
Inputs may be any that keep to these rules, and one draw needn't show every extreme that they name: states[0] is pressure; states[1] is water saturation, between 0.05 and 0.95. `candidates`: each tile's 64 entries are distinct cell numbers (z * 8 + x) * 128 + y of that tile's own cells. `merge_order`: each row is a permutation of 0 to 127.
All inputs are finite; a program needn't handle non-finite values.
Results may differ from a plain program's by a relative error of at most 0.001.
Values may be sent and summed in bfloat16 or wider, within the bound.
No kernel may reach another device: no remote copies, remote signals or barrier semaphores. Data moves between devices by JAX's collectives and lax.ppermute only.
A program may use at most 128 MiB of HBM per device.

v0:
```python
import jax
import jax.numpy as jnp
from jax import lax
from jax.sharding import PartitionSpec as P


def padded_2(block, sides, width):
    for axis, dim in sides:
        count = lax.axis_size(axis)
        forward = [(i, i + 1) for i in range(count - 1)]
        forward.append((count - 1, 0))
        backward = [(target, source) for source, target in forward]
        low = lax.ppermute(
            lax.slice_in_dim(block, block.shape[dim] - width, None, axis=dim), axis, forward
        )
        high = lax.ppermute(lax.slice_in_dim(block, 0, width, axis=dim), axis, backward)
        block = jnp.concatenate([low, block, high], axis=dim)
    return block


def face_term(p_here, m_here, k_here, p_next, m_next, k_next):
    transmit = 2.0 * k_here * k_next / (k_here + k_next)
    return transmit * (0.5 * (m_here + m_next)) * (p_next - p_here)


def kept_sources(tile_count, kept_count, merge_order):
    level_ids = jnp.arange(tile_count * kept_count, dtype=jnp.int32).reshape(tile_count, kept_count)
    offset = 0
    kept_list = []
    for level_num in range(tile_count.bit_length() - 1):
        groups = level_ids.shape[0] // 2
        paired = level_ids.reshape(groups, 2 * kept_count)
        node_order = merge_order[offset : offset + groups, :kept_count]
        level_ids = jnp.take_along_axis(paired, node_order, axis=1)
        kept_list.append(level_ids)
        offset = offset + groups
    return jnp.concatenate(kept_list, axis=0)


def neighbour(centre, padded, which):
    if which == 0:
        return centre
    if which in (1, 2):
        row = lax.broadcasted_iota(jnp.int32, centre.shape, centre.ndim - 2)
        height = centre.shape[-2]
        if which == 1:
            return jnp.where(row == height - 1, padded[..., -1:, 1:-1], jnp.roll(centre, -1, -2))
        return jnp.where(row == 0, padded[..., :1, 1:-1], jnp.roll(centre, 1, -2))
    if which in (3, 4):
        column = lax.broadcasted_iota(jnp.int32, centre.shape, centre.ndim - 1)
        width_y = centre.shape[-1]
        if which == 3:
            return jnp.where(
                column == width_y - 1, padded[..., 1:-1, -1:], jnp.roll(centre, -1, -1)
            )
        return jnp.where(column == 0, padded[..., 1:-1, :1], jnp.roll(centre, 1, -1))
    zero_plane = jnp.zeros(centre.shape[:-3] + (1,) + centre.shape[-2:], centre.dtype)
    if which == 5:
        return jnp.concatenate([centre[..., 1:, :, :], zero_plane], axis=-3)
    return jnp.concatenate([zero_plane, centre[..., :-1, :, :]], axis=-3)


def full_flux(states, padded, perm_here, perm_pad):

    def fields(which):
        pressure = neighbour(states[0], padded[0], which).astype(jnp.float32)
        saturation = neighbour(states[1], padded[1], which).astype(jnp.float32)
        return (pressure, saturation * saturation, neighbour(perm_here, perm_pad, which)[None])

    here_p, here_m, here_k = fields(0)

    def side(which):
        there_p, there_m, there_k = fields(which)
        return face_term(here_p, here_m, here_k, there_p, there_m, there_k)

    summed = side(1) + side(2)
    summed = summed + side(3)
    summed = summed + side(4)
    summed = summed + side(5)
    summed = summed + side(6)
    return summed


def collect(my_rows, merge_order):
    kept_count = my_rows.shape[0]
    tile_count = lax.axis_size("gx") * lax.axis_size("gy")
    kept_ids = kept_sources(tile_count, kept_count, merge_order)
    all_rows = lax.all_gather(my_rows[None], ("gx", "gy"), axis=0, tiled=True)
    flat_rows = all_rows.reshape(tile_count * kept_count, my_rows.shape[1])
    return flat_rows[kept_ids.reshape(-1)].reshape(kept_ids.shape + (my_rows.shape[1],))


def local(states, class_map, perm_table, candidates, merge_order):
    padded = padded_2(states, (("gx", 3), ("gy", 4)), 1)
    class_pad = padded_2(class_map, (("gx", 1), ("gy", 2)), 1)
    perm_pad = jnp.zeros(class_pad.shape, jnp.float32)
    perm_here = jnp.zeros(class_map.shape, jnp.float32)
    for class_num in range(perm_table.shape[0]):
        perm_pad = perm_pad + jnp.where(class_pad == class_num, perm_table[class_num], 0.0)
        perm_here = perm_here + jnp.where(class_map == class_num, perm_table[class_num], 0.0)
    tile_x = lax.axis_index("gx")
    tile_y = lax.axis_index("gy")
    tile_cells = lax.dynamic_index_in_dim(
        lax.dynamic_index_in_dim(candidates, tile_x, 0, False), tile_y, 0, False
    )
    cell_total = class_map.shape[0] * class_map.shape[1] * class_map.shape[2]
    cell_ids = lax.broadcasted_iota(jnp.int32, (cell_total, tile_cells.shape[0]), 0)
    picker = jnp.where(cell_ids == tile_cells[None, :], 1.0, 0.0).astype(jnp.float32)
    flux_full = full_flux(states, padded, perm_here, perm_pad)
    flat_flux = flux_full.reshape(flux_full.shape[0], -1)
    my_rows = jnp.einsum(
        "sc,ci->is",
        flat_flux,
        picker,
        precision=lax.Precision.HIGHEST,
        preferred_element_type=jnp.float32,
    )
    kept_rows = collect(my_rows, merge_order)
    return (flux_full.astype(jnp.bfloat16), kept_rows)


def solution(mesh):
    in_specs = (P(None, None, None, "gx", "gy"), P(None, "gx", "gy"), P(), P(), P())
    out_specs = (P(None, None, "gx", "gy"), P())
    return jax.shard_map(local, mesh=mesh, in_specs=in_specs, out_specs=out_specs, check_vma=False)
```

profile of v0, /device:TPU:1, one launch (start us, length us, event | category | flops | bytes accessed | tf_op | source)
XLA Modules:
  0.0 305.4 jit_solution(611514117082606638)
XLA Ops:
  7.2 0.8 fusion.47
  8.7 2.5 collective-permute-start.4
  11.7 4.3 %collective-permute-start.5 = (s32[8,1,128]{2,0,1:T(8,128)}, s32[8,1,128]{2,0,1:T(8,128)}, u32[]{:S(2)}, u32[]{:S(2)}) collective-permute-start(s32[8,1,128]{2,0,1:T(8,128)} %copy.84), channel_id=1, source_target_pairs={{8,0},{16,8},{24,16},{32,24},{40,32},{48,40},{56,48},{64,56},{72,6... | collective-permute-start | bytes 12296 | tf_op jit(solution)/shard_map/ppermute | solution.py:16
  16.0 3.2 %fusion.30 = (bf16[2,64,8,1,128]{4,3,2,1,0:T(2,128)(2,1)S(1)}, bf16[2,64,8,1,128]{4,3,2,1,0:T(2,128)(2,1)S(1)}) fusion(bf16[2,64,8,8,128]{4,3,2,1,0:T(8,128)(2,1)} %param.5), kind=kLoop, calls=%fused_computation.113 | loop fusion | bytes 1048576 | tf_op jit(solution)/shard_map/slice | solution.py:16
  19.3 0.7 copy.85
  20.0 0.7 copy.86
  20.7 4.8 %collective-permute-start.1 = (bf16[2,64,8,1,128]{4,2,1,3,0:T(8,128)(2,1)}, bf16[2,64,8,1,128]{4,2,1,3,0:T(8,128)(2,1)}, u32[]{:S(2)}, u32[]{:S(2)}) collective-permute-start(bf16[2,64,8,1,128]{4,2,1,3,0:T(8,128)(2,1)} %copy.86), channel_id=1, source_target_pairs={{8,0},{16,8},{24,16},{32,24},{40,32},{48,40},{56,48},{64,56},{72,6... | collective-permute-start | bytes 786440 | tf_op jit(solution)/shard_map/ppermute | solution.py:16
  25.5 0.7 fusion.49
  26.2 5.1 %select_add_fusion.1 = f32[8,8,128]{2,1,0:T(8,128)S(1)} fusion(s32[8,8,128]{2,1,0:T(8,128)S(1)} %copy-done.4, f32[]{:T(128)} %bitcast.10, f32[]{:T(128)} %bitcast.9, f32[]{:T(128)} %bitcast.8, f32[]{:T(128)} %bitcast.7, f32[]{:T(128)} %bitcast.6, f32[]{:T(128)} %bitcast.5, f32[]{:T(128)} %bitcast.4, f32[]{:T(128)} %bitcast.3), kind=kLoop, calls=%fused_computation.74 | loop fusion | flops 188416 | bytes 65568 | tf_op jit(solution)/shard_map/add | solution.py:100
  32.0 0.7 fusion.45
  35.3 2.1 fusion.31
  37.4 2.8 fusion.35
  40.1 2.8 fusion.36
  43.0 2.1 fusion.39
  45.1 1.6 fusion.32
  47.9 0.8 reshape.223
  48.7 43.2 %gather_fusion.2 = s32[4096]{0:T(1024)} fusion(s32[64,128]{1,0:T(8,128)S(1)} %multiply_add_fusion, s32[4096]{0:T(1024)S(1)} %reshape.223), kind=kCustom, calls=%fused_computation.2 | custom fusion | bytes 65536 | tf_op jit(solution)/shard_map/jit(take_along_axis)/gather | solution.py:34
  92.0 1.4 reshape.226
  93.3 0.8 and_select_fusion
  94.8 0.8 reshape.229
  95.6 13.1 %gather_fusion.3 = s32[2048]{0:T(1024)S(1)} fusion(s32[32,128]{1,0:T(8,128)S(1)} %select_n.240, s32[2048]{0:T(1024)S(1)} %reshape.229), kind=kCustom, calls=%fused_computation.3 | custom fusion | bytes 32768 | tf_op jit(solution)/shard_map/jit(take_along_axis)/gather | solution.py:34
  108.7 1.3 and_select_fusion.1
  111.4 0.7 constant_dynamic-update-slice_fusion.3
  112.0 0.7 fusion.42
  112.7 2.7 collective-permute-start.6
  116.0 0.8 select_n.243
  116.9 2.3 collective-permute-done.7
  119.2 6.0 %select_add_fusion = f32[8,10,130]{2,0,1:T(8,128)S(1)} fusion(s32[8,10,1]{2,0,1:T(8,128)} %collective-permute-done.7, s32[8,10,128]{2,0,1:T(8,128)S(1)} %constant_dynamic-update-slice_fusion.3, s32[8,10,1]{2,0,1:T(8,128)} %collective-permute-done.6, f32[]{:T(128)} %bitcast.10, f32[]{:T(128)} %bitcast.9, f32[]{:T(128)} %bitcast.8, f32[]{:T(128)} %bitcast.7, ...), kind=kLoop, calls=%fused_computation.53 | loop fusion | flops 260000 | bytes 83232 | tf_op jit(solution)/shard_map/add | solution.py:99
  126.2 0.8 slice_bitcast_fusion.9
  127.0 1.0 constant_dynamic-update-slice_fusion.2
  128.6 1.0 constant_dynamic-update-slice_fusion
  129.6 3.4 %fusion.29 = (bf16[2,64,8,10,1]{4,2,1,3,0:T(8,128)(2,1)}, bf16[2,64,8,10,1]{4,2,1,3,0:T(8,128)(2,1)}) fusion(bf16[2,64,8,10,128]{4,2,1,3,0:T(8,128)(2,1)S(1)} %constant_dynamic-update-slice_fusion), kind=kLoop, calls=%fused_computation.112 | loop fusion | bytes 81920 | tf_op jit(solution)/shard_map/slice | solution.py:14
  133.0 3.7 %copy.54 = bf16[2,64,8,10,1]{1,2,4,3,0:T(8,128)(2,1)} copy(bf16[2,64,8,10,1]{4,2,1,3,0:T(8,128)(2,1)} %get-tuple-element.22) | data formatting | bytes 40960 | tf_op jit(solution)/shard_map/slice | solution.py:14
  136.6 3.7 %copy.55 = bf16[2,64,8,10,1]{1,2,4,3,0:T(8,128)(2,1)} copy(bf16[2,64,8,10,1]{4,2,1,3,0:T(8,128)(2,1)} %get-tuple-element.23) | data formatting | bytes 40960 | tf_op jit(solution)/shard_map/slice | solution.py:16
  140.9 6.8 %divide_multiply_fusion.3 = (f32[8,8,128]{2,1,0:T(8,128)S(1)}, f32[8,8,128]{2,1,0:T(8,128)S(1)}, f32[8,8,128]{2,1,0:T(8,128)}, f32[8,8,128]{2,1,0:T(8,128)}, f32[8,8,128]{2,1,0:T(8,128)}, /*index=5*/f32[8,8,128]{2,1,0:T(8,128)}) fusion(f32[8,1,128]{2,1,0:T(1,128)S(1)} %copy-done.12, f32[8,7,128]{2,1,0:T(8,128)} %get-tuple-element.60, ...), kind=kLoop, calls=%fused_computation.73 | loop fusion | flops 458752 | bytes 426800 | tf_op jit(solution)/shard_map/mul | solution.py:23
  147.6 3.2 %copy.56 = bf16[2,64,8,10,1]{4,2,1,3,0:T(8,128)(2,1)} copy(bf16[2,64,8,10,1]{1,2,4,3,0:T(8,128)(2,1)} %collective-permute-done.2) | data formatting | bytes 40960 | tf_op jit(solution)/shard_map/ppermute | solution.py:13
  150.8 3.2 %copy.57 = bf16[2,64,8,10,1]{4,2,1,3,0:T(8,128)(2,1)} copy(bf16[2,64,8,10,1]{1,2,4,3,0:T(8,128)(2,1)} %collective-permute-done.3) | data formatting | bytes 40960 | tf_op jit(solution)/shard_map/ppermute | solution.py:16
  153.9 6.1 %pad_maximum_fusion = bf16[2,64,8,10,130]{4,2,1,3,0:T(8,128)(2,1)S(1)} fusion(bf16[2,64,8,10,1]{4,2,1,3,0:T(8,128)(2,1)} %copy.57, bf16[2,64,8,10,128]{4,2,1,3,0:T(8,128)(2,1)} %copy-done.3, bf16[2,64,8,10,1]{4,2,1,3,0:T(8,128)(2,1)} %copy.56), kind=kLoop, calls=%fused_computation.8 | loop fusion | flops 7987200 | bytes 5324800 | tf_op jit(solution)/shard_map/concatenate | solution.py:17
  160.6 1.0 slice_bitcast_fusion.6
  161.6 2.8 fusion.27
  164.4 5.0 %copy.72 = bf16[64,8,8,1]{2,1,0,3:T(8,128)(2,1)} copy(bf16[64,8,8,1]{3,1,0,2:T(8,128)(2,1)} %get-tuple-element.18) | data formatting | bytes 16384 | tf_op jit(solution)/shard_map/jit(_where)/broadcast_in_dim | solution.py:53
  169.3 5.0 %copy.73 = bf16[64,8,8,1]{2,1,0,3:T(8,128)(2,1)} copy(bf16[64,8,8,1]{3,1,0,2:T(8,128)(2,1)} %get-tuple-element.97) | data formatting | bytes 16384 | tf_op jit(solution)/shard_map/jit(_where)/broadcast_in_dim | solution.py:53
  174.3 4.9 %copy.74 = bf16[64,8,8,1]{2,1,0,3:T(8,128)(2,1)} copy(bf16[64,8,8,1]{3,1,0,2:T(8,128)(2,1)} %get-tuple-element.19) | data formatting | bytes 16384 | tf_op jit(solution)/shard_map/jit(_where)/broadcast_in_dim | solution.py:56
  179.3 5.2 %copy.75 = bf16[64,8,8,1]{2,1,0,3:T(8,128)(2,1)} copy(bf16[64,8,8,1]{3,1,0,2:T(8,128)(2,1)} %get-tuple-element.96) | data formatting | bytes 16384 | tf_op jit(solution)/shard_map/jit(_where)/broadcast_in_dim | solution.py:56
  184.5 12.3 %fusion.25 = (bf16[64,8,8,128]{3,2,1,0:T(8,128)(2,1)}, f32[64,8,8,128]{3,2,1,0:T(8,128)S(1)}) fusion(bf16[64,7,8,128]{3,2,1,0:T(8,128)(2,1)} %get-tuple-element.88, f32[8,8,128]{2,1,0:T(8,128)} %get-tuple-element.59, bf16[64,7,8,128]{3,2,1,0:T(8,128)(2,1)} %get-tuple-element.45, bf16[64,7,8,128]{3,2,1,0:T(8,128)(2,1)} %get-tuple-element.89, ...), kind=kLoop, calls=%fused_computation.109 | loop fusion | flops 47710208 | bytes 18055440 | tf_op jit(solution)/shard_map/convert_element_type | solution.py:119
  196.8 3.5 %fusion.11 = f32[64,64]{1,0:T(8,128)} fusion(f32[8,8,64,128]{3,2,1,0:T(8,128)S(1)} %bitcast.82, s32[64]{0:T(128)S(1)} %copy-done.18), kind=kOutput, calls=%fused_computation.28 | convolution fusion | flops 403701760 | bytes 2113792 | tf_op jit(solution)/shard_map/sc,ci->is/dot_general | solution.py:111
  200.3 0.7 bitcast_or_fusion.2
  201.1 6.8 %gather_fusion.4 = s32[1024]{0:T(1024)S(1)} fusion(s32[16,128]{1,0:T(8,128)S(1)} %select_n.243, s32[1024]{0:T(1024)S(1)} %reshape.235), kind=kCustom, calls=%fused_computation.4 | custom fusion | bytes 16384 | tf_op jit(solution)/shard_map/jit(take_along_axis)/gather | solution.py:34
  208.0 0.7 and_select_fusion.2
  208.7 0.7 bitcast_or_fusion.3
  209.5 2.5 gather_fusion.5
  212.1 0.7 and_select_fusion.3
  212.9 0.7 bitcast_or_fusion.4
  213.7 2.4 gather_fusion.6
  216.1 0.7 and_select_fusion.6
  216.9 0.7 bitcast_or_fusion.5
  217.7 1.5 gather_fusion.7
  219.3 0.7 and_select_fusion.5
  220.1 0.7 fusion.24
  220.8 0.8 gather_fusion
  221.5 0.7 and_select_fusion.4
  222.4 41.2 %all-gather.3.cloned.1.call-done = f32[8192,64]{1,0:T(8,128)} async-done(((f32[64,64]{1,0:T(8,128)}), f32[8192,64]{1,0:T(8,128)}) %all-gather.3.cloned.1.call-update) | async-done | bytes 2097168 | tf_op jit(solution)/shard_map/all_gather | solution.py:88
  263.6 30.1 %gather_fusion.1 = f32[8128,64]{1,0:T(8,128)} fusion(f32[8192,64]{1,0:T(8,128)} %all-gather.3.cloned.1.call-done, s32[8192]{0:T(1024)S(1)} %pad_clamp_fusion), kind=kCustom, calls=%fused_computation.1 | custom fusion | bytes 4194048 | tf_op jit(solution)/shard_map/gather | solution.py:90
  293.7 4.9 %copy.71 = f32[127,64,64]{0,2,1:T(8,128)} copy(f32[127,64,64]{2,1,0:T(8,128)} %bitcast.81) | data formatting | bytes 4161536
  (90 shorter events, 12.1 us)
Async XLA Ops:
  7.2 108.3 %copy-start = (s32[16,8,64]{2,1,0:T(8,128)S(1)}, s32[16,8,64]{2,1,0:T(8,128)}, u32[]{:S(2)}) copy-start(s32[16,8,64]{2,1,0:T(8,128)} %param.8) | copy-start | bytes 98308
  7.2 19.0 %copy-start.4 = (s32[8,8,128]{2,1,0:T(8,128)S(1)}, s32[8,8,128]{2,1,0:T(8,128)}, u32[]{:S(2)}) copy-start(s32[8,8,128]{2,1,0:T(8,128)} %param.6) | copy-start | bytes 98308
  7.2 18.3 %copy-start.11 = (f32[8]{0:T(128)S(1)}, f32[8]{0:T(128)}, u32[]{:S(2)}) copy-start(f32[8]{0:T(128)} %param.7) | copy-start | bytes 100
  7.2 256.4 %all-gather.3.cloned.1.call-start = ((), (), s32[]{:S(2)}) async-start(), calls=%async_computation | async-start | bytes 4227072 | tf_op jit(solution)/shard_map/all_gather | solution.py:88
  8.7 102.0 %collective-permute-start.4 = (s32[8,1,128]{2,0,1:T(8,128)}, s32[8,1,128]{2,0,1:T(8,128)}, u32[]{:S(2)}, u32[]{:S(2)}) collective-permute-start(s32[8,1,128]{2,0,1:T(8,128)} %copy.83), channel_id=1, source_target_pairs={{0,8},{8,16},{16,24},{24,32},{32,40},{40,48},{48,56},{56,64},{64,7... | collective-permute-start | bytes 12296 | tf_op jit(solution)/shard_map/ppermute | solution.py:13
  11.7 23.4 %copy-start.2 = (bf16[2,64,8,8,128]{4,3,2,1,0:T(8,128)(2,1)S(1)}, bf16[2,64,8,8,128]{4,3,2,1,0:T(8,128)(2,1)}, u32[]{:S(2)}) copy-start(bf16[2,64,8,8,128]{4,3,2,1,0:T(8,128)(2,1)} %param.5) | copy-start | bytes 6291460
  11.7 99.6 %collective-permute-start.5 = (s32[8,1,128]{2,0,1:T(8,128)}, s32[8,1,128]{2,0,1:T(8,128)}, u32[]{:S(2)}, u32[]{:S(2)}) collective-permute-start(s32[8,1,128]{2,0,1:T(8,128)} %copy.84), channel_id=1, source_target_pairs={{8,0},{16,8},{24,16},{32,24},{40,32},{48,40},{56,48},{64,56},{72,6... | collective-permute-start | bytes 12296 | tf_op jit(solution)/shard_map/ppermute | solution.py:16
  20.0 107.0 %collective-permute-start = (bf16[2,64,8,1,128]{4,2,1,3,0:T(8,128)(2,1)}, bf16[2,64,8,1,128]{4,2,1,3,0:T(8,128)(2,1)}, u32[]{:S(2)}, u32[]{:S(2)}) collective-permute-start(bf16[2,64,8,1,128]{4,2,1,3,0:T(8,128)(2,1)} %copy.85), channel_id=1, source_target_pairs={{0,8},{8,16},{16,24},{24,32},{32,40},{40,48},{48,56},{56,64},{64,7... | collective-permute-start | bytes 786440 | tf_op jit(solution)/shard_map/ppermute | solution.py:13
  20.7 107.8 %collective-permute-start.1 = (bf16[2,64,8,1,128]{4,2,1,3,0:T(8,128)(2,1)}, bf16[2,64,8,1,128]{4,2,1,3,0:T(8,128)(2,1)}, u32[]{:S(2)}, u32[]{:S(2)}) collective-permute-start(bf16[2,64,8,1,128]{4,2,1,3,0:T(8,128)(2,1)} %copy.86), channel_id=1, source_target_pairs={{8,0},{16,8},{24,16},{32,24},{40,32},{48,40},{56,48},{64,56},{72,6... | collective-permute-start | bytes 786440 | tf_op jit(solution)/shard_map/ppermute | solution.py:16
  45.1 1.6 copy-start.8
  94.1 0.6 copy-start.6
  112.7 4.1 %collective-permute-start.6 = (s32[8,10,1]{2,0,1:T(8,128)}, s32[8,10,1]{2,0,1:T(8,128)}, u32[]{:S(2)}, u32[]{:S(2)}) collective-permute-start(s32[8,10,1]{2,0,1:T(8,128)} %get-tuple-element.52), channel_id=1, source_target_pairs={{0,1},{1,2},{2,3},{3,4},{4,5},{5,6},{6,7},{7,0},{8,9},{9,10},{10,1... | collective-permute-start | bytes 968 | tf_op jit(solution)/shard_map/ppermute | solution.py:13
  115.4 3.7 %collective-permute-start.7 = (s32[8,10,1]{2,0,1:T(8,128)}, s32[8,10,1]{2,0,1:T(8,128)}, u32[]{:S(2)}, u32[]{:S(2)}) collective-permute-start(s32[8,10,1]{2,0,1:T(8,128)} %get-tuple-element.53), channel_id=1, source_target_pairs={{1,0},{2,1},{3,2},{4,3},{5,4},{6,5},{7,6},{0,7},{9,8},{10,9},{11,1... | collective-permute-start | bytes 968 | tf_op jit(solution)/shard_map/ppermute | solution.py:16
  125.2 0.6 copy-start.5
  129.5 3.4 %copy-start.3 = (bf16[2,64,8,10,128]{4,2,1,3,0:T(8,128)(2,1)}, bf16[2,64,8,10,128]{4,2,1,3,0:T(8,128)(2,1)S(1)}, u32[]{:S(2)}) copy-start(bf16[2,64,8,10,128]{4,2,1,3,0:T(8,128)(2,1)S(1)} %constant_dynamic-update-slice_fusion) | copy-start | bytes 7864324
  132.9 7.9 %copy-start.12 = (f32[8,1,128]{2,1,0:T(1,128)S(1)}, f32[8,1,128]{2,1,0:T(1,128)}, u32[]{:S(2)}) copy-start(f32[8,1,128]{2,1,0:T(1,128)} %get-tuple-element.62) | copy-start | bytes 12292
  132.9 7.9 %copy-start.13 = (f32[8,1,128]{2,1,0:T(1,128)S(1)}, f32[8,1,128]{2,1,0:T(1,128)}, u32[]{:S(2)}) copy-start(f32[8,1,128]{2,1,0:T(1,128)} %get-tuple-element.63) | copy-start | bytes 12292
  132.9 7.9 %copy-start.14 = (pred[128]{0:T(512)(128)(4,1)S(1)}, pred[128]{0:T(512)(128)(4,1)}, u32[]{:S(2)}) copy-start(pred[128]{0:T(512)(128)(4,1)} %get-tuple-element.90) | copy-start | bytes 388
  132.9 7.9 %copy-start.15 = (pred[128]{0:T(512)(128)(4,1)S(1)}, pred[128]{0:T(512)(128)(4,1)}, u32[]{:S(2)}) copy-start(pred[128]{0:T(512)(128)(4,1)} %get-tuple-element.91) | copy-start | bytes 388
  132.9 7.9 %copy-start.16 = (pred[8]{0:T(512)(128)(4,1)S(1)}, pred[8]{0:T(512)(128)(4,1)}, u32[]{:S(2)}) copy-start(pred[8]{0:T(512)(128)(4,1)} %get-tuple-element.92) | copy-start | bytes 28
  132.9 7.9 %copy-start.17 = (pred[8]{0:T(512)(128)(4,1)S(1)}, pred[8]{0:T(512)(128)(4,1)}, u32[]{:S(2)}) copy-start(pred[8]{0:T(512)(128)(4,1)} %get-tuple-element.93) | copy-start | bytes 28
  136.6 11.0 %collective-permute-start.2 = (bf16[2,64,8,10,1]{1,2,4,3,0:T(8,128)(2,1)}, bf16[2,64,8,10,1]{1,2,4,3,0:T(8,128)(2,1)}, u32[]{:S(2)}, u32[]{:S(2)}) collective-permute-start(bf16[2,64,8,10,1]{1,2,4,3,0:T(8,128)(2,1)} %copy.54), channel_id=1, source_target_pairs={{0,1},{1,2},{2,3},{3,4},{4,5},{5,6},{6,7},{7,0},{8,9},{9,10},{10,1... | collective-permute-start | bytes 61448 | tf_op jit(solution)/shard_map/ppermute | solution.py:13
  140.3 10.5 %collective-permute-start.3 = (bf16[2,64,8,10,1]{1,2,4,3,0:T(8,128)(2,1)}, bf16[2,64,8,10,1]{1,2,4,3,0:T(8,128)(2,1)}, u32[]{:S(2)}, u32[]{:S(2)}) collective-permute-start(bf16[2,64,8,10,1]{1,2,4,3,0:T(8,128)(2,1)} %copy.55), channel_id=1, source_target_pairs={{1,0},{2,1},{3,2},{4,3},{5,4},{6,5},{7,6},{0,7},{9,8},{10,9},{11,1... | collective-permute-start | bytes 61448 | tf_op jit(solution)/shard_map/ppermute | solution.py:16
  169.3 15.1 %copy-start.10 = (f32[8,8,128]{2,1,0:T(8,128)S(1)}, f32[8,8,128]{2,1,0:T(8,128)}, u32[]{:S(2)}) copy-start(f32[8,8,128]{2,1,0:T(8,128)} %get-tuple-element.56) | copy-start | bytes 98308
  184.5 12.3 %copy-start.18 = (s32[64]{0:T(128)S(1)}, s32[64]{0:T(128)}, u32[]{:S(2)}) copy-start(s32[64]{0:T(128)} %dynamic-slice_bitcast_fusion) | copy-start | bytes 772
  212.0 10.2 %copy-start.7 = (s32[64,64]{1,0:T(8,128)S(1)}, s32[64,64]{1,0:T(8,128)}, u32[]{:S(2)}) copy-start(s32[64,64]{1,0:T(8,128)} %copy-done.6) | copy-start | bytes 49156
  212.0 10.2 %copy-start.9 = (s32[32,64]{1,0:T(8,128)S(1)}, s32[32,64]{1,0:T(8,128)}, u32[]{:S(2)}) copy-start(s32[32,64]{1,0:T(8,128)} %and_select_fusion.1) | copy-start | bytes 24580
  293.7 4.9 %copy-start.1 = (s32[16,8,64]{2,1,0:T(8,128)S(1)}, s32[16,8,64]{2,1,0:T(8,128)}, u32[]{:S(2)}) copy-start(s32[16,8,64]{2,1,0:T(8,128)} %param.8) | copy-start | bytes 98308
Sparse Core Ops, SparseCore 0:
  200.4 63.1 all-gather.2
where the time goes:
time: 307 us; the launch traced here: 305 us
  local copies, waits for them, and re-layouts  181 us (59%)
  other arithmetic  47.8 us (16%)
  waiting for transfers between devices  43.6 us (14%)
  starting transfers between devices  14.8 us (5%)
  between operations  14.3 us (5%)
  matrix products  3.52 us (1%)
    gather x19, local copies, waits for them, and re-layouts, kept_sources(): level_ids = jnp.take_along_axis(paired, node_order, axis=1)  74 us
    all_gather x1, waiting for transfers between devices, collect(): all_rows = lax.all_gather(my_rows[None], ('gx', 'gy'), axis=0, tiled=True)  41.2 us
    gather x1, local copies, waits for them, and re-layouts, collect(): flat_rows[kept_ids.reshape(-1)]  30.1 us
    convert_element_type x1, other arithmetic, local(): return (flux_full.astype(jnp.bfloat16), kept_rows)  12.3 us
    unnamed x47, local copies, waits for them, and re-layouts  11.1 us
    broadcast_in_dim x2, local copies, waits for them, and re-layouts, neighbour(): jnp.where(column == 0, padded[..., 1:-1, :1], jnp.roll(centre, 1, -1))  10.2 us
    broadcast_in_dim x2, local copies, waits for them, and re-layouts, neighbour(): jnp.where(column == width_y - 1, padded[..., 1:-1, -1:], jnp.roll(centre,...  9.92 us
    ppermute x4, starting transfers between devices, padded_2(): lax.ppermute(lax.slice_in_dim(block, 0, width, axis=dim), axis, backward)  9.61 us
  transfers between devices with their start and end apart: 9, of which 2 were waited for; matrix products, arithmetic and copies ran while one was open for 45% of the time, Pallas kernels for 0%

commit v1 on v0

v1 whole, which is shorter than its diff:
```python
import functools

import jax
import jax.numpy as jnp
from jax import lax
from jax.experimental import pallas as pl
from jax.experimental.pallas import tpu as pltpu
from jax.sharding import PartitionSpec as P

F32 = jnp.float32
BF16 = jnp.bfloat16
CHUNK = 16


def lane_of(shape):
    return lax.broadcasted_iota(jnp.int32, shape, len(shape) - 1)


def edge_kernel(states_ref, class_ref, low_ref, high_ref, side_ref, wide_ref, acc_ref):
    step = pl.program_id(0)
    chunk = states_ref.shape[1]
    snaps = chunk * pl.num_programs(0)
    base = step * chunk
    cells = 64

    @pl.when(step == 0)
    def _():
        acc_ref[...] = jnp.zeros_like(acc_ref)
        kind = class_ref[...].astype(F32)
        wide_ref[pl.ds(0, cells), :] = kind.reshape(cells, 128)
        low_ref[2 * 64] = wide_ref[pl.ds(0, 8, stride=8), :].astype(BF16)
        high_ref[2 * 64] = wide_ref[pl.ds(7, 8, stride=8), :].astype(BF16)
        first = jnp.broadcast_to(kind[:, :, 0:1], kind.shape)
        last = jnp.broadcast_to(kind[:, :, 127:128], kind.shape)
        even = lane_of(kind.shape) % 2 == 0
        side_ref[2] = jnp.where(even, first, last).astype(BF16)

    for field in range(2):
        acc = acc_ref[field]
        for k in range(chunk):
            value = states_ref[field, k].astype(F32).reshape(cells, 128)
            slot = (field * chunk + k) * cells
            wide_ref[pl.ds(slot, cells), :] = value
            place = 2 * (base + k)
            turned = pltpu.roll(value, place, 1)
            lane = lane_of(value.shape)
            acc = jnp.where((lane == place) | (lane == (place + 127) % 128), turned, acc)
            low_ref[field * 64 + base + k] = wide_ref[pl.ds(slot, 8, stride=8), :].astype(BF16)
            high_ref[field * 64 + base + k] = wide_ref[pl.ds(slot + 7, 8, stride=8), :].astype(BF16)
        acc_ref[field] = acc

    @pl.when(step == pl.num_programs(0) - 1)
    def _():
        side_ref[0] = acc_ref[0].reshape(8, 8, 128).astype(BF16)
        side_ref[1] = acc_ref[1].reshape(8, 8, 128).astype(BF16)


def look_up(kind, table_ref):
    value = jnp.zeros(kind.shape, F32)
    for number in range(8):
        value = jnp.where(kind == number, table_ref[number], value)
    return value


def trans(k_here, k_next):
    return k_here * k_next / (k_here + k_next)


def flux_kernel(
    table_ref, cand_ref, where_ref, states_ref, class_ref, low_ref, high_ref, side_ref,
    from_low_ref, from_high_ref, side_low_ref, side_high_ref,
    out_ref, rows_ref, flux_ref, tx_ref, ty_ref, tz_ref, txe_ref, qy_ref,
):
    step = pl.program_id(0)
    chunk = states_ref.shape[1]
    base = step * chunk
    shape = (8, 8, 128)

    @pl.when(step == 0)
    def _():
        perm = look_up(class_ref[...], table_ref)
        row = lax.broadcasted_iota(jnp.int32, shape, 1)
        lane = lane_of(shape)
        flat = perm.reshape(64, 128)
        next_x = jnp.roll(perm, -1, 1)
        next_y = pltpu.roll(flat, 127, 1).reshape(shape)
        tx_ref[...] = jnp.where(row == 7, 0.0, trans(perm, next_x))
        ty_ref[...] = jnp.where(lane == 127, 0.0, trans(perm, next_y))
        tz_ref[...] = trans(perm[:-1], perm[1:])
        k_low = look_up(low_ref[128].astype(F32), table_ref)
        k_high = look_up(high_ref[128].astype(F32), table_ref)
        txe_ref[0] = trans(k_low, look_up(from_low_ref[128].astype(F32), table_ref))
        txe_ref[1] = trans(k_high, look_up(from_high_ref[128].astype(F32), table_ref))
        even = lax.broadcasted_iota(jnp.int32, (64, 128), 1) % 2 == 0

        def beyond(which):
            below = side_low_ref[which].astype(F32).reshape(64, 128)
            above = side_high_ref[which].astype(F32).reshape(64, 128)
            return jnp.where(even, pltpu.roll(below, 1, 1), pltpu.roll(above, 127, 1))

        def here(which):
            return side_ref[which].astype(F32).reshape(64, 128)

        t_side = trans(look_up(here(2), table_ref), look_up(beyond(2), table_ref))
        s_here, s_next = here(1), beyond(1)
        qy_ref[...] = t_side * (s_here * s_here + s_next * s_next) * (beyond(0) - here(0))

    def face(t, l_here, l_next, p_here, p_next):
        return t * (l_here + l_next) * (p_next - p_here)

    lane = lax.broadcasted_iota(jnp.int32, (64, 128), 1)
    at_edge = (lane == 0) | (lane == 127)

    for k in range(chunk):
        snap = base + k
        p = states_ref[0, k].astype(F32)
        s = states_ref[1, k].astype(F32)
        m = s * s
        fx = face(tx_ref[...], m, jnp.roll(m, -1, 1), p, jnp.roll(p, -1, 1))
        total = fx - jnp.roll(fx, 1, 1)
        pf, mf = p.reshape(64, 128), m.reshape(64, 128)
        fy = face(
            ty_ref[...].reshape(64, 128), mf, pltpu.roll(mf, 127, 1), pf, pltpu.roll(pf, 127, 1)
        )
        total = total + (fy - pltpu.roll(fy, 1, 1)).reshape(shape)
        fz = face(tz_ref[...], m[:-1], m[1:], p[:-1], p[1:])
        zero = jnp.zeros((1, 8, 128), F32)
        total = total + (jnp.concatenate([fz, zero], 0) - jnp.concatenate([zero, fz], 0))
        turned = pltpu.roll(qy_ref[...], (256 - 2 * snap) % 128, 1)
        flat = total.reshape(64, 128) + jnp.where(at_edge, turned, 0.0)
        start = pl.multiple_of(snap * 64, 64)
        flux_ref[pl.ds(start, 64), :] = flat

        def edge(own_ref, other_ref, which):
            s_here = own_ref[64 + snap].astype(F32)
            s_next = other_ref[64 + snap].astype(F32)
            p_here, p_next = own_ref[snap].astype(F32), other_ref[snap].astype(F32)
            return face(txe_ref[which], s_here * s_here, s_next * s_next, p_here, p_next)

        low = pl.ds(start, 8, stride=8)
        high = pl.ds(start + 7, 8, stride=8)
        flux_ref[low, :] = flux_ref[low, :] + edge(low_ref, from_low_ref, 0)
        flux_ref[high, :] = flux_ref[high, :] + edge(high_ref, from_high_ref, 1)
        out_ref[k] = flux_ref[pl.ds(start, 64), :].reshape(shape).astype(BF16)

    @pl.when(step == pl.num_programs(0) - 1)
    def _():
        tile = where_ref[0]
        lane = lax.broadcasted_iota(jnp.int32, (64, 128), 1)

        def pick(i, acc):
            cell = cand_ref[tile, i]
            values = flux_ref[pl.ds(cell // 128, 64, stride=64), :]
            turned = pltpu.roll(values, (i - cell % 128 + 128) % 128, 1)
            return jnp.where(lane == i, turned, acc)

        acc = lax.fori_loop(0, 64, pick, jnp.zeros((64, 128), F32), unroll=4)
        full = jnp.concatenate([acc, jnp.zeros((64, 128), F32)], 0)
        rows_ref[...] = jnp.transpose(full)[:64, :]


def pair_kernel(order_ref, where_ref, mine_ref, other_ref, out_ref, stack_ref):
    tile = where_ref[0]
    core = tile % 2
    node = tile // 2
    stack_ref[pl.ds(pl.multiple_of(core * 64, 64), 64), :] = mine_ref[...]
    stack_ref[pl.ds(pl.multiple_of(64 - core * 64, 64), 64), :] = other_ref[...]
    left, right = [], []
    for r in range(16):
        left.append(stack_ref[pl.ds(order_ref[node, core * 32 + r], 1), :])
        right.append(stack_ref[pl.ds(order_ref[node, core * 32 + 16 + r], 1), :])
    packed = jnp.concatenate(left, 0) + pltpu.roll(jnp.concatenate(right, 0), 64, 1)
    out_ref[...] = jnp.broadcast_to(packed[None], out_ref.shape)


def tree_kernel(where_ref, pick_ref, mine_ref, other_ref, out_ref, half_ref, level_ref):
    core = where_ref[0] % 2
    half_ref[core] = mine_ref[...]
    half_ref[1 - core] = other_ref[...]
    lane = lax.broadcasted_iota(jnp.int32, (16, 128), 1)
    left = lane < 64

    def unpack(chip, carry):
        for half in range(2):
            both = half_ref[half, chip]
            for part in range(2):
                value = both if part == 0 else pltpu.roll(both, 64, 1)
                top = value.astype(BF16).astype(F32)
                rest = value - top
                pieces = jnp.where(left, top, pltpu.roll(rest, 64, 1)).astype(BF16)
                at = half * 32 + part * 16
                out_ref[chip, pl.ds(at, 16), :] = value[:, :64]
                level_ref[chip, pl.ds(at, 16), :] = pieces
        return carry

    lax.fori_loop(0, 64, unpack, 0, unroll=2)
    before, offset, count = 0, 64, 32
    while count >= 1:
        for j in range(count):
            stack = level_ref[pl.ds(before + 2 * j, 2)].reshape(128, 128)
            got = jnp.dot(pick_ref[offset - 64 + j], stack, preferred_element_type=F32)
            level_ref[offset + j] = got.astype(BF16)
            out_ref[offset + j] = (got + pltpu.roll(got, 64, 1))[:, :64]
        before, offset, count = offset, offset + count, count // 2


def whole(shape):
    return pl.BlockSpec(shape, lambda *_: (0,) * len(shape))


SMEM = pl.BlockSpec(memory_space=pltpu.SMEM)
LIMIT = pltpu.CompilerParams(vmem_limit_bytes=48 * 1024 * 1024)


def local(states, class_map, perm_table, candidates, merge_order):
    tile = lax.axis_index("gx") * lax.axis_size("gy") + lax.axis_index("gy")
    where = tile.reshape(1).astype(jnp.int32)
    steps = 64 // CHUNK
    states_spec = pl.BlockSpec((2, CHUNK, 8, 8, 128), lambda i: (0, i, 0, 0, 0))
    edge_shape = jax.ShapeDtypeStruct((129, 8, 128), BF16)
    side_shape = jax.ShapeDtypeStruct((3, 8, 8, 128), BF16)
    low, high, side = pl.pallas_call(
        edge_kernel,
        grid=(steps,),
        in_specs=[states_spec, whole((8, 8, 128))],
        out_specs=[whole((129, 8, 128)), whole((129, 8, 128)), whole((3, 8, 8, 128))],
        out_shape=[edge_shape, edge_shape, side_shape],
        scratch_shapes=[pltpu.VMEM((2 * CHUNK * 64, 128), F32), pltpu.VMEM((2, 64, 128), F32)],
        compiler_params=LIMIT,
    )(states, class_map)

    def shift(value, axis, by):
        count = lax.axis_size(axis)
        return lax.ppermute(value, axis, [(i, (i + by) % count) for i in range(count)])

    from_low = shift(high, "gx", 1)
    from_high = shift(low, "gx", -1)
    side_low = shift(side, "gy", 1)
    side_high = shift(side, "gy", -1)

    flux, rows = pl.pallas_call(
        flux_kernel,
        grid=(steps,),
        in_specs=[SMEM, SMEM, SMEM, states_spec, whole((8, 8, 128))]
        + [whole((129, 8, 128))] * 2 + [whole((3, 8, 8, 128))]
        + [whole((129, 8, 128))] * 2 + [whole((3, 8, 8, 128))] * 2,
        out_specs=[pl.BlockSpec((CHUNK, 8, 8, 128), lambda i: (i, 0, 0, 0)), whole((64, 128))],
        out_shape=[
            jax.ShapeDtypeStruct((64, 8, 8, 128), BF16),
            jax.ShapeDtypeStruct((64, 128), F32),
        ],
        scratch_shapes=[
            pltpu.VMEM((4096, 128), F32),
            pltpu.VMEM((8, 8, 128), F32),
            pltpu.VMEM((8, 8, 128), F32),
            pltpu.VMEM((7, 8, 128), F32),
            pltpu.VMEM((2, 8, 128), F32),
            pltpu.VMEM((64, 128), F32),
        ],
        compiler_params=LIMIT,
    )(
        perm_table, candidates.reshape(128, 64), where, states, class_map, low, high, side,
        from_low, from_high, side_low, side_high,
    )

    swap = [(i, i ^ 1) for i in range(8)]
    other_rows = lax.ppermute(rows, "gy", swap)
    spread = pl.pallas_call(
        pair_kernel,
        in_specs=[SMEM, SMEM, whole((64, 128)), whole((64, 128))],
        out_specs=whole((64, 16, 128)),
        out_shape=jax.ShapeDtypeStruct((64, 16, 128), F32),
        scratch_shapes=[pltpu.VMEM((128, 128), F32)],
        compiler_params=LIMIT,
    )(merge_order, where, rows, other_rows)
    peers = [[i * 8 + j * 2 + c for i in range(16) for j in range(4)] for c in range(2)]
    mine = lax.all_to_all(spread, ("gx", "gy"), 0, 0, axis_index_groups=peers)
    other = lax.ppermute(mine, "gy", swap)

    numbers = lax.broadcasted_iota(jnp.int32, (63, 64, 128), 2)
    picks = (merge_order[64:, :64, None] == numbers).astype(BF16)
    kept = pl.pallas_call(
        tree_kernel,
        in_specs=[SMEM, whole((63, 64, 128)), whole((64, 16, 128)), whole((64, 16, 128))],
        out_specs=whole((127, 64, 64)),
        out_shape=jax.ShapeDtypeStruct((127, 64, 64), F32),
        scratch_shapes=[pltpu.VMEM((2, 64, 16, 128), F32), pltpu.VMEM((127, 64, 128), BF16)],
        compiler_params=LIMIT,
    )(where, picks, mine, other)
    return flux, kept


def solution(mesh):
    in_specs = (P(None, None, None, "gx", "gy"), P(None, "gx", "gy"), P(), P(), P())
    out_specs = (P(None, None, "gx", "gy"), P())
    return jax.shard_map(local, mesh=mesh, in_specs=in_specs, out_specs=out_specs, check_vma=False)
```

time: 307 us -> 72.8 us (0.24)
  local copies, waits for them, and re-layouts: 181 us -> 8.69 us
  other arithmetic: 47.8 us -> 0.83 us
  waiting for transfers between devices: 43.6 us -> 9.63 us
  Pallas kernels: 0 us -> 22.8 us
  blocking collectives: 0 us -> 17 us
  between operations: 14.3 us -> 0.68 us
  matrix products: 3.52 us -> 0 us
    gather x20 -> x0, local copies, waits for them, and re-layouts: 104 us -> none  [the longest x19 74 us: kept_sources(): level_ids = jnp.take_along_axis(paired, node_order, axis=1)]
    all_gather x1 -> x0, waiting for transfers between devices: 41.2 us -> none  [collect(): all_rows = lax.all_gather(my_rows[None], ('gx', 'gy'), axis=0, tiled=True)]
    slice x21 -> x1, local copies, waits for them, and re-layouts: 33.8 us -> 0.01 us  [local(): picks = (merge_order[64:, :64, None] == numbers).astype(BF16)]
    pallas_call x0 -> x4, Pallas kernels: none -> 22.8 us  [the longest x1 11.7 us: local(): pl.pallas_call(flux_kernel, grid=(steps,), in_specs=[SMEM, SMEM, SMEM, st...]
    broadcast_in_dim x6 -> x0, local copies, waits for them, and re-layouts: 21.9 us -> none  [the longest x2 10.2 us: neighbour(): jnp.where(column == 0, padded[..., 1:-1, :1], jnp.roll(centre, 1, -1))]
    all_to_all x0 -> x1, blocking collectives: none -> 17 us  [local(): mine = lax.all_to_all(spread, ('gx', 'gy'), 0, 0, axis_index_groups=peers)]
    convert_element_type x1, other arithmetic: 12.3 us -> 0.83 us  [local(): picks = (merge_order[64:, :64, None] == numbers).astype(BF16)]
    add x2 -> x0, other arithmetic: 11.2 us -> none  [the longest x1 6.04 us: local(): perm_pad + jnp.where(class_pad == class_num, perm_table[class_num], 0.0)]
  transfers between devices with their start and end apart: 9 -> 6, of which waited for: 2 -> 5; matrix products, arithmetic and copies ran while one was open for 45% -> 1% of each run, Pallas kernels for 0% -> 0%
where the time goes in v1:
time: 72.8 us; the launch traced here: 72.5 us
  Pallas kernels  22.8 us (31%)
  blocking collectives  17 us (23%)
  starting transfers between devices  12.9 us (18%)
  waiting for transfers between devices  9.63 us (13%)
  local copies, waits for them, and re-layouts  8.69 us (12%)
  other arithmetic  0.83 us (1%)
    all_to_all x1, blocking collectives, local(): mine = lax.all_to_all(spread, ('gx', 'gy'), 0, 0, axis_index_groups=peers)  17 us
    pallas_call x1, Pallas kernels, local(): pl.pallas_call(flux_kernel, grid=(steps,), in_specs=[SMEM, SMEM, SMEM, st...  11.7 us
    ppermute x4, starting transfers between devices, shift(): lax.ppermute(value, axis, [(i, (i + by) % count) for i in range(count)])  8.99 us
    unnamed x15, local copies, waits for them, and re-layouts  8.69 us
    pallas_call x1, Pallas kernels, local(): pl.pallas_call(tree_kernel, in_specs=[SMEM, whole((63, 64, 128)), whole((...  8.08 us
    ppermute x4, waiting for transfers between devices, shift(): lax.ppermute(value, axis, [(i, (i + by) % count) for i in range(count)])  8.07 us
    ppermute x1, starting transfers between devices, local(): other = lax.ppermute(mine, 'gy', swap)  2.05 us
    ppermute x1, starting transfers between devices, local(): other_rows = lax.ppermute(rows, 'gy', swap)  1.87 us
  transfers between devices with their start and end apart: 6, of which 5 were waited for; matrix products, arithmetic and copies ran while one was open for 1% of the time, Pallas kernels for 0%

profile of v1, /device:TPU:1, one launch (start us, length us, event | category | flops | bytes accessed | tf_op | source)
XLA Modules:
  0.0 72.5 jit_solution(3489525912520077630)
XLA Ops:
  0.6 0.0 copy-start
  0.6 1.6 %copy-done = bf16[2,64,8,8,128]{4,3,2,1,0:T(8,128)(2,1)S(1)} copy-done((bf16[2,64,8,8,128]{4,3,2,1,0:T(8,128)(2,1)S(1)}, bf16[2,64,8,8,128]{4,3,2,1,0:T(8,128)(2,1)}, u32[]{:S(2)}) %copy-start) | copy-done | bytes 2097176
  2.2 0.0 copy-start.3
  2.2 0.8 %copy-done.3 = s32[8,8,128]{2,1,0:T(8,128)S(1)} copy-done((s32[8,8,128]{2,1,0:T(8,128)S(1)}, s32[8,8,128]{2,1,0:T(8,128)}, u32[]{:S(2)}) %copy-start.3) | copy-done | bytes 32792
  3.0 0.0 copy-start.1
  3.0 0.0 copy-start.4
  3.0 1.3 %shard_map.68 = (bf16[129,8,128]{2,1,0:T(8,128)(2,1)S(1)}, bf16[129,8,128]{2,1,0:T(8,128)(2,1)S(1)}, bf16[3,8,8,128]{3,2,1,0:T(8,128)(2,1)S(1)}) custom-call(bf16[2,64,8,8,128]{4,3,2,1,0:T(8,128)(2,1)S(1)} %copy-done, s32[8,8,128]{2,1,0:T(8,128)S(1)} %copy-done.3), custom_call_target="tpu_custom_call" | custom-call | tf_op jit(solution)/shard_map/pallas_call | solution.py:222
  4.3 0.0 copy-start.2
  4.3 6.8 %collective-permute-start.1 = (bf16[129,8,128]{2,1,0:T(8,128)(2,1)S(1)}, bf16[129,8,128]{2,1,0:T(8,128)(2,1)S(1)}, u32[]{:S(2)}, u32[]{:S(2)}) collective-permute-start(bf16[129,8,128]{2,1,0:T(8,128)(2,1)S(1)} %get-tuple-element.7.low_ref), channel_id=1, source_target_pairs={{0,120},{8,0},{16,8},{24,16},{32,24},{40,32},{48,40},{56,48},{64,5... | collective-permute-start | bytes 792584 | tf_op jit(solution)/shard_map/ppermute | solution.py:234
  11.2 0.0 collective-permute-start
  11.2 1.0 %collective-permute-start.3 = (bf16[3,8,8,128]{3,2,1,0:T(8,128)(2,1)S(1)}, bf16[3,8,8,128]{3,2,1,0:T(8,128)(2,1)S(1)}, u32[]{:S(2)}, u32[]{:S(2)}) collective-permute-start(bf16[3,8,8,128]{3,2,1,0:T(8,128)(2,1)S(1)} %get-tuple-element.9.side_ref), channel_id=1, source_target_pairs={{0,7},{1,0},{2,1},{3,2},{4,3},{5,4},{6,5},{7,6},{8,15},{9,8},{10,9... | collective-permute-start | bytes 147464 | tf_op jit(solution)/shard_map/ppermute | solution.py:234
  12.1 1.2 %collective-permute-start.2 = (bf16[3,8,8,128]{3,2,1,0:T(8,128)(2,1)S(1)}, bf16[3,8,8,128]{3,2,1,0:T(8,128)(2,1)S(1)}, u32[]{:S(2)}, u32[]{:S(2)}) collective-permute-start(bf16[3,8,8,128]{3,2,1,0:T(8,128)(2,1)S(1)} %get-tuple-element.9.side_ref), channel_id=1, source_target_pairs={{0,1},{1,2},{2,3},{3,4},{4,5},{5,6},{6,7},{7,0},{8,9},{9,10},{10,1... | collective-permute-start | bytes 147464 | tf_op jit(solution)/shard_map/ppermute | solution.py:234
  13.3 1.8 %collective-permute-done.3.side_high_ref = bf16[3,8,8,128]{3,2,1,0:T(8,128)(2,1)S(1)} collective-permute-done((bf16[3,8,8,128]{3,2,1,0:T(8,128)(2,1)S(1)}, bf16[3,8,8,128]{3,2,1,0:T(8,128)(2,1)S(1)}, u32[]{:S(2)}, u32[]{:S(2)}) %collective-permute-start.3) | collective-permute-done | bytes 49184 | tf_op jit(solution)/shard_map/ppermute | solution.py:234
  15.1 0.0 collective-permute-done.2.side_low_ref
  15.1 1.1 %collective-permute-done.1.from_high_ref = bf16[129,8,128]{2,1,0:T(8,128)(2,1)S(1)} collective-permute-done((bf16[129,8,128]{2,1,0:T(8,128)(2,1)S(1)}, bf16[129,8,128]{2,1,0:T(8,128)(2,1)S(1)}, u32[]{:S(2)}, u32[]{:S(2)}) %collective-permute-start.1) | collective-permute-done | bytes 264224 | tf_op jit(solution)/shard_map/ppermute | solution.py:234
  16.2 5.2 %collective-permute-done.from_low_ref = bf16[129,8,128]{2,1,0:T(8,128)(2,1)S(1)} collective-permute-done((bf16[129,8,128]{2,1,0:T(8,128)(2,1)S(1)}, bf16[129,8,128]{2,1,0:T(8,128)(2,1)S(1)}, u32[]{:S(2)}, u32[]{:S(2)}) %collective-permute-start) | collective-permute-done | bytes 264224 | tf_op jit(solution)/shard_map/ppermute | solution.py:234
  21.4 0.0 copy-done.1
  21.4 0.0 copy-done.4
  21.4 0.0 copy-start.5
  21.4 0.8 %copy-done.5 = s32[16,8,64]{2,1,0:T(8,128)S(1)} copy-done((s32[16,8,64]{2,1,0:T(8,128)S(1)}, s32[16,8,64]{2,1,0:T(8,128)}, u32[]{:S(2)}) %copy-start.5) | copy-done | bytes 32792
  22.3 0.0 copy-start.6
  22.3 0.7 copy-done.6
  22.9 11.7 %shard_map.69 = (bf16[64,8,8,128]{3,2,1,0:T(8,128)(2,1)}, f32[64,128]{1,0:T(8,128)S(1)}) custom-call(f32[8]{0:T(128)S(1)} %copy-done.6, s32[128,64]{1,0:T(8,128)S(1)} %bitcast.2, s32[1]{0:T(128)} %bitcast.1.where_ref, bf16[2,64,8,8,128]{4,3,2,1,0:T(8,128)(2,1)S(1)} %copy-done.1, s32[8,8,128]{2,1,0:T(8,128)S(1)} %copy-done.4, ...), custom_call_target="tpu_custom_call" | custom-call | tf_op jit(solution)/shard_map/pallas_call | solution.py:241
  34.6 1.9 %collective-permute-start.4 = (f32[64,128]{1,0:T(8,128)S(1)}, f32[64,128]{1,0:T(8,128)S(1)}, u32[]{:S(2)}, u32[]{:S(2)}) collective-permute-start(f32[64,128]{1,0:T(8,128)S(1)} %get-tuple-element.11.mine_ref), channel_id=1, source_target_pairs={{0,1},{1,0},{2,3},{3,2},{4,5},{5,4},{6,7},{7,6},{8,9},{9,8},{10,11... | collective-permute-start | bytes 98312 | tf_op jit(solution)/shard_map/ppermute | solution.py:267
  36.4 0.9 %collective-permute-done.4.other_ref = f32[64,128]{1,0:T(8,128)S(1)} collective-permute-done((f32[64,128]{1,0:T(8,128)S(1)}, f32[64,128]{1,0:T(8,128)S(1)}, u32[]{:S(2)}, u32[]{:S(2)}) %collective-permute-start.4) | collective-permute-done | bytes 32800 | tf_op jit(solution)/shard_map/ppermute | solution.py:267
  37.3 0.0 copy-done.2
  37.3 1.7 %shard_map.70 = f32[64,16,128]{2,1,0:T(8,128)S(1)} custom-call(s32[127,128]{1,0:T(8,128)S(1)} %copy-done.2, s32[1]{0:T(128)} %bitcast.1.where_ref, f32[64,128]{1,0:T(8,128)S(1)} %get-tuple-element.11.mine_ref, f32[64,128]{1,0:T(8,128)S(1)} %collective-permute-done.4.other_ref), custom_call_target="tpu_custom_call" | custom-call | tf_op jit(solution)/shard_map/pallas_call | solution.py:268
  39.0 17.0 %all_to_all.5.mine_ref = f32[64,16,128]{2,1,0:T(8,128)S(1)} all-to-all(f32[64,16,128]{2,1,0:T(8,128)S(1)} %shard_map.70), channel_id=1, replica_groups={{0,2,4,6,8,10,12,14,16,18,20,22,24,26,28,30,32,34,36,38,40,42,44,46,48,..., dimensions={0} | all-to-all | bytes 1048576 | tf_op jit(solution)/shard_map/all_to_all | solution.py:277
  56.0 2.0 %collective-permute-start.5 = (f32[64,16,128]{2,1,0:T(8,128)S(1)}, f32[64,16,128]{2,1,0:T(8,128)S(1)}, u32[]{:S(2)}, u32[]{:S(2)}) collective-permute-start(f32[64,16,128]{2,1,0:T(8,128)S(1)} %all_to_all.5.mine_ref), channel_id=1, source_target_pairs={{0,1},{1,0},{2,3},{3,2},{4,5},{5,4},{6,7},{7,6},{8,9},{9,8},{10,11... | collective-permute-start | bytes 1572872 | tf_op jit(solution)/shard_map/ppermute | solution.py:278
  58.1 0.8 %fusion.pick_ref = bf16[63,64,128]{2,1,0:T(8,128)(2,1)S(1)} fusion(s32[63,64]{1,0:T(8,128)S(1)} %slice.3), kind=kLoop, calls=%fused_computation.1 | loop fusion | flops 1032192 | bytes 1048320 | tf_op jit(solution)/shard_map/convert_element_type | solution.py:281
  58.9 0.7 collective-permute-done.5.other_ref
  59.6 8.1 %shard_map.71 = f32[127,64,64]{2,1,0:T(8,128)} custom-call(s32[1]{0:T(128)} %bitcast.1.where_ref, bf16[63,64,128]{2,1,0:T(8,128)(2,1)S(1)} %fusion.pick_ref, f32[64,16,128]{2,1,0:T(8,128)S(1)} %all_to_all.5.mine_ref, f32[64,16,128]{2,1,0:T(8,128)S(1)} %collective-permute-done.5.other_ref), custom_call_target="tpu_custom_call" | custom-call | tf_op jit(solution)/shard_map/pallas_call | solution.py:282
  67.7 4.8 %copy.7 = f32[127,64,64]{0,2,1:T(8,128)} copy(f32[127,64,64]{2,1,0:T(8,128)} %shard_map.71) | data formatting | bytes 4161536
  (1 shorter events, 0.0 us)
Async XLA Ops:
  0.6 1.6 %copy-start = (bf16[2,64,8,8,128]{4,3,2,1,0:T(8,128)(2,1)S(1)}, bf16[2,64,8,8,128]{4,3,2,1,0:T(8,128)(2,1)}, u32[]{:S(2)}) copy-start(bf16[2,64,8,8,128]{4,3,2,1,0:T(8,128)(2,1)} %states_ref.3) | copy-start | bytes 6291460
  2.2 0.8 %copy-start.3 = (s32[8,8,128]{2,1,0:T(8,128)S(1)}, s32[8,8,128]{2,1,0:T(8,128)}, u32[]{:S(2)}) copy-start(s32[8,8,128]{2,1,0:T(8,128)} %class_ref.3) | copy-start | bytes 98308
  3.0 18.4 %copy-start.1 = (bf16[2,64,8,8,128]{4,3,2,1,0:T(8,128)(2,1)S(1)}, bf16[2,64,8,8,128]{4,3,2,1,0:T(8,128)(2,1)}, u32[]{:S(2)}) copy-start(bf16[2,64,8,8,128]{4,3,2,1,0:T(8,128)(2,1)} %states_ref.3) | copy-start | bytes 6291460
  3.0 18.4 %copy-start.4 = (s32[8,8,128]{2,1,0:T(8,128)S(1)}, s32[8,8,128]{2,1,0:T(8,128)}, u32[]{:S(2)}) copy-start(s32[8,8,128]{2,1,0:T(8,128)} %class_ref.3) | copy-start | bytes 98308
  4.3 33.0 %copy-start.2 = (s32[127,128]{1,0:T(8,128)S(1)}, s32[127,128]{1,0:T(8,128)}, u32[]{:S(2)}) copy-start(s32[127,128]{1,0:T(8,128)} %order_ref.1) | copy-start | bytes 195076
  4.3 11.9 %collective-permute-start.1 = (bf16[129,8,128]{2,1,0:T(8,128)(2,1)S(1)}, bf16[129,8,128]{2,1,0:T(8,128)(2,1)S(1)}, u32[]{:S(2)}, u32[]{:S(2)}) collective-permute-start(bf16[129,8,128]{2,1,0:T(8,128)(2,1)S(1)} %get-tuple-element.7.low_ref), channel_id=1, source_target_pairs={{0,120},{8,0},{16,8},{24,16},{32,24},{40,32},{48,40},{56,48},{64,5... | collective-permute-start | bytes 792584 | tf_op jit(solution)/shard_map/ppermute | solution.py:234
  11.2 10.2 %collective-permute-start = (bf16[129,8,128]{2,1,0:T(8,128)(2,1)S(1)}, bf16[129,8,128]{2,1,0:T(8,128)(2,1)S(1)}, u32[]{:S(2)}, u32[]{:S(2)}) collective-permute-start(bf16[129,8,128]{2,1,0:T(8,128)(2,1)S(1)} %get-tuple-element.8.high_ref), channel_id=1, source_target_pairs={{0,8},{8,16},{16,24},{24,32},{32,40},{40,48},{48,56},{56,64},{64,7... | collective-permute-start | bytes 792584 | tf_op jit(solution)/shard_map/ppermute | solution.py:234
  11.2 3.9 %collective-permute-start.3 = (bf16[3,8,8,128]{3,2,1,0:T(8,128)(2,1)S(1)}, bf16[3,8,8,128]{3,2,1,0:T(8,128)(2,1)S(1)}, u32[]{:S(2)}, u32[]{:S(2)}) collective-permute-start(bf16[3,8,8,128]{3,2,1,0:T(8,128)(2,1)S(1)} %get-tuple-element.9.side_ref), channel_id=1, source_target_pairs={{0,7},{1,0},{2,1},{3,2},{4,3},{5,4},{6,5},{7,6},{8,15},{9,8},{10,9... | collective-permute-start | bytes 147464 | tf_op jit(solution)/shard_map/ppermute | solution.py:234
  12.1 3.0 %collective-permute-start.2 = (bf16[3,8,8,128]{3,2,1,0:T(8,128)(2,1)S(1)}, bf16[3,8,8,128]{3,2,1,0:T(8,128)(2,1)S(1)}, u32[]{:S(2)}, u32[]{:S(2)}) collective-permute-start(bf16[3,8,8,128]{3,2,1,0:T(8,128)(2,1)S(1)} %get-tuple-element.9.side_ref), channel_id=1, source_target_pairs={{0,1},{1,2},{2,3},{3,4},{4,5},{5,6},{6,7},{7,0},{8,9},{9,10},{10,1... | collective-permute-start | bytes 147464 | tf_op jit(solution)/shard_map/ppermute | solution.py:234
  21.4 0.8 %copy-start.5 = (s32[16,8,64]{2,1,0:T(8,128)S(1)}, s32[16,8,64]{2,1,0:T(8,128)}, u32[]{:S(2)}) copy-start(s32[16,8,64]{2,1,0:T(8,128)} %param.8) | copy-start | bytes 98308
  22.3 0.7 copy-start.6
  34.6 2.7 %collective-permute-start.4 = (f32[64,128]{1,0:T(8,128)S(1)}, f32[64,128]{1,0:T(8,128)S(1)}, u32[]{:S(2)}, u32[]{:S(2)}) collective-permute-start(f32[64,128]{1,0:T(8,128)S(1)} %get-tuple-element.11.mine_ref), channel_id=1, source_target_pairs={{0,1},{1,0},{2,3},{3,2},{4,5},{5,4},{6,7},{7,6},{8,9},{9,8},{10,11... | collective-permute-start | bytes 98312 | tf_op jit(solution)/shard_map/ppermute | solution.py:267
  56.0 3.6 %collective-permute-start.5 = (f32[64,16,128]{2,1,0:T(8,128)S(1)}, f32[64,16,128]{2,1,0:T(8,128)S(1)}, u32[]{:S(2)}, u32[]{:S(2)}) collective-permute-start(f32[64,16,128]{2,1,0:T(8,128)S(1)} %all_to_all.5.mine_ref), channel_id=1, source_target_pairs={{0,1},{1,0},{2,3},{3,2},{4,5},{5,4},{6,7},{7,6},{8,9},{9,8},{10,11... | collective-permute-start | bytes 1572872 | tf_op jit(solution)/shard_map/ppermute | solution.py:278

commit v2 on v0

v2 whole, which is shorter than its diff:
```python
import jax
import jax.numpy as jnp
from jax import lax
from jax.experimental import pallas as pl
from jax.experimental.pallas import tpu as pltpu
from jax.sharding import PartitionSpec as P

F32 = jnp.float32
BF16 = jnp.bfloat16
PARTS = 8
PER = 64 // PARTS
CUBE = (8, 8, 128)
FLAT = (64, 128)
HBM = pl.BlockSpec(memory_space=pltpu.HBM)
SMEM = pl.BlockSpec(memory_space=pltpu.SMEM)
LIMIT = pltpu.CompilerParams(vmem_limit_bytes=48 * 1024 * 1024)


def whole(shape):
    return pl.BlockSpec(shape, lambda *_: (0,) * len(shape))


def lane_of(shape):
    return lax.broadcasted_iota(jnp.int32, shape, len(shape) - 1)


def turn(value, by):
    return pltpu.roll(value, by, 1)


def look_up(kind, table_ref):
    value = jnp.zeros(kind.shape, F32)
    for number in range(8):
        value = jnp.where(kind == number, table_ref[number], value)
    return value


def trans(k_here, k_next):
    return k_here * k_next / (k_here + k_next)


def face(t, m_here, m_next, p_here, p_next):
    return t * (m_here + m_next) * (p_next - p_here)


def three_pieces(value):
    high = value.astype(BF16)
    rest = value - high.astype(F32)
    middle = rest.astype(BF16)
    return high, middle, (rest - middle.astype(F32)).astype(BF16)


def part_copy(states_hbm, states_ref, sem, part):
    span = pl.ds(part * PER, PER)
    return pltpu.make_async_copy(states_hbm.at[:, span], states_ref.at[:, span], sem.at[part])


def edge_kernel(
    table_hbm, class_hbm, states_hbm, low_ref, high_ref, side_ref,
    states_ref, class_ref, table_ref, wide_ref, sem, small_sem,
):
    get_table = pltpu.make_async_copy(table_hbm, table_ref, small_sem.at[0])
    get_class = pltpu.make_async_copy(class_hbm, class_ref, small_sem.at[1])
    get_table.start()
    get_class.start()
    for part in range(PARTS):
        part_copy(states_hbm, states_ref, sem, part).start()
    lane = lane_of(FLAT)
    get_table.wait()
    get_class.wait()
    perm = look_up(class_ref[...], table_ref)
    wide_ref[pl.ds(0, 64), :] = perm.reshape(FLAT)
    for ref, at in ((low_ref, 0), (high_ref, 7)):
        for n, piece in enumerate(three_pieces(wide_ref[pl.ds(at, 8, stride=8), :])):
            ref[128 + n] = piece
    first = jnp.broadcast_to(perm[:, :, 0:1], CUBE)
    last = jnp.broadcast_to(perm[:, :, 127:128], CUBE)
    for n, piece in enumerate(three_pieces(jnp.where(lane_of(CUBE) % 2 == 0, first, last))):
        side_ref[2 + n] = piece
    acc = [jnp.zeros(FLAT, F32), jnp.zeros(FLAT, F32)]
    for part in range(PARTS):
        part_copy(states_hbm, states_ref, sem, part).wait()
        for k in range(PER):
            snap = part * PER + k
            for field in range(2):
                value = states_ref[field, snap].astype(F32).reshape(FLAT)
                slot = (1 + field + 2 * snap) * 64
                wide_ref[pl.ds(slot, 64), :] = value
                keep = (lane == 2 * snap) | (lane == (2 * snap + 127) % 128)
                acc[field] = jnp.where(keep, turn(value, 2 * snap), acc[field])
                low_ref[field * 64 + snap] = wide_ref[pl.ds(slot, 8, stride=8), :].astype(BF16)
                high_ref[field * 64 + snap] = wide_ref[pl.ds(slot + 7, 8, stride=8), :].astype(BF16)
    for field in range(2):
        side_ref[field] = acc[field].reshape(CUBE).astype(BF16)


def inner_kernel(
    table_hbm, class_hbm, states_hbm, out_ref,
    states_ref, class_ref, table_ref, tx_ref, ty_ref, tz_ref, sem, small_sem,
):
    get_table = pltpu.make_async_copy(table_hbm, table_ref, small_sem.at[0])
    get_class = pltpu.make_async_copy(class_hbm, class_ref, small_sem.at[1])
    get_table.start()
    get_class.start()
    for part in range(PARTS):
        part_copy(states_hbm, states_ref, sem, part).start()
    get_table.wait()
    get_class.wait()
    perm = look_up(class_ref[...], table_ref)
    row = lax.broadcasted_iota(jnp.int32, CUBE, 1)
    next_y = turn(perm.reshape(FLAT), 127).reshape(CUBE)
    tx_ref[...] = jnp.where(row == 7, 0.0, trans(perm, jnp.roll(perm, -1, 1)))
    ty_ref[...] = jnp.where(lane_of(CUBE) == 127, 0.0, trans(perm, next_y))
    tz_ref[...] = trans(perm[:-1], perm[1:])
    for part in range(PARTS):
        part_copy(states_hbm, states_ref, sem, part).wait()
        for k in range(PER):
            snap = part * PER + k
            p = states_ref[0, snap].astype(F32)
            s = states_ref[1, snap].astype(F32)
            m = s * s
            fx = face(tx_ref[...], m, jnp.roll(m, -1, 1), p, jnp.roll(p, -1, 1))
            total = fx - jnp.roll(fx, 1, 1)
            pf, mf = p.reshape(FLAT), m.reshape(FLAT)
            fy = face(ty_ref[...].reshape(FLAT), mf, turn(mf, 127), pf, turn(pf, 127))
            total = total + (fy - turn(fy, 1)).reshape(CUBE)
            fz = face(tz_ref[...], m[:-1], m[1:], p[:-1], p[1:])
            zero = jnp.zeros((1, 8, 128), F32)
            total = total + (jnp.concatenate([fz, zero], 0) - jnp.concatenate([zero, fz], 0))
            out_ref[pl.ds(snap * 64, 64), :] = total.reshape(FLAT)


def outer_kernel(
    where_ref, cand_hbm, order_hbm, inner_ref, low_ref, high_ref, side_ref,
    from_low_ref, from_high_ref, side_low_ref, side_high_ref,
    out_hbm, mine_ref, send_ref,
    flux_ref, out_ref, txe_ref, qy_ref, cand_ref, order_ref, sem, small_sem,
):
    tile = where_ref[0]
    core = tile % 2
    get_cand = pltpu.make_async_copy(cand_hbm.at[pl.ds(tile, 1)], cand_ref, small_sem.at[0])
    get_order = pltpu.make_async_copy(order_hbm.at[pl.ds(tile // 2, 1)], order_ref, small_sem.at[1])
    get_cand.start()
    get_order.start()
    lane = lane_of(FLAT)

    def perm_of(ref, at):
        high, middle, low = (ref[at + n].astype(F32) for n in range(3))
        return (high + middle) + low

    txe_ref[0] = trans(perm_of(low_ref, 128), perm_of(from_low_ref, 128))
    txe_ref[1] = trans(perm_of(high_ref, 128), perm_of(from_high_ref, 128))

    def beyond(below, above):
        below, above = below.reshape(FLAT), above.reshape(FLAT)
        return jnp.where(lane % 2 == 0, turn(below, 1), turn(above, 127))

    t_side = trans(
        perm_of(side_ref, 2).reshape(FLAT), beyond(perm_of(side_low_ref, 2), perm_of(side_high_ref, 2))
    )

    def side_pair(which):
        here = side_ref[which].astype(F32).reshape(FLAT)
        return here, beyond(side_low_ref[which].astype(F32), side_high_ref[which].astype(F32))

    p_here, p_next = side_pair(0)
    s_here, s_next = side_pair(1)
    qy_ref[...] = face(t_side, s_here * s_here, s_next * s_next, p_here, p_next)
    at_edge = (lane == 0) | (lane == 127)

    def edge(own_ref, other_ref, which, snap):
        s_here, s_next = own_ref[64 + snap].astype(F32), other_ref[64 + snap].astype(F32)
        p_here, p_next = own_ref[snap].astype(F32), other_ref[snap].astype(F32)
        return face(txe_ref[which], s_here * s_here, s_next * s_next, p_here, p_next)

    def put(part):
        span = pl.ds(part * PER, PER)
        return pltpu.make_async_copy(out_ref.at[span], out_hbm.at[span], sem.at[part])

    for part in range(PARTS):
        for k in range(PER):
            snap = part * PER + k
            start = snap * 64
            turned = turn(qy_ref[...], (128 - 2 * snap) % 128)
            flux_ref[pl.ds(start, 64), :] = inner_ref[pl.ds(start, 64), :] + jnp.where(at_edge, turned, 0.0)
            low, high = pl.ds(start, 8, stride=8), pl.ds(start + 7, 8, stride=8)
            flux_ref[low, :] = flux_ref[low, :] + edge(low_ref, from_low_ref, 0, snap)
            flux_ref[high, :] = flux_ref[high, :] + edge(high_ref, from_high_ref, 1, snap)
        for k in range(PER):
            snap = part * PER + k
            out_ref[snap] = flux_ref[pl.ds(snap * 64, 64), :].reshape(CUBE).astype(BF16)
        put(part).start()

    get_cand.wait()
    get_order.wait()

    def pick(i, acc):
        source = order_ref[0, i]
        cell = cand_ref[0, source % 64]
        slot = (i + 32 * core) % 64
        values = flux_ref[pl.ds(cell // 128, 64, stride=64), :]
        turned = turn(values, (slot - cell % 128 + 128) % 128)
        return jnp.where(lane == jnp.where(source // 64 == core, slot, -1), turned, acc)

    acc = lax.fori_loop(0, 64, pick, jnp.zeros(FLAT, F32), unroll=8)
    rows = jnp.transpose(jnp.concatenate([acc, jnp.zeros(FLAT, F32)], 0))
    mine_ref[...] = rows[:32]
    send_ref[...] = rows[32:64]
    for part in range(PARTS):
        put(part).wait()


def tree_kernel(
    where_ref, pick_ref, mine_ref, other_ref, out_hbm, half_ref, level_ref, kept_ref, out_ref, sem
):
    core = where_ref[0] % 2
    half_ref[core] = mine_ref[...]
    half_ref[1 - core] = other_ref[...]
    left = lane_of((32, 128)) < 64

    def keep(node, upper, lower):
        upper, lower = upper + turn(upper, 64), lower + turn(lower, 64)
        kept_ref[pl.ds(node * 32, 32), :] = jnp.where(left, upper, lower)

    for chip in range(64):
        keep(chip, half_ref[0, chip].astype(F32), half_ref[1, chip].astype(F32))
    before, offset, count = 0, 64, 32
    while count >= 1:
        for j in range(count):
            first = before + 2 * j
            if before == 0:
                stack = jnp.concatenate(
                    [half_ref[0, first], half_ref[1, first], half_ref[0, first + 1], half_ref[1, first + 1]], 0
                )
            else:
                stack = level_ref[pl.ds(first - 64, 2)].reshape(128, 128)
            got = jnp.dot(pick_ref[offset - 64 + j], stack, preferred_element_type=F32)
            level_ref[offset - 64 + j] = got.astype(BF16)
            keep(offset + j, got[:32], got[32:])
        before, offset, count = offset, offset + count, count // 2

    def put(at):
        span = pl.ds(at, 4)
        return pltpu.make_async_copy(out_ref.at[span], out_hbm.at[span], sem.at[at // 4])

    for group in range(8):
        for q in range(4 * group, 4 * group + 4):
            turned = jnp.transpose(kept_ref[pl.ds(q, 128, stride=32), :])
            out_ref[q] = turned[:64, :127]
            out_ref[q + 32] = turned[64:, :127]
        put(4 * group).start()
        put(4 * group + 32).start()
    for at in range(0, 64, 4):
        put(at).wait()


def local(states, class_map, perm_table, candidates, merge_order):
    tile = lax.axis_index("gx") * lax.axis_size("gy") + lax.axis_index("gy")
    where = tile.reshape(1).astype(jnp.int32)
    states, class_map, perm_table, candidates, merge_rows = (
        pltpu.with_memory_space_constraint(value, pltpu.HBM)
        for value in (states, class_map, perm_table, candidates.reshape(128, 64), merge_order)
    )
    edge_shape, side_shape = (131, 8, 128), (5, 8, 8, 128)
    states_scratch = [
        pltpu.VMEM((2, 64, 8, 8, 128), BF16), pltpu.VMEM(CUBE, jnp.int32), pltpu.SMEM((8,), F32)
    ]
    sems = [pltpu.SemaphoreType.DMA((PARTS,)), pltpu.SemaphoreType.DMA((2,))]
    low, high, side = pl.pallas_call(
        edge_kernel,
        in_specs=[HBM, HBM, HBM],
        out_specs=[whole(edge_shape), whole(edge_shape), whole(side_shape)],
        out_shape=[
            jax.ShapeDtypeStruct(edge_shape, BF16),
            jax.ShapeDtypeStruct(edge_shape, BF16),
            jax.ShapeDtypeStruct(side_shape, BF16),
        ],
        scratch_shapes=states_scratch + [pltpu.VMEM((129 * 64, 128), F32)] + sems,
        compiler_params=LIMIT,
    )(perm_table, class_map, states)

    def shift(value, axis, by):
        count = lax.axis_size(axis)
        return lax.ppermute(value, axis, [(i, (i + by) % count) for i in range(count)])

    from_low = shift(high, "gx", 1)
    from_high = shift(low, "gx", -1)
    side_low = shift(side, "gy", 1)
    side_high = shift(side, "gy", -1)

    inner = pl.pallas_call(
        inner_kernel,
        in_specs=[HBM, HBM, HBM],
        out_specs=whole((4096, 128)),
        out_shape=jax.ShapeDtypeStruct((4096, 128), F32),
        scratch_shapes=states_scratch
        + [pltpu.VMEM(CUBE, F32), pltpu.VMEM(CUBE, F32), pltpu.VMEM((7, 8, 128), F32)]
        + sems,
        compiler_params=LIMIT,
    )(perm_table, class_map, states)

    flux, mine_rows, send_rows = pl.pallas_call(
        outer_kernel,
        in_specs=[SMEM, HBM, HBM, whole((4096, 128))]
        + [whole(edge_shape)] * 2 + [whole(side_shape)] + [whole(edge_shape)] * 2 + [whole(side_shape)] * 2,
        out_specs=[HBM, whole((32, 128)), whole((32, 128))],
        out_shape=[
            jax.ShapeDtypeStruct((64, 8, 8, 128), BF16),
            jax.ShapeDtypeStruct((32, 128), F32),
            jax.ShapeDtypeStruct((32, 128), F32),
        ],
        scratch_shapes=[
            pltpu.VMEM((4096, 128), F32),
            pltpu.VMEM((64, 8, 8, 128), BF16),
            pltpu.VMEM((2, 8, 128), F32),
            pltpu.VMEM(FLAT, F32),
            pltpu.SMEM((1, 64), jnp.int32),
            pltpu.SMEM((1, 128), jnp.int32),
        ]
        + sems,
        compiler_params=LIMIT,
    )(
        where, candidates, merge_rows, inner, low, high, side,
        from_low, from_high, side_low, side_high,
    )

    swap = [(i, i ^ 1) for i in range(8)]
    got_rows = lax.ppermute(send_rows, "gy", swap)
    merged = mine_rows[:, :64] + got_rows[:, :64]
    top = merged.astype(BF16)
    rest = (merged - lax.reduce_precision(merged, 8, 7)).astype(BF16)
    spread = jnp.broadcast_to(jnp.concatenate([top, rest], 1)[None], (64, 32, 128))
    peers = [[i * 8 + j * 2 + c for i in range(16) for j in range(4)] for c in range(2)]
    mine = lax.all_to_all(spread, ("gx", "gy"), 0, 0, axis_index_groups=peers)
    other = lax.ppermute(mine, "gy", swap)

    numbers = lax.broadcasted_iota(jnp.int32, (63, 64, 128), 2)
    picks = (merge_order[64:, :64, None] == numbers).astype(BF16)
    kept = pl.pallas_call(
        tree_kernel,
        in_specs=[SMEM, whole((63, 64, 128)), whole((64, 32, 128)), whole((64, 32, 128))],
        out_specs=HBM,
        out_shape=jax.ShapeDtypeStruct((64, 64, 127), F32),
        scratch_shapes=[
            pltpu.VMEM((2, 64, 32, 128), BF16),
            pltpu.VMEM((63, 64, 128), BF16),
            pltpu.VMEM((128 * 32, 128), F32),
            pltpu.VMEM((64, 64, 127), F32),
            pltpu.SemaphoreType.DMA((16,)),
        ],
        compiler_params=LIMIT,
    )(where, picks, mine, other)
    return flux, jnp.transpose(kept, (2, 0, 1))


def solution(mesh):
    in_specs = (P(None, None, None, "gx", "gy"), P(None, "gx", "gy"), P(), P(), P())
    out_specs = (P(None, None, "gx", "gy"), P())
    return jax.shard_map(local, mesh=mesh, in_specs=in_specs, out_specs=out_specs, check_vma=False)
```

time: 307 us -> 52 us (0.17)
  local copies, waits for them, and re-layouts: 181 us -> 0.08 us
  other arithmetic: 47.8 us -> 0.92 us
  waiting for transfers between devices: 43.6 us -> 1.54 us
  blocking collectives: 0 us -> 20.2 us
  Pallas kernels: 0 us -> 15.4 us
  between operations: 14.3 us -> 0.72 us
  matrix products: 3.52 us -> 0 us
    gather x20 -> x0, local copies, waits for them, and re-layouts: 104 us -> none  [the longest x19 74 us: kept_sources(): level_ids = jnp.take_along_axis(paired, node_order, axis=1)]
    all_gather x1 -> x0, waiting for transfers between devices: 41.2 us -> none  [collect(): all_rows = lax.all_gather(my_rows[None], ('gx', 'gy'), axis=0, tiled=True)]
    slice x21 -> x1, local copies, waits for them, and re-layouts: 33.8 us -> 0.01 us  [local(): picks = (merge_order[64:, :64, None] == numbers).astype(BF16)]
    broadcast_in_dim x6 -> x1, local copies, waits for them, and re-layouts: 21.9 us -> 0.07 us  [local(): jnp.broadcast_to(jnp.concatenate([top, rest], 1)[None], (64, 32, 128))]
    all_to_all x0 -> x1, blocking collectives: none -> 20.2 us  [local(): mine = lax.all_to_all(spread, ('gx', 'gy'), 0, 0, axis_index_groups=peers)]
    pallas_call x0 -> x4, Pallas kernels: none -> 15.4 us  [the longest x1 4.75 us: local(): pl.pallas_call(inner_kernel, in_specs=[HBM, HBM, HBM], out_specs=whole((4...]
    convert_element_type x1 -> x2, other arithmetic: 12.3 us -> 0.84 us  [the longest x1 0.83 us: local(): picks = (merge_order[64:, :64, None] == numbers).astype(BF16)]
    add x2 -> x0, other arithmetic: 11.2 us -> none  [the longest x1 6.04 us: local(): perm_pad + jnp.where(class_pad == class_num, perm_table[class_num], 0.0)]
  transfers between devices with their start and end apart: 9 -> 6, of which waited for: 2 -> 2; matrix products, arithmetic and copies ran while one was open for 45% -> 2% of each run, Pallas kernels for 0% -> 9%
where the time goes in v2:
time: 52 us; the launch traced here: 51.8 us
  blocking collectives  20.2 us (39%)
  Pallas kernels  15.4 us (30%)
  starting transfers between devices  13 us (25%)
  waiting for transfers between devices  1.54 us (3%)
  other arithmetic  0.92 us (2%)
  between operations  0.72 us (1%)
    all_to_all x1, blocking collectives, local(): mine = lax.all_to_all(spread, ('gx', 'gy'), 0, 0, axis_index_groups=peers)  20.2 us
    ppermute x4, starting transfers between devices, shift(): lax.ppermute(value, axis, [(i, (i + by) % count) for i in range(count)])  9.07 us
    pallas_call x1, Pallas kernels, local(): pl.pallas_call(inner_kernel, in_specs=[HBM, HBM, HBM], out_specs=whole((4...  4.75 us
    pallas_call x1, Pallas kernels, local(): pl.pallas_call(outer_kernel, in_specs=[SMEM, HBM, HBM, whole((4096, 128))...  4.46 us
    pallas_call x1, Pallas kernels, local(): pl.pallas_call(tree_kernel, in_specs=[SMEM, whole((63, 64, 128)), whole((...  3.4 us
    pallas_call x1, Pallas kernels, local(): pl.pallas_call(edge_kernel, in_specs=[HBM, HBM, HBM], out_specs=[whole(ed...  2.78 us
    ppermute x1, starting transfers between devices, local(): other = lax.ppermute(mine, 'gy', swap)  2.04 us
    ppermute x1, starting transfers between devices, local(): got_rows = lax.ppermute(send_rows, 'gy', swap)  1.85 us
  transfers between devices with their start and end apart: 6, of which 2 were waited for; matrix products, arithmetic and copies ran while one was open for 2% of the time, Pallas kernels for 9%

profile of v2, /device:TPU:1, one launch (start us, length us, event | category | flops | bytes accessed | tf_op | source)
XLA Modules:
  0.0 51.8 jit_solution(16733796088692947056)
XLA Ops:
  0.6 2.8 %shard_map.69 = (bf16[131,8,128]{2,1,0:T(8,128)(2,1)S(1)}, bf16[131,8,128]{2,1,0:T(8,128)(2,1)S(1)}, bf16[5,8,8,128]{3,2,1,0:T(8,128)(2,1)S(1)}) custom-call(f32[8]{0:T(128)} %table_hbm.3, s32[8,8,128]{2,1,0:T(8,128)} %class_hbm.3, bf16[2,64,8,8,128]{4,3,2,1,0:T(8,128)(2,1)} %states_hbm.3), custom_call_target="tpu_custom_call" | custom-call | tf_op jit(solution)/shard_map/pallas_call | solution.py:269
  3.4 2.5 %collective-permute-start = (bf16[131,8,128]{2,1,0:T(8,128)(2,1)S(1)}, bf16[131,8,128]{2,1,0:T(8,128)(2,1)S(1)}, u32[]{:S(2)}, u32[]{:S(2)}) collective-permute-start(bf16[131,8,128]{2,1,0:T(8,128)(2,1)S(1)} %get-tuple-element.9.high_ref), channel_id=1, source_target_pairs={{0,8},{8,16},{16,24},{24,32},{32,40},{40,48},{48,56},{56,64},{64,7... | collective-permute-start | bytes 804872 | tf_op jit(solution)/shard_map/ppermute | solution.py:284
  5.9 4.4 %collective-permute-start.1 = (bf16[131,8,128]{2,1,0:T(8,128)(2,1)S(1)}, bf16[131,8,128]{2,1,0:T(8,128)(2,1)S(1)}, u32[]{:S(2)}, u32[]{:S(2)}) collective-permute-start(bf16[131,8,128]{2,1,0:T(8,128)(2,1)S(1)} %get-tuple-element.8.low_ref), channel_id=1, source_target_pairs={{0,120},{8,0},{16,8},{24,16},{32,24},{40,32},{48,40},{56,48},{64,5... | collective-permute-start | bytes 804872 | tf_op jit(solution)/shard_map/ppermute | solution.py:284
  10.3 2.1 %collective-permute-start.2 = (bf16[5,8,8,128]{3,2,1,0:T(8,128)(2,1)S(1)}, bf16[5,8,8,128]{3,2,1,0:T(8,128)(2,1)S(1)}, u32[]{:S(2)}, u32[]{:S(2)}) collective-permute-start(bf16[5,8,8,128]{3,2,1,0:T(8,128)(2,1)S(1)} %get-tuple-element.10.side_ref), channel_id=1, source_target_pairs={{0,1},{1,2},{2,3},{3,4},{4,5},{5,6},{6,7},{7,0},{8,9},{9,10},{10,1... | collective-permute-start | bytes 245768 | tf_op jit(solution)/shard_map/ppermute | solution.py:284
  12.5 0.0 collective-permute-start.3
  12.5 4.7 %shard_map.68.inner_ref = f32[4096,128]{1,0:T(8,128)S(1)} custom-call(f32[8]{0:T(128)} %table_hbm.3, s32[8,8,128]{2,1,0:T(8,128)} %class_hbm.3, bf16[2,64,8,8,128]{4,3,2,1,0:T(8,128)(2,1)} %states_hbm.3), custom_call_target="tpu_custom_call" | custom-call | tf_op jit(solution)/shard_map/pallas_call | solution.py:291
  17.2 0.0 collective-permute-done.2.side_low_ref
  17.3 0.0 collective-permute-done.3.side_high_ref
  17.3 0.0 collective-permute-done.from_low_ref
  17.3 0.0 collective-permute-done.1.from_high_ref
  17.3 0.0 copy-start
  17.3 4.5 %shard_map.70 = (bf16[64,8,8,128]{3,2,1,0:T(8,128)(2,1)}, f32[32,128]{1,0:T(8,128)S(1)}, f32[32,128]{1,0:T(8,128)S(1)}) custom-call(s32[1]{0:T(128)} %bitcast.where_ref, s32[128,64]{1,0:T(8,128)} %bitcast.4, s32[127,128]{1,0:T(8,128)} %order_hbm.1, f32[4096,128]{1,0:T(8,128)S(1)} %shard_map.68.inner_ref, bf16[131,8,128]{2,1,0:T(8,128)(2,1)S(1)} %get-tuple-element.8.low_ref, ...), custom_call_target="tpu_custom_call" | custom-call | tf_op jit(solution)/shard_map/pallas_call | solution.py:302
  21.8 1.9 %collective-permute-start.4 = (f32[32,128]{1,0:T(8,128)S(1)}, f32[32,128]{1,0:T(8,128)S(1)}, u32[]{:S(2)}, u32[]{:S(2)}) collective-permute-start(f32[32,128]{1,0:T(8,128)S(1)} %get-tuple-element.13), channel_id=1, source_target_pairs={{0,1},{1,0},{2,3},{3,2},{4,5},{5,4},{6,7},{7,6},{8,9},{9,8},{10,11... | collective-permute-start | bytes 49160 | tf_op jit(solution)/shard_map/ppermute | solution.py:328
  23.6 0.8 %collective-permute-done.4 = f32[32,128]{1,0:T(8,128)S(1)} collective-permute-done((f32[32,128]{1,0:T(8,128)S(1)}, f32[32,128]{1,0:T(8,128)S(1)}, u32[]{:S(2)}, u32[]{:S(2)}) %collective-permute-start.4) | collective-permute-done | bytes 16416 | tf_op jit(solution)/shard_map/ppermute | solution.py:328
  24.5 0.1 pad_maximum_fusion
  24.5 0.1 broadcast_in_dim.2
  24.6 20.2 %all_to_all.5.mine_ref = bf16[64,32,128]{2,1,0:T(8,128)(2,1)S(1)} all-to-all(bf16[64,32,128]{2,1,0:T(8,128)(2,1)S(1)} %broadcast_in_dim.2), channel_id=1, replica_groups={{0,2,4,6,8,10,12,14,16,18,20,22,24,26,28,30,32,34,36,38,40,42,44,46,48,..., dimensions={0} | all-to-all | bytes 1048576 | tf_op jit(solution)/shard_map/all_to_all | solution.py:334
  44.8 2.0 %collective-permute-start.5 = (bf16[64,32,128]{2,1,0:T(8,128)(2,1)S(1)}, bf16[64,32,128]{2,1,0:T(8,128)(2,1)S(1)}, u32[]{:S(2)}, u32[]{:S(2)}) collective-permute-start(bf16[64,32,128]{2,1,0:T(8,128)(2,1)S(1)} %all_to_all.5.mine_ref), channel_id=1, source_target_pairs={{0,1},{1,0},{2,3},{3,2},{4,5},{5,4},{6,7},{7,6},{8,9},{9,8},{10,11... | collective-permute-start | bytes 1572872 | tf_op jit(solution)/shard_map/ppermute | solution.py:335
  46.8 0.0 copy-done
  46.8 0.8 %fusion.pick_ref = bf16[63,64,128]{2,1,0:T(8,128)(2,1)S(1)} fusion(s32[63,64]{1,0:T(8,128)S(1)} %slice.9), kind=kLoop, calls=%fused_computation.1 | loop fusion | flops 1032192 | bytes 1048320 | tf_op jit(solution)/shard_map/convert_element_type | solution.py:338
  47.7 0.7 %collective-permute-done.5.other_ref = bf16[64,32,128]{2,1,0:T(8,128)(2,1)S(1)} collective-permute-done((bf16[64,32,128]{2,1,0:T(8,128)(2,1)S(1)}, bf16[64,32,128]{2,1,0:T(8,128)(2,1)S(1)}, u32[]{:S(2)}, u32[]{:S(2)}) %collective-permute-start.5) | collective-permute-done | bytes 524320 | tf_op jit(solution)/shard_map/ppermute | solution.py:335
  48.4 3.4 %shard_map.71 = f32[64,64,127]{2,1,0:T(8,128)} custom-call(s32[1]{0:T(128)} %bitcast.where_ref, bf16[63,64,128]{2,1,0:T(8,128)(2,1)S(1)} %fusion.pick_ref, bf16[64,32,128]{2,1,0:T(8,128)(2,1)S(1)} %all_to_all.5.mine_ref, bf16[64,32,128]{2,1,0:T(8,128)(2,1)S(1)} %collective-permute-done.5.other_ref), custom_call_target="tpu_custom_call" | custom-call | tf_op jit(solution)/shard_map/pallas_call | solution.py:339
  (2 shorter events, 0.0 us)
Async XLA Ops:
  3.4 13.9 %collective-permute-start = (bf16[131,8,128]{2,1,0:T(8,128)(2,1)S(1)}, bf16[131,8,128]{2,1,0:T(8,128)(2,1)S(1)}, u32[]{:S(2)}, u32[]{:S(2)}) collective-permute-start(bf16[131,8,128]{2,1,0:T(8,128)(2,1)S(1)} %get-tuple-element.9.high_ref), channel_id=1, source_target_pairs={{0,8},{8,16},{16,24},{24,32},{32,40},{40,48},{48,56},{56,64},{64,7... | collective-permute-start | bytes 804872 | tf_op jit(solution)/shard_map/ppermute | solution.py:284
  5.9 11.3 %collective-permute-start.1 = (bf16[131,8,128]{2,1,0:T(8,128)(2,1)S(1)}, bf16[131,8,128]{2,1,0:T(8,128)(2,1)S(1)}, u32[]{:S(2)}, u32[]{:S(2)}) collective-permute-start(bf16[131,8,128]{2,1,0:T(8,128)(2,1)S(1)} %get-tuple-element.8.low_ref), channel_id=1, source_target_pairs={{0,120},{8,0},{16,8},{24,16},{32,24},{40,32},{48,40},{56,48},{64,5... | collective-permute-start | bytes 804872 | tf_op jit(solution)/shard_map/ppermute | solution.py:284
  10.3 6.9 %collective-permute-start.2 = (bf16[5,8,8,128]{3,2,1,0:T(8,128)(2,1)S(1)}, bf16[5,8,8,128]{3,2,1,0:T(8,128)(2,1)S(1)}, u32[]{:S(2)}, u32[]{:S(2)}) collective-permute-start(bf16[5,8,8,128]{3,2,1,0:T(8,128)(2,1)S(1)} %get-tuple-element.10.side_ref), channel_id=1, source_target_pairs={{0,1},{1,2},{2,3},{3,4},{4,5},{5,6},{6,7},{7,0},{8,9},{9,10},{10,1... | collective-permute-start | bytes 245768 | tf_op jit(solution)/shard_map/ppermute | solution.py:284
  12.5 4.8 %collective-permute-start.3 = (bf16[5,8,8,128]{3,2,1,0:T(8,128)(2,1)S(1)}, bf16[5,8,8,128]{3,2,1,0:T(8,128)(2,1)S(1)}, u32[]{:S(2)}, u32[]{:S(2)}) collective-permute-start(bf16[5,8,8,128]{3,2,1,0:T(8,128)(2,1)S(1)} %get-tuple-element.10.side_ref), channel_id=1, source_target_pairs={{0,7},{1,0},{2,1},{3,2},{4,3},{5,4},{6,5},{7,6},{8,15},{9,8},{10,9... | collective-permute-start | bytes 245768 | tf_op jit(solution)/shard_map/ppermute | solution.py:284
  17.3 29.6 %copy-start = (s32[127,128]{1,0:T(8,128)S(1)}, s32[127,128]{1,0:T(8,128)}, u32[]{:S(2)}) copy-start(s32[127,128]{1,0:T(8,128)} %order_hbm.1) | copy-start | bytes 195076
  21.8 2.7 %collective-permute-start.4 = (f32[32,128]{1,0:T(8,128)S(1)}, f32[32,128]{1,0:T(8,128)S(1)}, u32[]{:S(2)}, u32[]{:S(2)}) collective-permute-start(f32[32,128]{1,0:T(8,128)S(1)} %get-tuple-element.13), channel_id=1, source_target_pairs={{0,1},{1,0},{2,3},{3,2},{4,5},{5,4},{6,7},{7,6},{8,9},{9,8},{10,11... | collective-permute-start | bytes 49160 | tf_op jit(solution)/shard_map/ppermute | solution.py:328
  44.8 3.6 %collective-permute-start.5 = (bf16[64,32,128]{2,1,0:T(8,128)(2,1)S(1)}, bf16[64,32,128]{2,1,0:T(8,128)(2,1)S(1)}, u32[]{:S(2)}, u32[]{:S(2)}) collective-permute-start(bf16[64,32,128]{2,1,0:T(8,128)(2,1)S(1)} %all_to_all.5.mine_ref), channel_id=1, source_target_pairs={{0,1},{1,0},{2,3},{3,2},{4,5},{5,4},{6,7},{7,6},{8,9},{9,8},{10,11... | collective-permute-start | bytes 1572872 | tf_op jit(solution)/shard_map/ppermute | solution.py:335

commit v3 on v2

--- a/solution.py
+++ b/solution.py
@@ -7,8 +7,7 @@
 
 F32 = jnp.float32
 BF16 = jnp.bfloat16
-PARTS = 8
-PER = 64 // PARTS
+PITCH = 72
 CUBE = (8, 8, 128)
 FLAT = (64, 128)
 HBM = pl.BlockSpec(memory_space=pltpu.HBM)
@@ -50,72 +49,77 @@
     return high, middle, (rest - middle.astype(F32)).astype(BF16)
 
 
-def part_copy(states_hbm, states_ref, sem, part):
-    span = pl.ds(part * PER, PER)
-    return pltpu.make_async_copy(states_hbm.at[:, span], states_ref.at[:, span], sem.at[part])
-
-
-def edge_kernel(
-    table_hbm, class_hbm, states_hbm, low_ref, high_ref, side_ref,
-    states_ref, class_ref, table_ref, wide_ref, sem, small_sem,
+def edge_x_kernel(
+    table_hbm, class_hbm, states_hbm, low_ref, high_ref, states_ref, class_ref, table_ref, wide_ref, sem
 ):
-    get_table = pltpu.make_async_copy(table_hbm, table_ref, small_sem.at[0])
-    get_class = pltpu.make_async_copy(class_hbm, class_ref, small_sem.at[1])
-    get_table.start()
-    get_class.start()
-    for part in range(PARTS):
-        part_copy(states_hbm, states_ref, sem, part).start()
-    lane = lane_of(FLAT)
-    get_table.wait()
-    get_class.wait()
-    perm = look_up(class_ref[...], table_ref)
-    wide_ref[pl.ds(0, 64), :] = perm.reshape(FLAT)
+    copies = [
+        pltpu.make_async_copy(table_hbm, table_ref, sem.at[0]),
+        pltpu.make_async_copy(class_hbm, class_ref, sem.at[1]),
+    ]
+    for n, rows in enumerate((pl.ds(0, 2), pl.ds(6, 2))):
+        copies.append(
+            pltpu.make_async_copy(states_hbm.at[:, :, :, rows], states_ref.at[:, :, :, rows], sem.at[2 + n])
+        )
+    for copy in copies:
+        copy.start()
+    copies[0].wait()
+    copies[1].wait()
+    wide_ref[pl.ds(0, 64), :] = look_up(class_ref[...], table_ref).reshape(FLAT)
     for ref, at in ((low_ref, 0), (high_ref, 7)):
         for n, piece in enumerate(three_pieces(wide_ref[pl.ds(at, 8, stride=8), :])):
             ref[128 + n] = piece
+    copies[2].wait()
+    copies[3].wait()
+    for snap in range(64):
+        for field in range(2):
+            slot = (1 + field + 2 * snap) * 64
+            wide_ref[pl.ds(slot, 64), :] = states_ref[field, snap].astype(F32).reshape(FLAT)
+            low_ref[field * 64 + snap] = wide_ref[pl.ds(slot, 8, stride=8), :].astype(BF16)
+            high_ref[field * 64 + snap] = wide_ref[pl.ds(slot + 7, 8, stride=8), :].astype(BF16)
+
+
+def edge_y_kernel(table_hbm, class_hbm, states_hbm, side_ref, perm_ref, states_ref, class_ref, table_ref, sem):
+    copies = [
+        pltpu.make_async_copy(table_hbm, table_ref, sem.at[0]),
+        pltpu.make_async_copy(class_hbm, class_ref, sem.at[1]),
+    ]
+    for n in range(2):
+        half = pl.ds(32 * n, 32)
+        copies.append(pltpu.make_async_copy(states_hbm.at[:, half], states_ref.at[:, half], sem.at[2 + n]))
+    for copy in copies:
+        copy.start()
+    copies[0].wait()
+    copies[1].wait()
+    perm = look_up(class_ref[...], table_ref)
+    perm_ref[...] = perm
     first = jnp.broadcast_to(perm[:, :, 0:1], CUBE)
     last = jnp.broadcast_to(perm[:, :, 127:128], CUBE)
     for n, piece in enumerate(three_pieces(jnp.where(lane_of(CUBE) % 2 == 0, first, last))):
         side_ref[2 + n] = piece
+    lane = lane_of(FLAT)
     acc = [jnp.zeros(FLAT, F32), jnp.zeros(FLAT, F32)]
-    for part in range(PARTS):
-        part_copy(states_hbm, states_ref, sem, part).wait()
-        for k in range(PER):
-            snap = part * PER + k
-            for field in range(2):
-                value = states_ref[field, snap].astype(F32).reshape(FLAT)
-                slot = (1 + field + 2 * snap) * 64
-                wide_ref[pl.ds(slot, 64), :] = value
-                keep = (lane == 2 * snap) | (lane == (2 * snap + 127) % 128)
-                acc[field] = jnp.where(keep, turn(value, 2 * snap), acc[field])
-                low_ref[field * 64 + snap] = wide_ref[pl.ds(slot, 8, stride=8), :].astype(BF16)
-                high_ref[field * 64 + snap] = wide_ref[pl.ds(slot + 7, 8, stride=8), :].astype(BF16)
+    for snap in range(64):
+        if snap % 32 == 0:
+            copies[2 + snap // 32].wait()
+        keep = (lane == 2 * snap) | (lane == (2 * snap + 127) % 128)
+        for field in range(2):
+            value = states_ref[field, snap].astype(F32).reshape(FLAT)
+            acc[field] = jnp.where(keep, turn(value, 2 * snap), acc[field])
     for field in range(2):
         side_ref[field] = acc[field].reshape(CUBE).astype(BF16)
 
 
-def inner_kernel(
-    table_hbm, class_hbm, states_hbm, out_ref,
-    states_ref, class_ref, table_ref, tx_ref, ty_ref, tz_ref, sem, small_sem,
-):
-    get_table = pltpu.make_async_copy(table_hbm, table_ref, small_sem.at[0])
-    get_class = pltpu.make_async_copy(class_hbm, class_ref, small_sem.at[1])
-    get_table.start()
-    get_class.start()
-    for part in range(PARTS):
-        part_copy(states_hbm, states_ref, sem, part).start()
-    get_table.wait()
-    get_class.wait()
-    perm = look_up(class_ref[...], table_ref)
+def inner_kernel(perm_ref, states_ref, out_ref, tx_ref, ty_ref, tz_ref):
+    perm = perm_ref[...]
     row = lax.broadcasted_iota(jnp.int32, CUBE, 1)
     next_y = turn(perm.reshape(FLAT), 127).reshape(CUBE)
     tx_ref[...] = jnp.where(row == 7, 0.0, trans(perm, jnp.roll(perm, -1, 1)))
     ty_ref[...] = jnp.where(lane_of(CUBE) == 127, 0.0, trans(perm, next_y))
     tz_ref[...] = trans(perm[:-1], perm[1:])
-    for part in range(PARTS):
-        part_copy(states_hbm, states_ref, sem, part).wait()
-        for k in range(PER):
-            snap = part * PER + k
+
+    def group(number, carry):
+        for k in range(16):
+            snap = number * 16 + k
             p = states_ref[0, snap].astype(F32)
             s = states_ref[1, snap].astype(F32)
             m = s * s
@@ -127,7 +131,10 @@
             fz = face(tz_ref[...], m[:-1], m[1:], p[:-1], p[1:])
             zero = jnp.zeros((1, 8, 128), F32)
             total = total + (jnp.concatenate([fz, zero], 0) - jnp.concatenate([zero, fz], 0))
-            out_ref[pl.ds(snap * 64, 64), :] = total.reshape(FLAT)
+            out_ref[pl.ds(pl.multiple_of(snap * 64, 64), 64), :] = total.reshape(FLAT)
+        return carry
+
+    lax.fori_loop(0, 4, group, 0)
 
 
 def outer_kernel(
@@ -174,21 +181,27 @@
         return face(txe_ref[which], s_here * s_here, s_next * s_next, p_here, p_next)
 
     def put(part):
-        span = pl.ds(part * PER, PER)
+        span = pl.ds(part * 32, 32)
         return pltpu.make_async_copy(out_ref.at[span], out_hbm.at[span], sem.at[part])
 
-    for part in range(PARTS):
-        for k in range(PER):
-            snap = part * PER + k
-            start = snap * 64
+    def group(number, carry):
+        for k in range(16):
+            snap = number * 16 + k
+            start = pl.multiple_of(snap * PITCH, 8)
             turned = turn(qy_ref[...], (128 - 2 * snap) % 128)
-            flux_ref[pl.ds(start, 64), :] = inner_ref[pl.ds(start, 64), :] + jnp.where(at_edge, turned, 0.0)
+            within = inner_ref[pl.ds(pl.multiple_of(snap * 64, 64), 64), :]
+            flux_ref[pl.ds(start, 64), :] = within + jnp.where(at_edge, turned, 0.0)
             low, high = pl.ds(start, 8, stride=8), pl.ds(start + 7, 8, stride=8)
             flux_ref[low, :] = flux_ref[low, :] + edge(low_ref, from_low_ref, 0, snap)
             flux_ref[high, :] = flux_ref[high, :] + edge(high_ref, from_high_ref, 1, snap)
-        for k in range(PER):
-            snap = part * PER + k
-            out_ref[snap] = flux_ref[pl.ds(snap * 64, 64), :].reshape(CUBE).astype(BF16)
+        for k in range(16):
+            snap = number * 16 + k
+            start = pl.multiple_of(snap * PITCH, 8)
+            out_ref[snap] = flux_ref[pl.ds(start, 64), :].reshape(CUBE).astype(BF16)
+        return carry
+
+    for part in range(2):
+        lax.fori_loop(2 * part, 2 * part + 2, group, 0)
         put(part).start()
 
     get_cand.wait()
@@ -198,7 +211,7 @@
         source = order_ref[0, i]
         cell = cand_ref[0, source % 64]
         slot = (i + 32 * core) % 64
-        values = flux_ref[pl.ds(cell // 128, 64, stride=64), :]
+        values = flux_ref[pl.ds(cell // 128, 64, stride=PITCH), :]
         turned = turn(values, (slot - cell % 128 + 128) % 128)
         return jnp.where(lane == jnp.where(source // 64 == core, slot, -1), turned, acc)
 
@@ -206,7 +219,7 @@
     rows = jnp.transpose(jnp.concatenate([acc, jnp.zeros(FLAT, F32)], 0))
     mine_ref[...] = rows[:32]
     send_ref[...] = rows[32:64]
-    for part in range(PARTS):
+    for part in range(2):
         put(part).wait()
 
 
@@ -261,21 +274,16 @@
         pltpu.with_memory_space_constraint(value, pltpu.HBM)
         for value in (states, class_map, perm_table, candidates.reshape(128, 64), merge_order)
     )
-    edge_shape, side_shape = (131, 8, 128), (5, 8, 8, 128)
-    states_scratch = [
-        pltpu.VMEM((2, 64, 8, 8, 128), BF16), pltpu.VMEM(CUBE, jnp.int32), pltpu.SMEM((8,), F32)
-    ]
-    sems = [pltpu.SemaphoreType.DMA((PARTS,)), pltpu.SemaphoreType.DMA((2,))]
-    low, high, side = pl.pallas_call(
-        edge_kernel,
+    edge_shape, side_shape, states_shape = (131, 8, 128), (5, 8, 8, 128), (2, 64, 8, 8, 128)
+    read_scratch = [pltpu.VMEM(CUBE, jnp.int32), pltpu.SMEM((8,), F32)]
+    low, high = pl.pallas_call(
+        edge_x_kernel,
         in_specs=[HBM, HBM, HBM],
-        out_specs=[whole(edge_shape), whole(edge_shape), whole(side_shape)],
-        out_shape=[
-            jax.ShapeDtypeStruct(edge_shape, BF16),
-            jax.ShapeDtypeStruct(edge_shape, BF16),
-            jax.ShapeDtypeStruct(side_shape, BF16),
-        ],
-        scratch_shapes=states_scratch + [pltpu.VMEM((129 * 64, 128), F32)] + sems,
+        out_specs=[whole(edge_shape), whole(edge_shape)],
+        out_shape=[jax.ShapeDtypeStruct(edge_shape, BF16), jax.ShapeDtypeStruct(edge_shape, BF16)],
+        scratch_shapes=[pltpu.VMEM(states_shape, BF16)]
+        + read_scratch
+        + [pltpu.VMEM((129 * 64, 128), F32), pltpu.SemaphoreType.DMA((4,))],
         compiler_params=LIMIT,
     )(perm_table, class_map, states)
 
@@ -285,19 +293,30 @@
 
     from_low = shift(high, "gx", 1)
     from_high = shift(low, "gx", -1)
+
+    side, perm, near_states = pl.pallas_call(
+        edge_y_kernel,
+        in_specs=[HBM, HBM, HBM],
+        out_specs=[whole(side_shape), whole(CUBE), whole(states_shape)],
+        out_shape=[
+            jax.ShapeDtypeStruct(side_shape, BF16),
+            jax.ShapeDtypeStruct(CUBE, F32),
+            jax.ShapeDtypeStruct(states_shape, BF16),
+        ],
+        scratch_shapes=read_scratch + [pltpu.SemaphoreType.DMA((4,))],
+        compiler_params=LIMIT,
+    )(perm_table, class_map, states)
     side_low = shift(side, "gy", 1)
     side_high = shift(side, "gy", -1)
 
     inner = pl.pallas_call(
         inner_kernel,
-        in_specs=[HBM, HBM, HBM],
+        in_specs=[whole(CUBE), whole(states_shape)],
         out_specs=whole((4096, 128)),
         out_shape=jax.ShapeDtypeStruct((4096, 128), F32),
-        scratch_shapes=states_scratch
-        + [pltpu.VMEM(CUBE, F32), pltpu.VMEM(CUBE, F32), pltpu.VMEM((7, 8, 128), F32)]
-        + sems,
-        compiler_params=LIMIT,
-    )(perm_table, class_map, states)
+        scratch_shapes=[pltpu.VMEM(CUBE, F32), pltpu.VMEM(CUBE, F32), pltpu.VMEM((7, 8, 128), F32)],
+        compiler_params=LIMIT,
+    )(perm, near_states)
 
     flux, mine_rows, send_rows = pl.pallas_call(
         outer_kernel,
@@ -310,14 +329,15 @@
             jax.ShapeDtypeStruct((32, 128), F32),
         ],
         scratch_shapes=[
-            pltpu.VMEM((4096, 128), F32),
+            pltpu.VMEM((64 * PITCH, 128), F32),
             pltpu.VMEM((64, 8, 8, 128), BF16),
             pltpu.VMEM((2, 8, 128), F32),
             pltpu.VMEM(FLAT, F32),
             pltpu.SMEM((1, 64), jnp.int32),
             pltpu.SMEM((1, 128), jnp.int32),
-        ]
-        + sems,
+            pltpu.SemaphoreType.DMA((2,)),
+            pltpu.SemaphoreType.DMA((2,)),
+        ],
         compiler_params=LIMIT,
     )(
         where, candidates, merge_rows, inner, low, high, side,

time: 52 us -> 49.2 us (0.946)
  blocking collectives: 20.2 us -> 18.5 us
  Pallas kernels: 15.4 us -> 14.3 us
    all_to_all x1, blocking collectives: 20.2 us -> 18.5 us  [local(): mine = lax.all_to_all(spread, ('gx', 'gy'), 0, 0, axis_index_groups=peers)]
    pallas_call x1, Pallas kernels: 4.46 us -> 2.8 us  [local(): pl.pallas_call(outer_kernel, in_specs=[SMEM, HBM, HBM, whole((4096, 128))...]
    pallas_call x2 -> x3, Pallas kernels: 7.52 us -> 8.13 us  [the longest x1 4.5 us: local(): pl.pallas_call(inner_kernel, in_specs=[whole(CUBE), whole(states_shape)],...]
  transfers between devices with their start and end apart: 6 -> 6, of which waited for: 2 -> 2; matrix products, arithmetic and copies ran while one was open for 2% -> 2% of each run, Pallas kernels for 9% -> 13%
where the time goes in v3:
time: 49.2 us; the launch traced here: 49 us
  blocking collectives  18.5 us (38%)
  Pallas kernels  14.3 us (29%)
  starting transfers between devices  13 us (26%)
  waiting for transfers between devices  1.54 us (3%)
  other arithmetic  0.92 us (2%)
  between operations  0.72 us (1%)
    all_to_all x1, blocking collectives, local(): mine = lax.all_to_all(spread, ('gx', 'gy'), 0, 0, axis_index_groups=peers)  18.5 us
    ppermute x4, starting transfers between devices, shift(): lax.ppermute(value, axis, [(i, (i + by) % count) for i in range(count)])  9.08 us
    pallas_call x1, Pallas kernels, local(): pl.pallas_call(inner_kernel, in_specs=[whole(CUBE), whole(states_shape)],...  4.5 us
    pallas_call x1, Pallas kernels, local(): pl.pallas_call(tree_kernel, in_specs=[SMEM, whole((63, 64, 128)), whole((...  3.4 us
    pallas_call x1, Pallas kernels, local(): pl.pallas_call(outer_kernel, in_specs=[SMEM, HBM, HBM, whole((4096, 128))...  2.8 us
    ppermute x1, starting transfers between devices, local(): other = lax.ppermute(mine, 'gy', swap)  2.04 us
    pallas_call x1, Pallas kernels, local(): pl.pallas_call(edge_y_kernel, in_specs=[HBM, HBM, HBM], out_specs=[whole(...  1.95 us
    ppermute x1, starting transfers between devices, local(): got_rows = lax.ppermute(send_rows, 'gy', swap)  1.85 us
  transfers between devices with their start and end apart: 6, of which 2 were waited for; matrix products, arithmetic and copies ran while one was open for 2% of the time, Pallas kernels for 13%

profile of v3, /device:TPU:1, one launch (start us, length us, event | category | flops | bytes accessed | tf_op | source)
XLA Modules:
  0.0 49.0 jit_solution(14691413439390802167)
XLA Ops:
  0.6 1.7 %shard_map.70 = (bf16[131,8,128]{2,1,0:T(8,128)(2,1)S(1)}, bf16[131,8,128]{2,1,0:T(8,128)(2,1)S(1)}) custom-call(f32[8]{0:T(128)} %table_hbm.3, s32[8,8,128]{2,1,0:T(8,128)} %class_hbm.3, bf16[2,64,8,8,128]{4,3,2,1,0:T(8,128)(2,1)} %states_hbm.3), custom_call_target="tpu_custom_call" | custom-call | tf_op jit(solution)/shard_map/pallas_call | solution.py:279
  2.3 2.5 %collective-permute-start = (bf16[131,8,128]{2,1,0:T(8,128)(2,1)S(1)}, bf16[131,8,128]{2,1,0:T(8,128)(2,1)S(1)}, u32[]{:S(2)}, u32[]{:S(2)}) collective-permute-start(bf16[131,8,128]{2,1,0:T(8,128)(2,1)S(1)} %get-tuple-element.13.high_ref), channel_id=1, source_target_pairs={{0,8},{8,16},{16,24},{24,32},{32,40},{40,48},{48,56},{56,64},{64,7... | collective-permute-start | bytes 804872 | tf_op jit(solution)/shard_map/ppermute | solution.py:292
  4.8 4.4 %collective-permute-start.1 = (bf16[131,8,128]{2,1,0:T(8,128)(2,1)S(1)}, bf16[131,8,128]{2,1,0:T(8,128)(2,1)S(1)}, u32[]{:S(2)}, u32[]{:S(2)}) collective-permute-start(bf16[131,8,128]{2,1,0:T(8,128)(2,1)S(1)} %get-tuple-element.12.low_ref), channel_id=1, source_target_pairs={{0,120},{8,0},{16,8},{24,16},{32,24},{40,32},{48,40},{56,48},{64,5... | collective-permute-start | bytes 804872 | tf_op jit(solution)/shard_map/ppermute | solution.py:292
  9.2 2.0 %shard_map.68 = (bf16[5,8,8,128]{3,2,1,0:T(8,128)(2,1)S(1)}, f32[8,8,128]{2,1,0:T(8,128)S(1)}, bf16[2,64,8,8,128]{4,3,2,1,0:T(8,128)(2,1)S(1)}) custom-call(f32[8]{0:T(128)} %table_hbm.3, s32[8,8,128]{2,1,0:T(8,128)} %class_hbm.3, bf16[2,64,8,8,128]{4,3,2,1,0:T(8,128)(2,1)} %states_hbm.3), custom_call_target="tpu_custom_call" | custom-call | tf_op jit(solution)/shard_map/pallas_call | solution.py:297
  11.2 2.1 %collective-permute-start.2 = (bf16[5,8,8,128]{3,2,1,0:T(8,128)(2,1)S(1)}, bf16[5,8,8,128]{3,2,1,0:T(8,128)(2,1)S(1)}, u32[]{:S(2)}, u32[]{:S(2)}) collective-permute-start(bf16[5,8,8,128]{3,2,1,0:T(8,128)(2,1)S(1)} %get-tuple-element.14.side_ref), channel_id=1, source_target_pairs={{0,1},{1,2},{2,3},{3,4},{4,5},{5,6},{6,7},{7,0},{8,9},{9,10},{10,1... | collective-permute-start | bytes 245768 | tf_op jit(solution)/shard_map/ppermute | solution.py:292
  13.4 0.0 collective-permute-start.3
  13.4 4.5 %shard_map.69.inner_ref = f32[4096,128]{1,0:T(8,128)S(1)} custom-call(f32[8,8,128]{2,1,0:T(8,128)S(1)} %get-tuple-element.10.perm_ref, bf16[2,64,8,8,128]{4,3,2,1,0:T(8,128)(2,1)S(1)} %get-tuple-element.11.states_ref), custom_call_target="tpu_custom_call" | custom-call | tf_op jit(solution)/shard_map/pallas_call | solution.py:312
  17.9 0.0 collective-permute-done.2.side_low_ref
  17.9 0.0 collective-permute-done.3.side_high_ref
  17.9 0.0 collective-permute-done.from_low_ref
  17.9 0.0 collective-permute-done.1.from_high_ref
  17.9 0.0 copy-start
  17.9 2.8 %shard_map.71 = (bf16[64,8,8,128]{3,2,1,0:T(8,128)(2,1)}, f32[32,128]{1,0:T(8,128)S(1)}, f32[32,128]{1,0:T(8,128)S(1)}) custom-call(s32[1]{0:T(128)} %bitcast.where_ref, s32[128,64]{1,0:T(8,128)} %bitcast.4, s32[127,128]{1,0:T(8,128)} %order_hbm.1, f32[4096,128]{1,0:T(8,128)S(1)} %shard_map.69.inner_ref, bf16[131,8,128]{2,1,0:T(8,128)(2,1)S(1)} %get-tuple-element.12.low_ref, ...), custom_call_target="tpu_custom_call" | custom-call | tf_op jit(solution)/shard_map/pallas_call | solution.py:321
  20.7 1.9 %collective-permute-start.4 = (f32[32,128]{1,0:T(8,128)S(1)}, f32[32,128]{1,0:T(8,128)S(1)}, u32[]{:S(2)}, u32[]{:S(2)}) collective-permute-start(f32[32,128]{1,0:T(8,128)S(1)} %get-tuple-element.17), channel_id=1, source_target_pairs={{0,1},{1,0},{2,3},{3,2},{4,5},{5,4},{6,7},{7,6},{8,9},{9,8},{10,11... | collective-permute-start | bytes 49160 | tf_op jit(solution)/shard_map/ppermute | solution.py:348
  22.6 0.8 %collective-permute-done.4 = f32[32,128]{1,0:T(8,128)S(1)} collective-permute-done((f32[32,128]{1,0:T(8,128)S(1)}, f32[32,128]{1,0:T(8,128)S(1)}, u32[]{:S(2)}, u32[]{:S(2)}) %collective-permute-start.4) | collective-permute-done | bytes 16416 | tf_op jit(solution)/shard_map/ppermute | solution.py:348
  23.4 0.1 pad_maximum_fusion
  23.5 0.1 broadcast_in_dim.2
  23.6 18.5 %all_to_all.5.mine_ref = bf16[64,32,128]{2,1,0:T(8,128)(2,1)S(1)} all-to-all(bf16[64,32,128]{2,1,0:T(8,128)(2,1)S(1)} %broadcast_in_dim.2), channel_id=1, replica_groups={{0,2,4,6,8,10,12,14,16,18,20,22,24,26,28,30,32,34,36,38,40,42,44,46,48,..., dimensions={0} | all-to-all | bytes 1048576 | tf_op jit(solution)/shard_map/all_to_all | solution.py:354
  42.0 2.0 %collective-permute-start.5 = (bf16[64,32,128]{2,1,0:T(8,128)(2,1)S(1)}, bf16[64,32,128]{2,1,0:T(8,128)(2,1)S(1)}, u32[]{:S(2)}, u32[]{:S(2)}) collective-permute-start(bf16[64,32,128]{2,1,0:T(8,128)(2,1)S(1)} %all_to_all.5.mine_ref), channel_id=1, source_target_pairs={{0,1},{1,0},{2,3},{3,2},{4,5},{5,4},{6,7},{7,6},{8,9},{9,8},{10,11... | collective-permute-start | bytes 1572872 | tf_op jit(solution)/shard_map/ppermute | solution.py:355
  44.1 0.0 copy-done
  44.1 0.8 %fusion.pick_ref = bf16[63,64,128]{2,1,0:T(8,128)(2,1)S(1)} fusion(s32[63,64]{1,0:T(8,128)S(1)} %slice.9), kind=kLoop, calls=%fused_computation.1 | loop fusion | flops 1032192 | bytes 1048320 | tf_op jit(solution)/shard_map/convert_element_type | solution.py:358
  44.9 0.7 %collective-permute-done.5.other_ref = bf16[64,32,128]{2,1,0:T(8,128)(2,1)S(1)} collective-permute-done((bf16[64,32,128]{2,1,0:T(8,128)(2,1)S(1)}, bf16[64,32,128]{2,1,0:T(8,128)(2,1)S(1)}, u32[]{:S(2)}, u32[]{:S(2)}) %collective-permute-start.5) | collective-permute-done | bytes 524320 | tf_op jit(solution)/shard_map/ppermute | solution.py:355
  45.6 3.4 %shard_map.72 = f32[64,64,127]{2,1,0:T(8,128)} custom-call(s32[1]{0:T(128)} %bitcast.where_ref, bf16[63,64,128]{2,1,0:T(8,128)(2,1)S(1)} %fusion.pick_ref, bf16[64,32,128]{2,1,0:T(8,128)(2,1)S(1)} %all_to_all.5.mine_ref, bf16[64,32,128]{2,1,0:T(8,128)(2,1)S(1)} %collective-permute-done.5.other_ref), custom_call_target="tpu_custom_call" | custom-call | tf_op jit(solution)/shard_map/pallas_call | solution.py:359
  (2 shorter events, 0.0 us)
Async XLA Ops:
  2.3 15.6 %collective-permute-start = (bf16[131,8,128]{2,1,0:T(8,128)(2,1)S(1)}, bf16[131,8,128]{2,1,0:T(8,128)(2,1)S(1)}, u32[]{:S(2)}, u32[]{:S(2)}) collective-permute-start(bf16[131,8,128]{2,1,0:T(8,128)(2,1)S(1)} %get-tuple-element.13.high_ref), channel_id=1, source_target_pairs={{0,8},{8,16},{16,24},{24,32},{32,40},{40,48},{48,56},{56,64},{64,7... | collective-permute-start | bytes 804872 | tf_op jit(solution)/shard_map/ppermute | solution.py:292
  4.8 13.1 %collective-permute-start.1 = (bf16[131,8,128]{2,1,0:T(8,128)(2,1)S(1)}, bf16[131,8,128]{2,1,0:T(8,128)(2,1)S(1)}, u32[]{:S(2)}, u32[]{:S(2)}) collective-permute-start(bf16[131,8,128]{2,1,0:T(8,128)(2,1)S(1)} %get-tuple-element.12.low_ref), channel_id=1, source_target_pairs={{0,120},{8,0},{16,8},{24,16},{32,24},{40,32},{48,40},{56,48},{64,5... | collective-permute-start | bytes 804872 | tf_op jit(solution)/shard_map/ppermute | solution.py:292
  11.2 6.7 %collective-permute-start.2 = (bf16[5,8,8,128]{3,2,1,0:T(8,128)(2,1)S(1)}, bf16[5,8,8,128]{3,2,1,0:T(8,128)(2,1)S(1)}, u32[]{:S(2)}, u32[]{:S(2)}) collective-permute-start(bf16[5,8,8,128]{3,2,1,0:T(8,128)(2,1)S(1)} %get-tuple-element.14.side_ref), channel_id=1, source_target_pairs={{0,1},{1,2},{2,3},{3,4},{4,5},{5,6},{6,7},{7,0},{8,9},{9,10},{10,1... | collective-permute-start | bytes 245768 | tf_op jit(solution)/shard_map/ppermute | solution.py:292
  13.4 4.5 %collective-permute-start.3 = (bf16[5,8,8,128]{3,2,1,0:T(8,128)(2,1)S(1)}, bf16[5,8,8,128]{3,2,1,0:T(8,128)(2,1)S(1)}, u32[]{:S(2)}, u32[]{:S(2)}) collective-permute-start(bf16[5,8,8,128]{3,2,1,0:T(8,128)(2,1)S(1)} %get-tuple-element.14.side_ref), channel_id=1, source_target_pairs={{0,7},{1,0},{2,1},{3,2},{4,3},{5,4},{6,5},{7,6},{8,15},{9,8},{10,9... | collective-permute-start | bytes 245768 | tf_op jit(solution)/shard_map/ppermute | solution.py:292
  17.9 26.2 %copy-start = (s32[127,128]{1,0:T(8,128)S(1)}, s32[127,128]{1,0:T(8,128)}, u32[]{:S(2)}) copy-start(s32[127,128]{1,0:T(8,128)} %order_hbm.1) | copy-start | bytes 195076
  20.7 2.7 %collective-permute-start.4 = (f32[32,128]{1,0:T(8,128)S(1)}, f32[32,128]{1,0:T(8,128)S(1)}, u32[]{:S(2)}, u32[]{:S(2)}) collective-permute-start(f32[32,128]{1,0:T(8,128)S(1)} %get-tuple-element.17), channel_id=1, source_target_pairs={{0,1},{1,0},{2,3},{3,2},{4,5},{5,4},{6,7},{7,6},{8,9},{9,8},{10,11... | collective-permute-start | bytes 49160 | tf_op jit(solution)/shard_map/ppermute | solution.py:348
  42.0 3.6 %collective-permute-start.5 = (bf16[64,32,128]{2,1,0:T(8,128)(2,1)S(1)}, bf16[64,32,128]{2,1,0:T(8,128)(2,1)S(1)}, u32[]{:S(2)}, u32[]{:S(2)}) collective-permute-start(bf16[64,32,128]{2,1,0:T(8,128)(2,1)S(1)} %all_to_all.5.mine_ref), channel_id=1, source_target_pairs={{0,1},{1,0},{2,3},{3,2},{4,5},{5,4},{6,7},{7,6},{8,9},{9,8},{10,11... | collective-permute-start | bytes 1572872 | tf_op jit(solution)/shard_map/ppermute | solution.py:355

commit v4 on v3

v4 whole, which is shorter than its diff:
```python
import jax
import jax.numpy as jnp
from jax import lax
from jax.experimental import pallas as pl
from jax.experimental.pallas import tpu as pltpu
from jax.sharding import PartitionSpec as P

F32 = jnp.float32
BF16 = jnp.bfloat16
KEPT = 40
CUBE = (8, 8, 128)
FLAT = (64, 128)
HBM = pl.BlockSpec(memory_space=pltpu.HBM)
SMEM = pl.BlockSpec(memory_space=pltpu.SMEM)
LIMIT = pltpu.CompilerParams(vmem_limit_bytes=48 * 1024 * 1024)


def whole(shape):
    return pl.BlockSpec(shape, lambda *_: (0,) * len(shape))


def lane_of(shape):
    return lax.broadcasted_iota(jnp.int32, shape, len(shape) - 1)


def turn(value, by):
    return pltpu.roll(value, by, 1)


def look_up(kind, table_ref):
    value = jnp.zeros(kind.shape, F32)
    for number in range(8):
        value = jnp.where(kind == number, table_ref[number], value)
    return value


def trans(k_here, k_next):
    return k_here * k_next / (k_here + k_next)


def face(t, m_here, m_next, p_here, p_next):
    return t * (m_here + m_next) * (p_next - p_here)


def three_pieces(value):
    high = value.astype(BF16)
    rest = value - high.astype(F32)
    middle = rest.astype(BF16)
    return high, middle, (rest - middle.astype(F32)).astype(BF16)


def edge_x_kernel(
    table_hbm, class_hbm, states_hbm, low_ref, high_ref, states_ref, class_ref, table_ref, wide_ref, sem
):
    copies = [
        pltpu.make_async_copy(table_hbm, table_ref, sem.at[0]),
        pltpu.make_async_copy(class_hbm, class_ref, sem.at[1]),
    ]
    for n, rows in enumerate((pl.ds(0, 2), pl.ds(6, 2))):
        copies.append(
            pltpu.make_async_copy(states_hbm.at[:, :, :, rows], states_ref.at[:, :, :, rows], sem.at[2 + n])
        )
    for copy in copies:
        copy.start()
    copies[0].wait()
    copies[1].wait()
    wide_ref[pl.ds(0, 64), :] = look_up(class_ref[...], table_ref).reshape(FLAT)
    for ref, at in ((low_ref, 0), (high_ref, 7)):
        for n, piece in enumerate(three_pieces(wide_ref[pl.ds(at, 8, stride=8), :])):
            ref[128 + n] = piece
    copies[2].wait()
    copies[3].wait()
    for snap in range(64):
        for field in range(2):
            slot = (1 + field + 2 * snap) * 64
            wide_ref[pl.ds(slot, 64), :] = states_ref[field, snap].astype(F32).reshape(FLAT)
            low_ref[field * 64 + snap] = wide_ref[pl.ds(slot, 8, stride=8), :].astype(BF16)
            high_ref[field * 64 + snap] = wide_ref[pl.ds(slot + 7, 8, stride=8), :].astype(BF16)


def two_times(weights):
    return jnp.concatenate([weights, weights], 0)


def two_pieces(value):
    high = value.astype(BF16)
    return jnp.concatenate([high, (value - high.astype(F32)).astype(BF16)], 1)


def matmul(left, right):
    return jnp.dot(left, right, preferred_element_type=F32)


def sub_of(shape):
    return lax.broadcasted_iota(jnp.int32, shape, 0)


def edge_y_kernel(
    where_ref, table_hbm, class_hbm, cand_hbm, order_hbm, states_hbm,
    side_ref, perm_ref, states_ref, cells_ref, hits_ref, class_ref, cand_ref, order_ref, table_ref, sem,
):
    tile = where_ref[0]
    core = tile % 2
    copies = [
        pltpu.make_async_copy(table_hbm, table_ref, sem.at[0]),
        pltpu.make_async_copy(class_hbm, class_ref, sem.at[1]),
        pltpu.make_async_copy(cand_hbm.at[pl.ds(tile, 1)], cand_ref, sem.at[2]),
        pltpu.make_async_copy(order_hbm.at[pl.ds(tile // 2, 1)], order_ref, sem.at[3]),
    ]
    for n in range(2):
        half = pl.ds(32 * n, 32)
        copies.append(pltpu.make_async_copy(states_hbm.at[:, half], states_ref.at[:, half], sem.at[4 + n]))
    for copy in copies:
        copy.start()
    for copy in copies[:4]:
        copy.wait()
    lane = lane_of(FLAT)
    order = jnp.broadcast_to(order_ref[...], FLAT)
    swapped = jnp.where(lane < 32, turn(order, 96), turn(order, 32))
    order = jnp.where(core == 1, swapped, order)
    match = (order == core * 64 + sub_of(FLAT)) & (lane < 64)
    column = jnp.transpose(jnp.broadcast_to(cand_ref[...].astype(F32), (64, 64)))[:, :1]
    cell = jnp.sum(jnp.where(match, jnp.broadcast_to(column, FLAT) + 1.0, 0.0), 0, keepdims=True)
    cell = cell.astype(jnp.int32) - 1
    at_y = jnp.where(cell < 0, -1, cell % 128)
    at_zx = jnp.where(cell < 0, -1, cell // 128)
    cells_ref[...] = two_times(jnp.where(sub_of((128, 128)) == at_y, 1.0, 0.0).astype(BF16))
    hits_ref[...] = jnp.where(sub_of(FLAT) == at_zx, 1.0, 0.0).reshape(CUBE)

    perm = look_up(class_ref[...], table_ref)
    perm_ref[...] = perm
    first = jnp.broadcast_to(perm[:, :, 0:1], CUBE)
    last = jnp.broadcast_to(perm[:, :, 127:128], CUBE)
    for n, piece in enumerate(three_pieces(jnp.where(lane_of(CUBE) % 2 == 0, first, last))):
        side_ref[2 + n] = piece
    square = (128, 128)
    spread = jnp.where(sub_of(square) == jnp.where(lane_of(square) % 2 == 0, 0, 127), 1.0, 0.0).astype(BF16)
    acc = [jnp.zeros(FLAT, F32), jnp.zeros(FLAT, F32)]
    for snap in range(64):
        if snap % 32 == 0:
            copies[4 + snap // 32].wait()
        keep = (lane == 2 * snap) | (lane == (2 * snap + 127) % 128)
        for field in range(2):
            value = matmul(states_ref[field, snap].reshape(FLAT), spread)
            acc[field] = jnp.where(keep, value, acc[field])
    for field in range(2):
        side_ref[field] = acc[field].reshape(CUBE).astype(BF16)


def inner_kernel(perm_ref, states_ref, out_ref, tx_ref, ty_ref, tz_ref, shift_ref, differ_ref):
    perm = perm_ref[...]
    row = lax.broadcasted_iota(jnp.int32, CUBE, 1)
    next_y = turn(perm.reshape(FLAT), 127).reshape(CUBE)
    tx_ref[...] = jnp.where(row == 7, 0.0, trans(perm, jnp.roll(perm, -1, 1)))
    ty_ref[...] = jnp.where(lane_of(CUBE) == 127, 0.0, trans(perm, next_y)).reshape(FLAT)
    tz_ref[...] = trans(perm[:-1], perm[1:])
    square = (128, 128)
    ahead = sub_of(square) - lane_of(square)
    shift_ref[...] = jnp.where(ahead == 1, 1.0, 0.0).astype(BF16)
    differ_ref[...] = two_times((jnp.where(ahead == 0, 1.0, 0.0) - jnp.where(ahead == -1, 1.0, 0.0)).astype(BF16))

    def group(number, carry):
        for k in range(8):
            snap = number * 8 + k
            p = states_ref[0, snap].astype(F32)
            s = states_ref[1, snap].astype(F32)
            m = s * s
            fx = face(tx_ref[...], m, jnp.roll(m, -1, 1), p, jnp.roll(p, -1, 1))
            total = fx - jnp.roll(fx, 1, 1)
            p_next = matmul(states_ref[0, snap].reshape(FLAT), shift_ref[...])
            s_next = matmul(states_ref[1, snap].reshape(FLAT), shift_ref[...])
            fy = face(ty_ref[...], m.reshape(FLAT), s_next * s_next, p.reshape(FLAT), p_next)
            total = total + matmul(two_pieces(fy), differ_ref[...]).reshape(CUBE)
            fz = face(tz_ref[...], m[:-1], m[1:], p[:-1], p[1:])
            zero = jnp.zeros((1, 8, 128), F32)
            total = total + (jnp.concatenate([fz, zero], 0) - jnp.concatenate([zero, fz], 0))
            out_ref[pl.ds(pl.multiple_of(snap * 64, 64), 64), :] = total.reshape(FLAT)
        return carry

    lax.fori_loop(0, 8, group, 0)


def outer_kernel(
    inner_ref, cells_ref, hits_ref, low_ref, high_ref, side_ref,
    from_low_ref, from_high_ref, side_low_ref, side_high_ref,
    out_hbm, mine_ref, send_ref,
    flux_ref, out_ref, txe_ref, qy_ref, ends_ref, picked_ref, sem,
):
    lane = lane_of(FLAT)

    def perm_of(ref, at):
        high, middle, low = (ref[at + n].astype(F32) for n in range(3))
        return (high + middle) + low

    txe_ref[0] = trans(perm_of(low_ref, 128), perm_of(from_low_ref, 128))
    txe_ref[1] = trans(perm_of(high_ref, 128), perm_of(from_high_ref, 128))

    def beyond(below, above):
        below, above = below.reshape(FLAT), above.reshape(FLAT)
        return jnp.where(lane % 2 == 0, turn(below, 1), turn(above, 127))

    t_side = trans(
        perm_of(side_ref, 2).reshape(FLAT), beyond(perm_of(side_low_ref, 2), perm_of(side_high_ref, 2))
    )

    def side_pair(which):
        here = side_ref[which].astype(F32).reshape(FLAT)
        return here, beyond(side_low_ref[which].astype(F32), side_high_ref[which].astype(F32))

    p_here, p_next = side_pair(0)
    s_here, s_next = side_pair(1)
    qy_ref[...] = two_pieces(face(t_side, s_here * s_here, s_next * s_next, p_here, p_next))
    square = (128, 128)
    ends = lane_of(square) == jnp.where(sub_of(square) % 2 == 0, 0, 127)
    ends_ref[...] = two_times(jnp.where(ends, 1.0, 0.0).astype(BF16))
    lane_row = lane_of((1, 128))

    def edge(own_ref, other_ref, which, snap):
        s_here, s_next = own_ref[64 + snap].astype(F32), other_ref[64 + snap].astype(F32)
        p_here, p_next = own_ref[snap].astype(F32), other_ref[snap].astype(F32)
        return face(txe_ref[which], s_here * s_here, s_next * s_next, p_here, p_next)

    def put(part):
        span = pl.ds(part * 32, 32)
        return pltpu.make_async_copy(out_ref.at[span], out_hbm.at[span], sem.at[part])

    def group(number, carry):
        for k in range(8):
            snap = number * 8 + k
            start = pl.multiple_of(snap * 64, 64)
            here = (lane_row == 2 * snap) | (lane_row == (2 * snap + 127) % 128)
            here = jnp.where(here, 1.0, 0.0).astype(BF16)
            sides = matmul(qy_ref[...] * jnp.concatenate([here, here], 1), ends_ref[...])
            flux_ref[pl.ds(start, 64), :] = inner_ref[pl.ds(start, 64), :] + sides
            low, high = pl.ds(start, 8, stride=8), pl.ds(start + 7, 8, stride=8)
            flux_ref[low, :] = flux_ref[low, :] + edge(low_ref, from_low_ref, 0, snap)
            flux_ref[high, :] = flux_ref[high, :] + edge(high_ref, from_high_ref, 1, snap)
        for k in range(8):
            snap = number * 8 + k
            flux = flux_ref[pl.ds(pl.multiple_of(snap * 64, 64), 64), :]
            out_ref[snap] = flux.reshape(CUBE).astype(BF16)
            rows = matmul(two_pieces(flux), cells_ref[...]).reshape(CUBE) * hits_ref[...]
            picked_ref[pl.ds(pl.multiple_of(snap * 8, 8), 8), :] = jnp.sum(rows, 0)
        return carry

    for part in range(2):
        lax.fori_loop(4 * part, 4 * part + 4, group, 0)
        put(part).start()

    total = picked_ref[pl.ds(0, 64, stride=8), :]
    for x in range(1, 8):
        total = total + picked_ref[pl.ds(x, 64, stride=8), :]
    rows = jnp.transpose(jnp.concatenate([total, jnp.zeros(FLAT, F32)], 0))
    mine_ref[...] = rows[:32]
    send_ref[...] = rows[32:64]
    for part in range(2):
        put(part).wait()


def tree_kernel(where_ref, pick_ref, mine_ref, other_ref, out_hbm, level_ref, kept_ref, out_ref, weights_ref, sem):
    tall = (256, 128)
    same = (sub_of(tall) % 64 == lane_of(tall) % 64) & (sub_of(tall) // 128 == lane_of(tall) // 64)
    weights_ref[...] = jnp.where(same, 1.0, 0.0).astype(BF16)

    def keep(node, upper, lower):
        both = matmul(jnp.concatenate([upper, lower], 1), weights_ref[...])
        kept_ref[pl.ds(node * KEPT, 32), :] = both

    def select(node, stack):
        rows = matmul(pick_ref[node - 64], stack).astype(BF16)
        level_ref[node - 64] = rows
        keep(node, rows[:32], rows[32:])

    def first_levels(low_ref, high_ref):
        for chip in range(64):
            keep(chip, low_ref[chip], high_ref[chip])
        for j in range(32):
            pair = [low_ref[2 * j], high_ref[2 * j], low_ref[2 * j + 1], high_ref[2 * j + 1]]
            select(64 + j, jnp.concatenate(pair, 0))

    @pl.when(where_ref[0] % 2 == 0)
    def _():
        first_levels(mine_ref, other_ref)

    @pl.when(where_ref[0] % 2 == 1)
    def _():
        first_levels(other_ref, mine_ref)

    before, offset, count = 64, 96, 16
    while count >= 1:
        for j in range(count):
            select(offset + j, level_ref[pl.ds(before + 2 * j - 64, 2)].reshape(128, 128))
        before, offset, count = offset, offset + count, count // 2

    def put(at):
        span = pl.ds(at, 8)
        return pltpu.make_async_copy(out_ref.at[span], out_hbm.at[span], sem.at[at // 8])

    for group in range(4):
        for q in range(8 * group, 8 * group + 8):
            turned = jnp.transpose(kept_ref[pl.ds(q, 128, stride=KEPT), :])
            out_ref[q] = turned[:64, :127]
            out_ref[q + 32] = turned[64:, :127]
        put(8 * group).start()
        put(8 * group + 32).start()
    for at in range(0, 64, 8):
        put(at).wait()


def local(states, class_map, perm_table, candidates, merge_order):
    tile = lax.axis_index("gx") * lax.axis_size("gy") + lax.axis_index("gy")
    where = tile.reshape(1).astype(jnp.int32)
    states, class_map, perm_table, candidates, merge_rows = (
        pltpu.with_memory_space_constraint(value, pltpu.HBM)
        for value in (states, class_map, perm_table, candidates.reshape(128, 64), merge_order)
    )
    edge_shape, side_shape, states_shape = (131, 8, 128), (5, 8, 8, 128), (2, 64, 8, 8, 128)
    read_scratch = [pltpu.VMEM(CUBE, jnp.int32), pltpu.SMEM((8,), F32)]
    low, high = pl.pallas_call(
        edge_x_kernel,
        in_specs=[HBM, HBM, HBM],
        out_specs=[whole(edge_shape), whole(edge_shape)],
        out_shape=[jax.ShapeDtypeStruct(edge_shape, BF16), jax.ShapeDtypeStruct(edge_shape, BF16)],
        scratch_shapes=[pltpu.VMEM(states_shape, BF16)]
        + read_scratch
        + [pltpu.VMEM((129 * 64, 128), F32), pltpu.SemaphoreType.DMA((4,))],
        compiler_params=LIMIT,
    )(perm_table, class_map, states)

    def shift(value, axis, by):
        count = lax.axis_size(axis)
        return lax.ppermute(value, axis, [(i, (i + by) % count) for i in range(count)])

    from_low = shift(high, "gx", 1)
    from_high = shift(low, "gx", -1)

    side, perm, near_states, cells, hits = pl.pallas_call(
        edge_y_kernel,
        in_specs=[SMEM] + [HBM] * 5,
        out_specs=[whole(side_shape), whole(CUBE), whole(states_shape), whole((256, 128)), whole(CUBE)],
        out_shape=[
            jax.ShapeDtypeStruct(side_shape, BF16),
            jax.ShapeDtypeStruct(CUBE, F32),
            jax.ShapeDtypeStruct(states_shape, BF16),
            jax.ShapeDtypeStruct((256, 128), BF16),
            jax.ShapeDtypeStruct(CUBE, F32),
        ],
        scratch_shapes=[
            pltpu.VMEM(CUBE, jnp.int32),
            pltpu.VMEM((1, 64), jnp.int32),
            pltpu.VMEM((1, 128), jnp.int32),
            pltpu.SMEM((8,), F32),
            pltpu.SemaphoreType.DMA((6,)),
        ],
        compiler_params=LIMIT,
    )(where, perm_table, class_map, candidates, merge_rows, states)
    side_low = shift(side, "gy", 1)
    side_high = shift(side, "gy", -1)

    inner = pl.pallas_call(
        inner_kernel,
        in_specs=[whole(CUBE), whole(states_shape)],
        out_specs=whole((4096, 128)),
        out_shape=jax.ShapeDtypeStruct((4096, 128), F32),
        scratch_shapes=[
            pltpu.VMEM(CUBE, F32),
            pltpu.VMEM(FLAT, F32),
            pltpu.VMEM((7, 8, 128), F32),
            pltpu.VMEM((128, 128), BF16),
            pltpu.VMEM((256, 128), BF16),
        ],
        compiler_params=LIMIT,
    )(perm, near_states)
    numbers = lax.broadcasted_iota(jnp.int32, (63, 64, 128), 2)
    picks = (merge_order[64:, :64, None] == numbers).astype(BF16)
    inner, picks = lax.optimization_barrier((inner, picks))

    flux, mine_rows, send_rows = pl.pallas_call(
        outer_kernel,
        in_specs=[whole((4096, 128)), whole((256, 128)), whole(CUBE)]
        + [whole(edge_shape)] * 2 + [whole(side_shape)] + [whole(edge_shape)] * 2 + [whole(side_shape)] * 2,
        out_specs=[HBM, whole((32, 128)), whole((32, 128))],
        out_shape=[
            jax.ShapeDtypeStruct((64, 8, 8, 128), BF16),
            jax.ShapeDtypeStruct((32, 128), F32),
            jax.ShapeDtypeStruct((32, 128), F32),
        ],
        scratch_shapes=[
            pltpu.VMEM((4096, 128), F32),
            pltpu.VMEM((64, 8, 8, 128), BF16),
            pltpu.VMEM((2, 8, 128), F32),
            pltpu.VMEM((64, 256), BF16),
            pltpu.VMEM((256, 128), BF16),
            pltpu.VMEM((512, 128), F32),
            pltpu.SemaphoreType.DMA((2,)),
        ],
        compiler_params=LIMIT,
    )(inner, cells, hits, low, high, side, from_low, from_high, side_low, side_high)

    swap = [(i, i ^ 1) for i in range(8)]
    got_rows = lax.ppermute(send_rows, "gy", swap)
    merged = mine_rows[:, :64] + got_rows[:, :64]
    top = merged.astype(BF16)
    rest = (merged - lax.reduce_precision(merged, 8, 7)).astype(BF16)
    spread = jnp.broadcast_to(jnp.concatenate([top, rest], 1)[None], (64, 32, 128))
    peers = [[i * 8 + j * 2 + c for i in range(16) for j in range(4)] for c in range(2)]
    mine = lax.all_to_all(spread, ("gx", "gy"), 0, 0, axis_index_groups=peers)
    other = lax.ppermute(mine, "gy", swap)

    kept = pl.pallas_call(
        tree_kernel,
        in_specs=[SMEM, whole((63, 64, 128)), whole((64, 32, 128)), whole((64, 32, 128))],
        out_specs=HBM,
        out_shape=jax.ShapeDtypeStruct((64, 64, 127), F32),
        scratch_shapes=[
            pltpu.VMEM((63, 64, 128), BF16),
            pltpu.VMEM((128 * KEPT, 128), F32),
            pltpu.VMEM((64, 64, 127), F32),
            pltpu.VMEM((256, 128), BF16),
            pltpu.SemaphoreType.DMA((8,)),
        ],
        compiler_params=LIMIT,
    )(where, picks, mine, other)
    return flux, jnp.transpose(kept, (2, 0, 1))


def solution(mesh):
    in_specs = (P(None, None, None, "gx", "gy"), P(None, "gx", "gy"), P(), P(), P())
    out_specs = (P(None, None, "gx", "gy"), P())
    return jax.shard_map(local, mesh=mesh, in_specs=in_specs, out_specs=out_specs, check_vma=False)
```

time: 49.2 us -> 57.5 us (1.17)
  Pallas kernels: 14.3 us -> 22.7 us
  blocking collectives: 18.5 us -> 17.4 us
  waiting for transfers between devices: 1.54 us -> 2.39 us
    pallas_call x1, Pallas kernels: 4.5 us -> 10.4 us  [local(): pl.pallas_call(inner_kernel, in_specs=[whole(CUBE), whole(states_shape)],...]
    pallas_call x2, Pallas kernels: 4.75 us -> 6.63 us  [the longest x1 3.94 us: local(): pl.pallas_call(outer_kernel, in_specs=[whole((4096, 128)), whole((256, 12...]
    all_to_all x1, blocking collectives: 18.5 us -> 17.4 us  [local(): mine = lax.all_to_all(spread, ('gx', 'gy'), 0, 0, axis_index_groups=peers)]
    ppermute x1, waiting for transfers between devices: 0.69 us -> 1.54 us  [local(): other = lax.ppermute(mine, 'gy', swap)]
    pallas_call x1, Pallas kernels: 3.4 us -> 4.03 us  [local(): pl.pallas_call(tree_kernel, in_specs=[SMEM, whole((63, 64, 128)), whole((...]
  transfers between devices with their start and end apart: 6 -> 6, of which waited for: 2 -> 2; matrix products, arithmetic and copies ran while one was open for 2% -> 1% of each run, Pallas kernels for 13% -> 23%
where the time goes in v4:
time: 57.5 us; the launch traced here: 57.3 us
  Pallas kernels  22.7 us (39%)
  blocking collectives  17.4 us (30%)
  starting transfers between devices  13 us (23%)
  waiting for transfers between devices  2.39 us (4%)
  other arithmetic  0.94 us (2%)
  between operations  0.72 us (1%)
    all_to_all x1, blocking collectives, local(): mine = lax.all_to_all(spread, ('gx', 'gy'), 0, 0, axis_index_groups=peers)  17.4 us
    pallas_call x1, Pallas kernels, local(): pl.pallas_call(inner_kernel, in_specs=[whole(CUBE), whole(states_shape)],...  10.4 us
    ppermute x4, starting transfers between devices, shift(): lax.ppermute(value, axis, [(i, (i + by) % count) for i in range(count)])  9.08 us
    pallas_call x1, Pallas kernels, local(): pl.pallas_call(tree_kernel, in_specs=[SMEM, whole((63, 64, 128)), whole((...  4.03 us
    pallas_call x1, Pallas kernels, local(): pl.pallas_call(outer_kernel, in_specs=[whole((4096, 128)), whole((256, 12...  3.94 us
    pallas_call x1, Pallas kernels, local(): pl.pallas_call(edge_y_kernel, in_specs=[SMEM] + [HBM] * 5, out_specs=[who...  2.69 us
    ppermute x1, starting transfers between devices, local(): other = lax.ppermute(mine, 'gy', swap)  2.04 us
    ppermute x1, starting transfers between devices, local(): got_rows = lax.ppermute(send_rows, 'gy', swap)  1.83 us
  transfers between devices with their start and end apart: 6, of which 2 were waited for; matrix products, arithmetic and copies ran while one was open for 1% of the time, Pallas kernels for 23%

profile of v4, /device:TPU:1, one launch (start us, length us, event | category | flops | bytes accessed | tf_op | source)
XLA Modules:
  0.0 57.3 jit_solution(4450920148555070369)
XLA Ops:
  0.6 0.0 copy-start
  0.6 1.7 %shard_map.70 = (bf16[131,8,128]{2,1,0:T(8,128)(2,1)S(1)}, bf16[131,8,128]{2,1,0:T(8,128)(2,1)S(1)}) custom-call(f32[8]{0:T(128)} %table_hbm.3, s32[8,8,128]{2,1,0:T(8,128)} %class_hbm.3, bf16[2,64,8,8,128]{4,3,2,1,0:T(8,128)(2,1)} %states_hbm.3), custom_call_target="tpu_custom_call" | custom-call | tf_op jit(solution)/shard_map/pallas_call | solution.py:319
  2.4 2.5 %collective-permute-start = (bf16[131,8,128]{2,1,0:T(8,128)(2,1)S(1)}, bf16[131,8,128]{2,1,0:T(8,128)(2,1)S(1)}, u32[]{:S(2)}, u32[]{:S(2)}) collective-permute-start(bf16[131,8,128]{2,1,0:T(8,128)(2,1)S(1)} %get-tuple-element.20.high_ref), channel_id=1, source_target_pairs={{0,8},{8,16},{16,24},{24,32},{32,40},{40,48},{48,56},{56,64},{64,7... | collective-permute-start | bytes 804872 | tf_op jit(solution)/shard_map/ppermute | solution.py:332
  4.9 4.4 %collective-permute-start.1 = (bf16[131,8,128]{2,1,0:T(8,128)(2,1)S(1)}, bf16[131,8,128]{2,1,0:T(8,128)(2,1)S(1)}, u32[]{:S(2)}, u32[]{:S(2)}) collective-permute-start(bf16[131,8,128]{2,1,0:T(8,128)(2,1)S(1)} %get-tuple-element.19.low_ref), channel_id=1, source_target_pairs={{0,120},{8,0},{16,8},{24,16},{32,24},{40,32},{48,40},{56,48},{64,5... | collective-permute-start | bytes 804872 | tf_op jit(solution)/shard_map/ppermute | solution.py:332
  9.3 2.7 %shard_map.68 = (bf16[5,8,8,128]{3,2,1,0:T(8,128)(2,1)S(1)}, f32[8,8,128]{2,1,0:T(8,128)S(1)}, bf16[2,64,8,8,128]{4,3,2,1,0:T(8,128)(2,1)S(1)}, bf16[256,128]{1,0:T(8,128)(2,1)S(1)}, f32[8,8,128]{2,1,0:T(8,128)S(1)}) custom-call(s32[1]{0:T(128)} %bitcast.where_ref, f32[8]{0:T(128)} %table_hbm.3, s32[8,8,128]{2,1,0:T(8,128)} %class_hbm.3, s32[128,64]{1,0:T(8,128)} %bitcast.4, ...), custom_call_target="tpu_custom_call" | custom-call | tf_op jit(solution)/shard_map/pallas_call | solution.py:337
  12.0 2.1 %collective-permute-start.2 = (bf16[5,8,8,128]{3,2,1,0:T(8,128)(2,1)S(1)}, bf16[5,8,8,128]{3,2,1,0:T(8,128)(2,1)S(1)}, u32[]{:S(2)}, u32[]{:S(2)}) collective-permute-start(bf16[5,8,8,128]{3,2,1,0:T(8,128)(2,1)S(1)} %get-tuple-element.21.side_ref), channel_id=1, source_target_pairs={{0,1},{1,2},{2,3},{3,4},{4,5},{5,6},{6,7},{7,0},{8,9},{9,10},{10,1... | collective-permute-start | bytes 245768 | tf_op jit(solution)/shard_map/ppermute | solution.py:332
  14.1 0.0 collective-permute-start.3
  14.1 0.0 copy-done
  14.2 0.8 %fusion.pick_ref = bf16[63,64,128]{2,1,0:T(8,128)(2,1)S(1)} fusion(s32[63,64]{1,0:T(8,128)S(1)} %slice.9), kind=kLoop, calls=%fused_computation.1 | loop fusion | flops 1032192 | bytes 1048320 | tf_op jit(solution)/shard_map/convert_element_type | solution.py:375
  15.0 10.4 %shard_map.69.inner_ref = f32[4096,128]{1,0:T(8,128)S(1)} custom-call(f32[8,8,128]{2,1,0:T(8,128)S(1)} %get-tuple-element.14.perm_ref, bf16[2,64,8,8,128]{4,3,2,1,0:T(8,128)(2,1)S(1)} %get-tuple-element.15.states_ref), custom_call_target="tpu_custom_call" | custom-call | tf_op jit(solution)/shard_map/pallas_call | solution.py:360
  25.4 0.0 collective-permute-done.2.side_low_ref
  25.4 0.0 collective-permute-done.3.side_high_ref
  25.4 0.0 collective-permute-done.from_low_ref
  25.4 0.0 collective-permute-done.1.from_high_ref
  25.4 3.9 %shard_map.71 = (bf16[64,8,8,128]{3,2,1,0:T(8,128)(2,1)}, f32[32,128]{1,0:T(8,128)S(1)}, f32[32,128]{1,0:T(8,128)S(1)}) custom-call(f32[4096,128]{1,0:T(8,128)S(1)} %shard_map.69.inner_ref, bf16[256,128]{1,0:T(8,128)(2,1)S(1)} %get-tuple-element.17.cells_ref, f32[8,8,128]{2,1,0:T(8,128)S(1)} %get-tuple-element.18.hits_ref, ...), custom_call_target="tpu_custom_call" | custom-call | tf_op jit(solution)/shard_map/pallas_call | solution.py:378
  29.4 1.8 %collective-permute-start.4 = (f32[32,128]{1,0:T(8,128)S(1)}, f32[32,128]{1,0:T(8,128)S(1)}, u32[]{:S(2)}, u32[]{:S(2)}) collective-permute-start(f32[32,128]{1,0:T(8,128)S(1)} %get-tuple-element.25), channel_id=1, source_target_pairs={{0,1},{1,0},{2,3},{3,2},{4,5},{5,4},{6,7},{7,6},{8,9},{9,8},{10,11... | collective-permute-start | bytes 49160 | tf_op jit(solution)/shard_map/ppermute | solution.py:401
  31.2 0.8 %collective-permute-done.4 = f32[32,128]{1,0:T(8,128)S(1)} collective-permute-done((f32[32,128]{1,0:T(8,128)S(1)}, f32[32,128]{1,0:T(8,128)S(1)}, u32[]{:S(2)}, u32[]{:S(2)}) %collective-permute-start.4) | collective-permute-done | bytes 16416 | tf_op jit(solution)/shard_map/ppermute | solution.py:401
  32.1 0.1 pad_maximum_fusion
  32.1 0.1 broadcast_in_dim.2
  32.2 17.4 %all_to_all.5.mine_ref = bf16[64,32,128]{2,1,0:T(8,128)(2,1)S(1)} all-to-all(bf16[64,32,128]{2,1,0:T(8,128)(2,1)S(1)} %broadcast_in_dim.2), channel_id=1, replica_groups={{0,2,4,6,8,10,12,14,16,18,20,22,24,26,28,30,32,34,36,38,40,42,44,46,48,..., dimensions={0} | all-to-all | bytes 1048576 | tf_op jit(solution)/shard_map/all_to_all | solution.py:407
  49.7 2.0 %collective-permute-start.5 = (bf16[64,32,128]{2,1,0:T(8,128)(2,1)S(1)}, bf16[64,32,128]{2,1,0:T(8,128)(2,1)S(1)}, u32[]{:S(2)}, u32[]{:S(2)}) collective-permute-start(bf16[64,32,128]{2,1,0:T(8,128)(2,1)S(1)} %all_to_all.5.mine_ref), channel_id=1, source_target_pairs={{0,1},{1,0},{2,3},{3,2},{4,5},{5,4},{6,7},{7,6},{8,9},{9,8},{10,11... | collective-permute-start | bytes 1572872 | tf_op jit(solution)/shard_map/ppermute | solution.py:408
  51.7 1.5 %collective-permute-done.5.other_ref = bf16[64,32,128]{2,1,0:T(8,128)(2,1)S(1)} collective-permute-done((bf16[64,32,128]{2,1,0:T(8,128)(2,1)S(1)}, bf16[64,32,128]{2,1,0:T(8,128)(2,1)S(1)}, u32[]{:S(2)}, u32[]{:S(2)}) %collective-permute-start.5) | collective-permute-done | bytes 524320 | tf_op jit(solution)/shard_map/ppermute | solution.py:408
  53.2 4.0 %shard_map.72 = f32[64,64,127]{2,1,0:T(8,128)} custom-call(s32[1]{0:T(128)} %bitcast.where_ref, bf16[63,64,128]{2,1,0:T(8,128)(2,1)S(1)} %fusion.pick_ref, bf16[64,32,128]{2,1,0:T(8,128)(2,1)S(1)} %all_to_all.5.mine_ref, bf16[64,32,128]{2,1,0:T(8,128)(2,1)S(1)} %collective-permute-done.5.other_ref), custom_call_target="tpu_custom_call" | custom-call | tf_op jit(solution)/shard_map/pallas_call | solution.py:410
  (2 shorter events, 0.0 us)
Async XLA Ops:
  0.6 13.5 %copy-start = (s32[127,128]{1,0:T(8,128)S(1)}, s32[127,128]{1,0:T(8,128)}, u32[]{:S(2)}) copy-start(s32[127,128]{1,0:T(8,128)} %order_hbm.1) | copy-start | bytes 195076
  2.4 23.1 %collective-permute-start = (bf16[131,8,128]{2,1,0:T(8,128)(2,1)S(1)}, bf16[131,8,128]{2,1,0:T(8,128)(2,1)S(1)}, u32[]{:S(2)}, u32[]{:S(2)}) collective-permute-start(bf16[131,8,128]{2,1,0:T(8,128)(2,1)S(1)} %get-tuple-element.20.high_ref), channel_id=1, source_target_pairs={{0,8},{8,16},{16,24},{24,32},{32,40},{40,48},{48,56},{56,64},{64,7... | collective-permute-start | bytes 804872 | tf_op jit(solution)/shard_map/ppermute | solution.py:332
  4.9 20.5 %collective-permute-start.1 = (bf16[131,8,128]{2,1,0:T(8,128)(2,1)S(1)}, bf16[131,8,128]{2,1,0:T(8,128)(2,1)S(1)}, u32[]{:S(2)}, u32[]{:S(2)}) collective-permute-start(bf16[131,8,128]{2,1,0:T(8,128)(2,1)S(1)} %get-tuple-element.19.low_ref), channel_id=1, source_target_pairs={{0,120},{8,0},{16,8},{24,16},{32,24},{40,32},{48,40},{56,48},{64,5... | collective-permute-start | bytes 804872 | tf_op jit(solution)/shard_map/ppermute | solution.py:332
  12.0 13.4 %collective-permute-start.2 = (bf16[5,8,8,128]{3,2,1,0:T(8,128)(2,1)S(1)}, bf16[5,8,8,128]{3,2,1,0:T(8,128)(2,1)S(1)}, u32[]{:S(2)}, u32[]{:S(2)}) collective-permute-start(bf16[5,8,8,128]{3,2,1,0:T(8,128)(2,1)S(1)} %get-tuple-element.21.side_ref), channel_id=1, source_target_pairs={{0,1},{1,2},{2,3},{3,4},{4,5},{5,6},{6,7},{7,0},{8,9},{9,10},{10,1... | collective-permute-start | bytes 245768 | tf_op jit(solution)/shard_map/ppermute | solution.py:332
  14.1 11.3 %collective-permute-start.3 = (bf16[5,8,8,128]{3,2,1,0:T(8,128)(2,1)S(1)}, bf16[5,8,8,128]{3,2,1,0:T(8,128)(2,1)S(1)}, u32[]{:S(2)}, u32[]{:S(2)}) collective-permute-start(bf16[5,8,8,128]{3,2,1,0:T(8,128)(2,1)S(1)} %get-tuple-element.21.side_ref), channel_id=1, source_target_pairs={{0,7},{1,0},{2,1},{3,2},{4,3},{5,4},{6,5},{7,6},{8,15},{9,8},{10,9... | collective-permute-start | bytes 245768 | tf_op jit(solution)/shard_map/ppermute | solution.py:332
  29.4 2.7 %collective-permute-start.4 = (f32[32,128]{1,0:T(8,128)S(1)}, f32[32,128]{1,0:T(8,128)S(1)}, u32[]{:S(2)}, u32[]{:S(2)}) collective-permute-start(f32[32,128]{1,0:T(8,128)S(1)} %get-tuple-element.25), channel_id=1, source_target_pairs={{0,1},{1,0},{2,3},{3,2},{4,5},{5,4},{6,7},{7,6},{8,9},{9,8},{10,11... | collective-permute-start | bytes 49160 | tf_op jit(solution)/shard_map/ppermute | solution.py:401
  49.7 3.6 %collective-permute-start.5 = (bf16[64,32,128]{2,1,0:T(8,128)(2,1)S(1)}, bf16[64,32,128]{2,1,0:T(8,128)(2,1)S(1)}, u32[]{:S(2)}, u32[]{:S(2)}) collective-permute-start(bf16[64,32,128]{2,1,0:T(8,128)(2,1)S(1)} %all_to_all.5.mine_ref), channel_id=1, source_target_pairs={{0,1},{1,0},{2,3},{3,2},{4,5},{5,4},{6,7},{7,6},{8,9},{9,8},{10,11... | collective-permute-start | bytes 1572872 | tf_op jit(solution)/shard_map/ppermute | solution.py:408

commit v5 on v4

--- a/solution.py
+++ b/solution.py
@@ -7,9 +7,12 @@
 
 F32 = jnp.float32
 BF16 = jnp.bfloat16
-KEPT = 40
+KEPT = 72
+UNROLL = 64
 CUBE = (8, 8, 128)
 FLAT = (64, 128)
+EDGE = (131, 8, 128)
+SIDE = (5, 8, 8, 128)
 HBM = pl.BlockSpec(memory_space=pltpu.HBM)
 SMEM = pl.BlockSpec(memory_space=pltpu.SMEM)
 LIMIT = pltpu.CompilerParams(vmem_limit_bytes=48 * 1024 * 1024)
@@ -125,7 +128,7 @@
     at_y = jnp.where(cell < 0, -1, cell % 128)
     at_zx = jnp.where(cell < 0, -1, cell // 128)
     cells_ref[...] = two_times(jnp.where(sub_of((128, 128)) == at_y, 1.0, 0.0).astype(BF16))
-    hits_ref[...] = jnp.where(sub_of(FLAT) == at_zx, 1.0, 0.0).reshape(CUBE)
+    hits_ref[...] = jnp.where(sub_of(FLAT) == at_zx, 1.0, 0.0)
 
     perm = look_up(class_ref[...], table_ref)
     perm_ref[...] = perm
@@ -147,7 +150,7 @@
         side_ref[field] = acc[field].reshape(CUBE).astype(BF16)
 
 
-def inner_kernel(perm_ref, states_ref, out_ref, tx_ref, ty_ref, tz_ref, shift_ref, differ_ref):
+def inner_kernel(perm_ref, states_ref, out_ref, tx_ref, ty_ref, tz_ref, shift_ref):
     perm = perm_ref[...]
     row = lax.broadcasted_iota(jnp.int32, CUBE, 1)
     next_y = turn(perm.reshape(FLAT), 127).reshape(CUBE)
@@ -155,13 +158,11 @@
     ty_ref[...] = jnp.where(lane_of(CUBE) == 127, 0.0, trans(perm, next_y)).reshape(FLAT)
     tz_ref[...] = trans(perm[:-1], perm[1:])
     square = (128, 128)
-    ahead = sub_of(square) - lane_of(square)
-    shift_ref[...] = jnp.where(ahead == 1, 1.0, 0.0).astype(BF16)
-    differ_ref[...] = two_times((jnp.where(ahead == 0, 1.0, 0.0) - jnp.where(ahead == -1, 1.0, 0.0)).astype(BF16))
+    shift_ref[...] = jnp.where(sub_of(square) == lane_of(square) + 1, 1.0, 0.0).astype(BF16)
 
     def group(number, carry):
-        for k in range(8):
-            snap = number * 8 + k
+        for k in range(16):
+            snap = number * 16 + k
             p = states_ref[0, snap].astype(F32)
             s = states_ref[1, snap].astype(F32)
             m = s * s
@@ -170,30 +171,32 @@
             p_next = matmul(states_ref[0, snap].reshape(FLAT), shift_ref[...])
             s_next = matmul(states_ref[1, snap].reshape(FLAT), shift_ref[...])
             fy = face(ty_ref[...], m.reshape(FLAT), s_next * s_next, p.reshape(FLAT), p_next)
-            total = total + matmul(two_pieces(fy), differ_ref[...]).reshape(CUBE)
+            total = total + (fy - turn(fy, 1)).reshape(CUBE)
             fz = face(tz_ref[...], m[:-1], m[1:], p[:-1], p[1:])
             zero = jnp.zeros((1, 8, 128), F32)
             total = total + (jnp.concatenate([fz, zero], 0) - jnp.concatenate([zero, fz], 0))
             out_ref[pl.ds(pl.multiple_of(snap * 64, 64), 64), :] = total.reshape(FLAT)
         return carry
 
-    lax.fori_loop(0, 8, group, 0)
-
-
-def outer_kernel(
-    inner_ref, cells_ref, hits_ref, low_ref, high_ref, side_ref,
-    from_low_ref, from_high_ref, side_low_ref, side_high_ref,
-    out_hbm, mine_ref, send_ref,
-    flux_ref, out_ref, txe_ref, qy_ref, ends_ref, picked_ref, sem,
+    lax.fori_loop(0, 4, group, 0)
+
+
+def sum_of_eights(picked_ref):
+    total = picked_ref[pl.ds(0, 64, stride=8), :]
+    for at in range(1, 8):
+        total = total + picked_ref[pl.ds(at, 64, stride=8), :]
+    return total
+
+
+def perm_of(ref, at):
+    high, middle, low = (ref[at + n].astype(F32) for n in range(3))
+    return (high + middle) + low
+
+
+def middle_kernel(
+    inner_ref, cells_ref, hits_ref, side_ref, side_low_ref, side_high_ref, flux_ref, rows_ref, qy_ref, picked_ref
 ):
     lane = lane_of(FLAT)
-
-    def perm_of(ref, at):
-        high, middle, low = (ref[at + n].astype(F32) for n in range(3))
-        return (high + middle) + low
-
-    txe_ref[0] = trans(perm_of(low_ref, 128), perm_of(from_low_ref, 128))
-    txe_ref[1] = trans(perm_of(high_ref, 128), perm_of(from_high_ref, 128))
 
     def beyond(below, above):
         below, above = below.reshape(FLAT), above.reshape(FLAT)
@@ -209,47 +212,69 @@
 
     p_here, p_next = side_pair(0)
     s_here, s_next = side_pair(1)
-    qy_ref[...] = two_pieces(face(t_side, s_here * s_here, s_next * s_next, p_here, p_next))
-    square = (128, 128)
-    ends = lane_of(square) == jnp.where(sub_of(square) % 2 == 0, 0, 127)
-    ends_ref[...] = two_times(jnp.where(ends, 1.0, 0.0).astype(BF16))
-    lane_row = lane_of((1, 128))
-
-    def edge(own_ref, other_ref, which, snap):
+    qy_ref[...] = face(t_side, s_here * s_here, s_next * s_next, p_here, p_next)
+    at_edge = (lane == 0) | (lane == 127)
+
+    def group(number, carry):
+        for k in range(UNROLL):
+            snap = number * UNROLL + k
+            span = pl.ds(pl.multiple_of(snap * 64, 64), 64)
+            turned = turn(qy_ref[...], (128 - 2 * snap) % 128)
+            flux = inner_ref[span, :] + jnp.where(at_edge, turned, 0.0)
+            flux_ref[span, :] = flux
+            rows = matmul(two_pieces(flux), cells_ref[...]) * hits_ref[...]
+            picked_ref[pl.ds(pl.multiple_of(snap * 8, 8), 8), :] = jnp.sum(rows.reshape(CUBE), 0)
+        return carry
+
+    lax.fori_loop(0, 64 // UNROLL, group, 0)
+    rows_ref[...] = sum_of_eights(picked_ref)
+
+
+def outer_kernel(
+    within_ref, rows_ref, cells_ref, hits_ref, low_ref, high_ref, from_low_ref, from_high_ref,
+    out_hbm, mine_ref, send_ref, out_ref, edge_ref, qx_ref, picked_ref, sem,
+):
+    t_low = trans(perm_of(low_ref, 128), perm_of(from_low_ref, 128))
+    t_high = trans(perm_of(high_ref, 128), perm_of(from_high_ref, 128))
+    edge_ref[...] = jnp.zeros_like(edge_ref)
+
+    def edge(own_ref, other_ref, t, snap):
         s_here, s_next = own_ref[64 + snap].astype(F32), other_ref[64 + snap].astype(F32)
         p_here, p_next = own_ref[snap].astype(F32), other_ref[snap].astype(F32)
-        return face(txe_ref[which], s_here * s_here, s_next * s_next, p_here, p_next)
+        return face(t, s_here * s_here, s_next * s_next, p_here, p_next)
 
     def put(part):
         span = pl.ds(part * 32, 32)
         return pltpu.make_async_copy(out_ref.at[span], out_hbm.at[span], sem.at[part])
 
     def group(number, carry):
-        for k in range(8):
-            snap = number * 8 + k
-            start = pl.multiple_of(snap * 64, 64)
-            here = (lane_row == 2 * snap) | (lane_row == (2 * snap + 127) % 128)
-            here = jnp.where(here, 1.0, 0.0).astype(BF16)
-            sides = matmul(qy_ref[...] * jnp.concatenate([here, here], 1), ends_ref[...])
-            flux_ref[pl.ds(start, 64), :] = inner_ref[pl.ds(start, 64), :] + sides
-            low, high = pl.ds(start, 8, stride=8), pl.ds(start + 7, 8, stride=8)
-            flux_ref[low, :] = flux_ref[low, :] + edge(low_ref, from_low_ref, 0, snap)
-            flux_ref[high, :] = flux_ref[high, :] + edge(high_ref, from_high_ref, 1, snap)
-        for k in range(8):
-            snap = number * 8 + k
-            flux = flux_ref[pl.ds(pl.multiple_of(snap * 64, 64), 64), :]
+        for k in range(16):
+            snap = number * 16 + k
+            q_low = edge(low_ref, from_low_ref, t_low, snap)
+            q_high = edge(high_ref, from_high_ref, t_high, snap)
+            at = pl.multiple_of(snap * 16, 16)
+            qx_ref[pl.ds(at, 8), :] = q_low
+            qx_ref[pl.ds(at + 8, 8), :] = q_high
+            edge_ref[pl.ds(k * 64, 8, stride=8), :] = q_low
+            edge_ref[pl.ds(k * 64 + 7, 8, stride=8), :] = q_high
+        for k in range(16):
+            snap = number * 16 + k
+            flux = within_ref[pl.ds(pl.multiple_of(snap * 64, 64), 64), :] + edge_ref[pl.ds(k * 64, 64), :]
             out_ref[snap] = flux.reshape(CUBE).astype(BF16)
-            rows = matmul(two_pieces(flux), cells_ref[...]).reshape(CUBE) * hits_ref[...]
-            picked_ref[pl.ds(pl.multiple_of(snap * 8, 8), 8), :] = jnp.sum(rows, 0)
         return carry
 
     for part in range(2):
-        lax.fori_loop(4 * part, 4 * part + 4, group, 0)
+        lax.fori_loop(2 * part, 2 * part + 2, group, 0)
         put(part).start()
 
-    total = picked_ref[pl.ds(0, 64, stride=8), :]
-    for x in range(1, 8):
-        total = total + picked_ref[pl.ds(x, 64, stride=8), :]
+    hit_low, hit_high = hits_ref[pl.ds(0, 8, stride=8), :], hits_ref[pl.ds(7, 8, stride=8), :]
+    for part in range(4):
+        rows = matmul(two_pieces(qx_ref[pl.ds(part * 256, 256), :]), cells_ref[...])
+        for k in range(16):
+            low = rows[k * 16 : k * 16 + 8] * hit_low
+            high = rows[k * 16 + 8 : k * 16 + 16] * hit_high
+            picked_ref[pl.ds((part * 16 + k) * 8, 8), :] = low + high
+    total = rows_ref[...] + sum_of_eights(picked_ref)
     rows = jnp.transpose(jnp.concatenate([total, jnp.zeros(FLAT, F32)], 0))
     mine_ref[...] = rows[:32]
     send_ref[...] = rows[32:64]
@@ -257,26 +282,19 @@
         put(part).wait()
 
 
-def tree_kernel(where_ref, pick_ref, mine_ref, other_ref, out_hbm, level_ref, kept_ref, out_ref, weights_ref, sem):
-    tall = (256, 128)
-    same = (sub_of(tall) % 64 == lane_of(tall) % 64) & (sub_of(tall) // 128 == lane_of(tall) // 64)
-    weights_ref[...] = jnp.where(same, 1.0, 0.0).astype(BF16)
-
-    def keep(node, upper, lower):
-        both = matmul(jnp.concatenate([upper, lower], 1), weights_ref[...])
-        kept_ref[pl.ds(node * KEPT, 32), :] = both
-
+def tree_kernel(where_ref, pick_ref, mine_ref, other_ref, out_hbm, level_ref, kept_ref, out_ref, sem):
     def select(node, stack):
-        rows = matmul(pick_ref[node - 64], stack).astype(BF16)
-        level_ref[node - 64] = rows
-        keep(node, rows[:32], rows[32:])
+        got = matmul(pick_ref[node - 64], stack)
+        kept_ref[pl.ds(node * KEPT, 64), :] = got
+        level_ref[node - 64] = got.astype(BF16)
 
     def first_levels(low_ref, high_ref):
-        for chip in range(64):
-            keep(chip, low_ref[chip], high_ref[chip])
         for j in range(32):
             pair = [low_ref[2 * j], high_ref[2 * j], low_ref[2 * j + 1], high_ref[2 * j + 1]]
             select(64 + j, jnp.concatenate(pair, 0))
+        for chip in range(64):
+            kept_ref[pl.ds(chip * KEPT, 32), :] = low_ref[chip].astype(F32)
+            kept_ref[pl.ds(chip * KEPT + 32, 32), :] = high_ref[chip].astype(F32)
 
     @pl.when(where_ref[0] % 2 == 0)
     def _():
@@ -293,18 +311,64 @@
         before, offset, count = offset, offset + count, count // 2
 
     def put(at):
-        span = pl.ds(at, 8)
-        return pltpu.make_async_copy(out_ref.at[span], out_hbm.at[span], sem.at[at // 8])
-
-    for group in range(4):
-        for q in range(8 * group, 8 * group + 8):
-            turned = jnp.transpose(kept_ref[pl.ds(q, 128, stride=KEPT), :])
-            out_ref[q] = turned[:64, :127]
-            out_ref[q + 32] = turned[64:, :127]
-        put(8 * group).start()
-        put(8 * group + 32).start()
-    for at in range(0, 64, 8):
+        span = pl.ds(at, 16)
+        return pltpu.make_async_copy(out_ref.at[span], out_hbm.at[span], sem.at[at // 16])
+
+    for slot in range(64):
+        turned = jnp.transpose(kept_ref[pl.ds(slot, 128, stride=KEPT), :])
+        out_ref[slot] = (turned[:64] + turned[64:])[:, :127]
+        if slot % 16 == 15:
+            put(slot - 15).start()
+    for at in range(0, 64, 16):
         put(at).wait()
+
+
+def middle_call(*operands):
+    return pl.pallas_call(
+        middle_kernel,
+        in_specs=[whole((4096, 128)), whole((256, 128)), whole(FLAT), whole(SIDE), whole(SIDE), whole(SIDE)],
+        out_specs=[whole((4096, 128)), whole(FLAT)],
+        out_shape=[jax.ShapeDtypeStruct((4096, 128), F32), jax.ShapeDtypeStruct(FLAT, F32)],
+        scratch_shapes=[pltpu.VMEM(FLAT, F32), pltpu.VMEM((512, 128), F32)],
+        compiler_params=LIMIT,
+    )(*operands)
+
+
+def outer_call(*operands):
+    return pl.pallas_call(
+        outer_kernel,
+        in_specs=[whole((4096, 128)), whole(FLAT), whole((256, 128)), whole(FLAT)] + [whole(EDGE)] * 4,
+        out_specs=[HBM, whole((32, 128)), whole((32, 128))],
+        out_shape=[
+            jax.ShapeDtypeStruct((64, 8, 8, 128), BF16),
+            jax.ShapeDtypeStruct((32, 128), F32),
+            jax.ShapeDtypeStruct((32, 128), F32),
+        ],
+        scratch_shapes=[
+            pltpu.VMEM((64, 8, 8, 128), BF16),
+            pltpu.VMEM((1024, 128), F32),
+            pltpu.VMEM((1024, 128), F32),
+            pltpu.VMEM((512, 128), F32),
+            pltpu.SemaphoreType.DMA((2,)),
+        ],
+        compiler_params=LIMIT,
+    )(*operands)
+
+
+def tree_call(*operands):
+    return pl.pallas_call(
+        tree_kernel,
+        in_specs=[SMEM, whole((63, 64, 128)), whole((64, 32, 128)), whole((64, 32, 128))],
+        out_specs=HBM,
+        out_shape=jax.ShapeDtypeStruct((64, 64, 127), F32),
+        scratch_shapes=[
+            pltpu.VMEM((63, 64, 128), BF16),
+            pltpu.VMEM((128 * KEPT, 128), F32),
+            pltpu.VMEM((64, 64, 127), F32),
+            pltpu.SemaphoreType.DMA((4,)),
+        ],
+        compiler_params=LIMIT,
+    )(*operands)
 
 
 def local(states, class_map, perm_table, candidates, merge_order):
@@ -314,13 +378,13 @@
         pltpu.with_memory_space_constraint(value, pltpu.HBM)
         for value in (states, class_map, perm_table, candidates.reshape(128, 64), merge_order)
     )
-    edge_shape, side_shape, states_shape = (131, 8, 128), (5, 8, 8, 128), (2, 64, 8, 8, 128)
+    states_shape = (2, 64, 8, 8, 128)
     read_scratch = [pltpu.VMEM(CUBE, jnp.int32), pltpu.SMEM((8,), F32)]
     low, high = pl.pallas_call(
         edge_x_kernel,
         in_specs=[HBM, HBM, HBM],
-        out_specs=[whole(edge_shape), whole(edge_shape)],
-        out_shape=[jax.ShapeDtypeStruct(edge_shape, BF16), jax.ShapeDtypeStruct(edge_shape, BF16)],
+        out_specs=[whole(EDGE), whole(EDGE)],
+        out_shape=[jax.ShapeDtypeStruct(EDGE, BF16), jax.ShapeDtypeStruct(EDGE, BF16)],
         scratch_shapes=[pltpu.VMEM(states_shape, BF16)]
         + read_scratch
         + [pltpu.VMEM((129 * 64, 128), F32), pltpu.SemaphoreType.DMA((4,))],
@@ -337,13 +401,13 @@
     side, perm, near_states, cells, hits = pl.pallas_call(
         edge_y_kernel,
         in_specs=[SMEM] + [HBM] * 5,
-        out_specs=[whole(side_shape), whole(CUBE), whole(states_shape), whole((256, 128)), whole(CUBE)],
+        out_specs=[whole(SIDE), whole(CUBE), whole(states_shape), whole((256, 128)), whole(FLAT)],
         out_shape=[
-            jax.ShapeDtypeStruct(side_shape, BF16),
+            jax.ShapeDtypeStruct(SIDE, BF16),
             jax.ShapeDtypeStruct(CUBE, F32),
             jax.ShapeDtypeStruct(states_shape, BF16),
             jax.ShapeDtypeStruct((256, 128), BF16),
-            jax.ShapeDtypeStruct(CUBE, F32),
+            jax.ShapeDtypeStruct(FLAT, F32),
         ],
         scratch_shapes=[
             pltpu.VMEM(CUBE, jnp.int32),
@@ -367,7 +431,6 @@
             pltpu.VMEM(FLAT, F32),
             pltpu.VMEM((7, 8, 128), F32),
             pltpu.VMEM((128, 128), BF16),
-            pltpu.VMEM((256, 128), BF16),
         ],
         compiler_params=LIMIT,
     )(perm, near_states)
@@ -375,27 +438,8 @@
     picks = (merge_order[64:, :64, None] == numbers).astype(BF16)
     inner, picks = lax.optimization_barrier((inner, picks))
 
-    flux, mine_rows, send_rows = pl.pallas_call(
-        outer_kernel,
-        in_specs=[whole((4096, 128)), whole((256, 128)), whole(CUBE)]
-        + [whole(edge_shape)] * 2 + [whole(side_shape)] + [whole(edge_shape)] * 2 + [whole(side_shape)] * 2,
-        out_specs=[HBM, whole((32, 128)), whole((32, 128))],
-        out_shape=[
-            jax.ShapeDtypeStruct((64, 8, 8, 128), BF16),
-            jax.ShapeDtypeStruct((32, 128), F32),
-            jax.ShapeDtypeStruct((32, 128), F32),
-        ],
-        scratch_shapes=[
-            pltpu.VMEM((4096, 128), F32),
-            pltpu.VMEM((64, 8, 8, 128), BF16),
-            pltpu.VMEM((2, 8, 128), F32),
-            pltpu.VMEM((64, 256), BF16),
-            pltpu.VMEM((256, 128), BF16),
-            pltpu.VMEM((512, 128), F32),
-            pltpu.SemaphoreType.DMA((2,)),
-        ],
-        compiler_params=LIMIT,
-    )(inner, cells, hits, low, high, side, from_low, from_high, side_low, side_high)
+    within, part_rows = middle_call(inner, cells, hits, side, side_low, side_high)
+    flux, mine_rows, send_rows = outer_call(within, part_rows, cells, hits, low, high, from_low, from_high)
 
     swap = [(i, i ^ 1) for i in range(8)]
     got_rows = lax.ppermute(send_rows, "gy", swap)
@@ -407,20 +451,7 @@
     mine = lax.all_to_all(spread, ("gx", "gy"), 0, 0, axis_index_groups=peers)
     other = lax.ppermute(mine, "gy", swap)
 
-    kept = pl.pallas_call(
-        tree_kernel,
-        in_specs=[SMEM, whole((63, 64, 128)), whole((64, 32, 128)), whole((64, 32, 128))],
-        out_specs=HBM,
-        out_shape=jax.ShapeDtypeStruct((64, 64, 127), F32),
-        scratch_shapes=[
-            pltpu.VMEM((63, 64, 128), BF16),
-            pltpu.VMEM((128 * KEPT, 128), F32),
-            pltpu.VMEM((64, 64, 127), F32),
-            pltpu.VMEM((256, 128), BF16),
-            pltpu.SemaphoreType.DMA((8,)),
-        ],
-        compiler_params=LIMIT,
-    )(where, picks, mine, other)
+    kept = tree_call(where, picks, mine, other)
     return flux, jnp.transpose(kept, (2, 0, 1))
 
 

time: 57.5 us -> 47.6 us (0.83)
  Pallas kernels: 22.7 us -> 12.2 us
  blocking collectives: 17.4 us -> 18.2 us
  starting transfers between devices: 13 us -> 12.3 us
  waiting for transfers between devices: 2.39 us -> 3.06 us
    pallas_call x1, Pallas kernels: 10.4 us -> 2.3 us  [local(): pl.pallas_call(inner_kernel, in_specs=[whole(CUBE), whole(states_shape)],...]
    pallas_call x2 -> x3, Pallas kernels: 7.97 us -> 5.49 us  [the longest x1 3.39 us: tree_call(): pl.pallas_call(tree_kernel, in_specs=[SMEM, whole((63, 64, 128)), whole((...]
    all_to_all x1, blocking collectives: 17.4 us -> 18.2 us  [local(): mine = lax.all_to_all(spread, ('gx', 'gy'), 0, 0, axis_index_groups=peers)]
    ppermute x4, waiting for transfers between devices: 0.01 us -> 0.68 us  [shift(): lax.ppermute(value, axis, [(i, (i + by) % count) for i in range(count)])]
    ppermute x1, starting transfers between devices: 1.83 us -> 1.17 us  [local(): got_rows = lax.ppermute(send_rows, 'gy', swap)]
  transfers between devices with their start and end apart: 6 -> 6, of which waited for: 2 -> 3; matrix products, arithmetic and copies ran while one was open for 1% -> 2% of each run, Pallas kernels for 23% -> 12%
where the time goes in v5:
time: 47.6 us; the launch traced here: 47.4 us
  blocking collectives  18.2 us (38%)
  starting transfers between devices  12.3 us (26%)
  Pallas kernels  12.2 us (26%)
  waiting for transfers between devices  3.06 us (6%)
  other arithmetic  0.94 us (2%)
  between operations  0.71 us (1%)
    all_to_all x1, blocking collectives, local(): mine = lax.all_to_all(spread, ('gx', 'gy'), 0, 0, axis_index_groups=peers)  18.2 us
    ppermute x4, starting transfers between devices, shift(): lax.ppermute(value, axis, [(i, (i + by) % count) for i in range(count)])  9.08 us
    pallas_call x1, Pallas kernels, tree_call(): pl.pallas_call(tree_kernel, in_specs=[SMEM, whole((63, 64, 128)), whole((...  3.39 us
    pallas_call x1, Pallas kernels, local(): pl.pallas_call(edge_y_kernel, in_specs=[SMEM] + [HBM] * 5, out_specs=[who...  2.69 us
    pallas_call x1, Pallas kernels, local(): pl.pallas_call(inner_kernel, in_specs=[whole(CUBE), whole(states_shape)],...  2.3 us
    ppermute x1, starting transfers between devices, local(): other = lax.ppermute(mine, 'gy', swap)  2.04 us
    pallas_call x1, Pallas kernels, local(): pl.pallas_call(edge_x_kernel, in_specs=[HBM, HBM, HBM], out_specs=[whole(...  1.71 us
    ppermute x1, waiting for transfers between devices, local(): other = lax.ppermute(mine, 'gy', swap)  1.54 us
  transfers between devices with their start and end apart: 6, of which 3 were waited for; matrix products, arithmetic and copies ran while one was open for 2% of the time, Pallas kernels for 12%

profile of v5, /device:TPU:1, one launch (start us, length us, event | category | flops | bytes accessed | tf_op | source)
XLA Modules:
  0.0 47.4 jit_solution(8898208148413032266)
XLA Ops:
  0.6 0.0 copy-start
  0.6 1.7 %shard_map.71 = (bf16[131,8,128]{2,1,0:T(8,128)(2,1)S(1)}, bf16[131,8,128]{2,1,0:T(8,128)(2,1)S(1)}) custom-call(f32[8]{0:T(128)} %table_hbm.3, s32[8,8,128]{2,1,0:T(8,128)} %class_hbm.3, bf16[2,64,8,8,128]{4,3,2,1,0:T(8,128)(2,1)} %states_hbm.3), custom_call_target="tpu_custom_call" | custom-call | tf_op jit(solution)/shard_map/pallas_call | solution.py:383
  2.4 2.5 %collective-permute-start.2 = (bf16[131,8,128]{2,1,0:T(8,128)(2,1)S(1)}, bf16[131,8,128]{2,1,0:T(8,128)(2,1)S(1)}, u32[]{:S(2)}, u32[]{:S(2)}) collective-permute-start(bf16[131,8,128]{2,1,0:T(8,128)(2,1)S(1)} %get-tuple-element.25.high_ref), channel_id=1, source_target_pairs={{0,8},{8,16},{16,24},{24,32},{32,40},{40,48},{48,56},{56,64},{64,7... | collective-permute-start | bytes 804872 | tf_op jit(solution)/shard_map/ppermute | solution.py:396
  4.9 4.4 %collective-permute-start.3 = (bf16[131,8,128]{2,1,0:T(8,128)(2,1)S(1)}, bf16[131,8,128]{2,1,0:T(8,128)(2,1)S(1)}, u32[]{:S(2)}, u32[]{:S(2)}) collective-permute-start(bf16[131,8,128]{2,1,0:T(8,128)(2,1)S(1)} %get-tuple-element.24.low_ref), channel_id=1, source_target_pairs={{0,120},{8,0},{16,8},{24,16},{32,24},{40,32},{48,40},{56,48},{64,5... | collective-permute-start | bytes 804872 | tf_op jit(solution)/shard_map/ppermute | solution.py:396
  9.3 2.7 %shard_map.68 = (bf16[5,8,8,128]{3,2,1,0:T(8,128)(2,1)S(1)}, f32[8,8,128]{2,1,0:T(8,128)S(1)}, bf16[2,64,8,8,128]{4,3,2,1,0:T(8,128)(2,1)S(1)}, bf16[256,128]{1,0:T(8,128)(2,1)S(1)}, f32[64,128]{1,0:T(8,128)S(1)}) custom-call(s32[1]{0:T(128)} %bitcast.where_ref, f32[8]{0:T(128)} %table_hbm.3, s32[8,8,128]{2,1,0:T(8,128)} %class_hbm.3, s32[128,64]{1,0:T(8,128)} %bitcast.4, ...), custom_call_target="tpu_custom_call" | custom-call | tf_op jit(solution)/shard_map/pallas_call | solution.py:401
  12.0 2.1 %collective-permute-start = (bf16[5,8,8,128]{3,2,1,0:T(8,128)(2,1)S(1)}, bf16[5,8,8,128]{3,2,1,0:T(8,128)(2,1)S(1)}, u32[]{:S(2)}, u32[]{:S(2)}) collective-permute-start(bf16[5,8,8,128]{3,2,1,0:T(8,128)(2,1)S(1)} %get-tuple-element.21.side_ref), channel_id=1, source_target_pairs={{0,1},{1,2},{2,3},{3,4},{4,5},{5,6},{6,7},{7,0},{8,9},{9,10},{10,1... | collective-permute-start | bytes 245768 | tf_op jit(solution)/shard_map/ppermute | solution.py:396
  14.1 0.0 collective-permute-start.1
  14.1 0.0 copy-done
  14.2 0.8 %fusion.pick_ref = bf16[63,64,128]{2,1,0:T(8,128)(2,1)S(1)} fusion(s32[63,64]{1,0:T(8,128)S(1)} %slice.9), kind=kLoop, calls=%fused_computation.1 | loop fusion | flops 1032192 | bytes 1048320 | tf_op jit(solution)/shard_map/convert_element_type | solution.py:438
  15.0 2.3 %shard_map.69.inner_ref = f32[4096,128]{1,0:T(8,128)S(1)} custom-call(f32[8,8,128]{2,1,0:T(8,128)S(1)} %get-tuple-element.16.perm_ref, bf16[2,64,8,8,128]{4,3,2,1,0:T(8,128)(2,1)S(1)} %get-tuple-element.17.states_ref), custom_call_target="tpu_custom_call" | custom-call | tf_op jit(solution)/shard_map/pallas_call | solution.py:424
  17.3 0.0 collective-permute-done.side_low_ref
  17.3 0.7 %collective-permute-done.1.side_high_ref = bf16[5,8,8,128]{3,2,1,0:T(8,128)(2,1)S(1)} collective-permute-done((bf16[5,8,8,128]{3,2,1,0:T(8,128)(2,1)S(1)}, bf16[5,8,8,128]{3,2,1,0:T(8,128)(2,1)S(1)}, u32[]{:S(2)}, u32[]{:S(2)}) %collective-permute-start.1) | collective-permute-done | bytes 81952 | tf_op jit(solution)/shard_map/ppermute | solution.py:396
  18.0 0.9 %shard_map.70 = (f32[4096,128]{1,0:T(8,128)S(1)}, f32[64,128]{1,0:T(8,128)S(1)}) custom-call(f32[4096,128]{1,0:T(8,128)S(1)} %shard_map.69.inner_ref, bf16[256,128]{1,0:T(8,128)(2,1)S(1)} %get-tuple-element.19.cells_ref, f32[64,128]{1,0:T(8,128)S(1)} %get-tuple-element.20.hits_ref, bf16[5,8,8,128]{3,2,1,0:T(8,128)(2,1)S(1)} %get-tuple-element.21.side_ref, ...), custom_call_target="tpu_custom_call" | custom-call | tf_op jit(solution)/shard_map/pallas_call | solution.py:327
  18.9 0.0 collective-permute-done.2.from_low_ref
  18.9 0.0 collective-permute-done.3.from_high_ref
  18.9 1.2 %shard_map.72 = (bf16[64,8,8,128]{3,2,1,0:T(8,128)(2,1)}, f32[32,128]{1,0:T(8,128)S(1)}, f32[32,128]{1,0:T(8,128)S(1)}) custom-call(f32[4096,128]{1,0:T(8,128)S(1)} %get-tuple-element.22.within_ref, f32[64,128]{1,0:T(8,128)S(1)} %get-tuple-element.23.rows_ref, bf16[256,128]{1,0:T(8,128)(2,1)S(1)} %get-tuple-element.19.cells_ref, ...), custom_call_target="tpu_custom_call" | custom-call | tf_op jit(solution)/shard_map/pallas_call | solution.py:338
  20.1 1.2 %collective-permute-start.4 = (f32[32,128]{1,0:T(8,128)S(1)}, f32[32,128]{1,0:T(8,128)S(1)}, u32[]{:S(2)}, u32[]{:S(2)}) collective-permute-start(f32[32,128]{1,0:T(8,128)S(1)} %get-tuple-element.29), channel_id=1, source_target_pairs={{0,1},{1,0},{2,3},{3,2},{4,5},{5,4},{6,7},{7,6},{8,9},{9,8},{10,11... | collective-permute-start | bytes 49160 | tf_op jit(solution)/shard_map/ppermute | solution.py:445
  21.3 0.8 %collective-permute-done.4 = f32[32,128]{1,0:T(8,128)S(1)} collective-permute-done((f32[32,128]{1,0:T(8,128)S(1)}, f32[32,128]{1,0:T(8,128)S(1)}, u32[]{:S(2)}, u32[]{:S(2)}) %collective-permute-start.4) | collective-permute-done | bytes 16416 | tf_op jit(solution)/shard_map/ppermute | solution.py:445
  22.2 0.1 pad_maximum_fusion
  22.2 0.1 broadcast_in_dim.2
  22.3 18.2 %all_to_all.5.mine_ref = bf16[64,32,128]{2,1,0:T(8,128)(2,1)S(1)} all-to-all(bf16[64,32,128]{2,1,0:T(8,128)(2,1)S(1)} %broadcast_in_dim.2), channel_id=1, replica_groups={{0,2,4,6,8,10,12,14,16,18,20,22,24,26,28,30,32,34,36,38,40,42,44,46,48,..., dimensions={0} | all-to-all | bytes 1048576 | tf_op jit(solution)/shard_map/all_to_all | solution.py:451
  40.5 2.0 %collective-permute-start.5 = (bf16[64,32,128]{2,1,0:T(8,128)(2,1)S(1)}, bf16[64,32,128]{2,1,0:T(8,128)(2,1)S(1)}, u32[]{:S(2)}, u32[]{:S(2)}) collective-permute-start(bf16[64,32,128]{2,1,0:T(8,128)(2,1)S(1)} %all_to_all.5.mine_ref), channel_id=1, source_target_pairs={{0,1},{1,0},{2,3},{3,2},{4,5},{5,4},{6,7},{7,6},{8,9},{9,8},{10,11... | collective-permute-start | bytes 1572872 | tf_op jit(solution)/shard_map/ppermute | solution.py:452
  42.5 1.5 %collective-permute-done.5.other_ref = bf16[64,32,128]{2,1,0:T(8,128)(2,1)S(1)} collective-permute-done((bf16[64,32,128]{2,1,0:T(8,128)(2,1)S(1)}, bf16[64,32,128]{2,1,0:T(8,128)(2,1)S(1)}, u32[]{:S(2)}, u32[]{:S(2)}) %collective-permute-start.5) | collective-permute-done | bytes 524320 | tf_op jit(solution)/shard_map/ppermute | solution.py:452
  44.1 3.4 %shard_map.73 = f32[64,64,127]{2,1,0:T(8,128)} custom-call(s32[1]{0:T(128)} %bitcast.where_ref, bf16[63,64,128]{2,1,0:T(8,128)(2,1)S(1)} %fusion.pick_ref, bf16[64,32,128]{2,1,0:T(8,128)(2,1)S(1)} %all_to_all.5.mine_ref, bf16[64,32,128]{2,1,0:T(8,128)(2,1)S(1)} %collective-permute-done.5.other_ref), custom_call_target="tpu_custom_call" | custom-call | tf_op jit(solution)/shard_map/pallas_call | solution.py:359
  (2 shorter events, 0.0 us)
Async XLA Ops:
  0.6 13.5 %copy-start = (s32[127,128]{1,0:T(8,128)S(1)}, s32[127,128]{1,0:T(8,128)}, u32[]{:S(2)}) copy-start(s32[127,128]{1,0:T(8,128)} %order_hbm.1) | copy-start | bytes 195076
  2.4 16.6 %collective-permute-start.2 = (bf16[131,8,128]{2,1,0:T(8,128)(2,1)S(1)}, bf16[131,8,128]{2,1,0:T(8,128)(2,1)S(1)}, u32[]{:S(2)}, u32[]{:S(2)}) collective-permute-start(bf16[131,8,128]{2,1,0:T(8,128)(2,1)S(1)} %get-tuple-element.25.high_ref), channel_id=1, source_target_pairs={{0,8},{8,16},{16,24},{24,32},{32,40},{40,48},{48,56},{56,64},{64,7... | collective-permute-start | bytes 804872 | tf_op jit(solution)/shard_map/ppermute | solution.py:396
  4.9 14.0 %collective-permute-start.3 = (bf16[131,8,128]{2,1,0:T(8,128)(2,1)S(1)}, bf16[131,8,128]{2,1,0:T(8,128)(2,1)S(1)}, u32[]{:S(2)}, u32[]{:S(2)}) collective-permute-start(bf16[131,8,128]{2,1,0:T(8,128)(2,1)S(1)} %get-tuple-element.24.low_ref), channel_id=1, source_target_pairs={{0,120},{8,0},{16,8},{24,16},{32,24},{40,32},{48,40},{56,48},{64,5... | collective-permute-start | bytes 804872 | tf_op jit(solution)/shard_map/ppermute | solution.py:396
  12.0 5.3 %collective-permute-start = (bf16[5,8,8,128]{3,2,1,0:T(8,128)(2,1)S(1)}, bf16[5,8,8,128]{3,2,1,0:T(8,128)(2,1)S(1)}, u32[]{:S(2)}, u32[]{:S(2)}) collective-permute-start(bf16[5,8,8,128]{3,2,1,0:T(8,128)(2,1)S(1)} %get-tuple-element.21.side_ref), channel_id=1, source_target_pairs={{0,1},{1,2},{2,3},{3,4},{4,5},{5,6},{6,7},{7,0},{8,9},{9,10},{10,1... | collective-permute-start | bytes 245768 | tf_op jit(solution)/shard_map/ppermute | solution.py:396
  14.1 3.9 %collective-permute-start.1 = (bf16[5,8,8,128]{3,2,1,0:T(8,128)(2,1)S(1)}, bf16[5,8,8,128]{3,2,1,0:T(8,128)(2,1)S(1)}, u32[]{:S(2)}, u32[]{:S(2)}) collective-permute-start(bf16[5,8,8,128]{3,2,1,0:T(8,128)(2,1)S(1)} %get-tuple-element.21.side_ref), channel_id=1, source_target_pairs={{0,7},{1,0},{2,1},{3,2},{4,3},{5,4},{6,5},{7,6},{8,15},{9,8},{10,9... | collective-permute-start | bytes 245768 | tf_op jit(solution)/shard_map/ppermute | solution.py:396
  20.1 2.0 %collective-permute-start.4 = (f32[32,128]{1,0:T(8,128)S(1)}, f32[32,128]{1,0:T(8,128)S(1)}, u32[]{:S(2)}, u32[]{:S(2)}) collective-permute-start(f32[32,128]{1,0:T(8,128)S(1)} %get-tuple-element.29), channel_id=1, source_target_pairs={{0,1},{1,0},{2,3},{3,2},{4,5},{5,4},{6,7},{7,6},{8,9},{9,8},{10,11... | collective-permute-start | bytes 49160 | tf_op jit(solution)/shard_map/ppermute | solution.py:445
  40.5 3.6 %collective-permute-start.5 = (bf16[64,32,128]{2,1,0:T(8,128)(2,1)S(1)}, bf16[64,32,128]{2,1,0:T(8,128)(2,1)S(1)}, u32[]{:S(2)}, u32[]{:S(2)}) collective-permute-start(bf16[64,32,128]{2,1,0:T(8,128)(2,1)S(1)} %all_to_all.5.mine_ref), channel_id=1, source_target_pairs={{0,1},{1,0},{2,3},{3,2},{4,5},{5,4},{6,7},{7,6},{8,9},{9,8},{10,11... | collective-permute-start | bytes 1572872 | tf_op jit(solution)/shard_map/ppermute | solution.py:452

commit v6 on v5

v6 whole, which is shorter than its diff:
```python
import jax
import jax.numpy as jnp
from jax import lax
from jax.experimental import pallas as pl
from jax.experimental.pallas import tpu as pltpu
from jax.sharding import PartitionSpec as P

F32 = jnp.float32
BF16 = jnp.bfloat16
KEPT = 72
CUBE = (8, 8, 128)
FLAT = (64, 128)
EDGE = (131, 8, 128)
SIDE = (5, 8, 8, 128)
HBM = pl.BlockSpec(memory_space=pltpu.HBM)
SMEM = pl.BlockSpec(memory_space=pltpu.SMEM)
LIMIT = pltpu.CompilerParams(vmem_limit_bytes=32 * 1024 * 1024)


def whole(shape):
    return pl.BlockSpec(shape, lambda *_: (0,) * len(shape))


def lane_of(shape):
    return lax.broadcasted_iota(jnp.int32, shape, len(shape) - 1)


def turn(value, by):
    return pltpu.roll(value, by, 1)


def look_up(kind, table_ref):
    value = jnp.zeros(kind.shape, F32)
    for number in range(8):
        value = jnp.where(kind == number, table_ref[number], value)
    return value


def trans(k_here, k_next):
    return k_here * k_next / (k_here + k_next)


def face(t, m_here, m_next, p_here, p_next):
    return t * (m_here + m_next) * (p_next - p_here)


def three_pieces(value):
    high = value.astype(BF16)
    rest = value - high.astype(F32)
    middle = rest.astype(BF16)
    return high, middle, (rest - middle.astype(F32)).astype(BF16)


def two_times(weights):
    return jnp.concatenate([weights, weights], 0)


def two_pieces(value):
    high = value.astype(BF16)
    return jnp.concatenate([high, (value - high.astype(F32)).astype(BF16)], 1)


def matmul(left, right):
    return jnp.dot(left, right, preferred_element_type=F32)


def sub_of(shape):
    return lax.broadcasted_iota(jnp.int32, shape, 0)


def slots_of(order_row, cand_row, core):
    lane = lane_of(FLAT)
    order = jnp.broadcast_to(order_row, FLAT)
    swapped = jnp.where(lane < 32, turn(order, 96), turn(order, 32))
    order = jnp.where(core == 1, swapped, order)
    match = (order == core * 64 + sub_of(FLAT)) & (lane < 64)
    column = jnp.transpose(jnp.broadcast_to(cand_row.astype(F32), (64, 64)))[:, :1]
    cell = jnp.sum(jnp.where(match, jnp.broadcast_to(column, FLAT) + 1.0, 0.0), 0, keepdims=True)
    cell = cell.astype(jnp.int32) - 1
    return jnp.where(cell < 0, -1, cell % 128), jnp.where(cell < 0, -1, cell // 128)


def one_hot(shape, at):
    return jnp.where(sub_of(shape) == at, 1.0, 0.0)


def edge_x_kernel(
    where_ref, table_hbm, class_hbm, cand_hbm, order_hbm, states_hbm,
    low_ref, high_ref, to_minus_ref, to_plus_ref, own_ref, cells_ref, hits_ref,
    states_ref, class_ref, cand_ref, order_ref, table_ref, wide_ref, weights_ref, product_ref, sem,
):
    tile = where_ref[0]
    core = tile % 2
    tiles = (tile, (tile + 120) % 128, (tile + 8) % 128)
    copies = [
        pltpu.make_async_copy(table_hbm, table_ref, sem.at[0]),
        pltpu.make_async_copy(class_hbm, class_ref, sem.at[1]),
    ]
    for n, at in enumerate(tiles):
        copies.append(pltpu.make_async_copy(cand_hbm.at[pl.ds(at, 1)], cand_ref.at[n], sem.at[2 + n]))
        copies.append(pltpu.make_async_copy(order_hbm.at[pl.ds(at // 2, 1)], order_ref.at[n], sem.at[5 + n]))
    for n, rows in enumerate((pl.ds(0, 2), pl.ds(6, 2))):
        copies.append(
            pltpu.make_async_copy(states_hbm.at[:, :, :, rows], states_ref.at[:, :, :, rows], sem.at[8 + n])
        )
    for copy in copies:
        copy.start()
    for copy in copies[:8]:
        copy.wait()
    wide_ref[pl.ds(0, 64), :] = look_up(class_ref[...], table_ref).reshape(FLAT)
    for ref, at in ((low_ref, 0), (high_ref, 7)):
        for n, piece in enumerate(three_pieces(wide_ref[pl.ds(at, 8, stride=8), :])):
            ref[128 + n] = piece
    own_y, own_zx = slots_of(order_ref[0], cand_ref[0], core)
    minus_y, minus_zx = slots_of(order_ref[1], cand_ref[1], core)
    plus_y, plus_zx = slots_of(order_ref[2], cand_ref[2], core)
    square, rows_of_z = (128, 128), (8, 128)
    own_cells = one_hot(square, own_y).astype(BF16)
    cells_ref[...] = two_times(own_cells)
    hits_ref[...] = one_hot(FLAT, own_zx)
    weights_ref[0] = jnp.concatenate([one_hot(square, minus_y).astype(BF16), own_cells], 1)
    weights_ref[1] = jnp.concatenate([one_hot(square, plus_y).astype(BF16), own_cells], 1)
    own_z = sub_of(rows_of_z) * 8
    mask_low = jnp.concatenate(
        [one_hot(rows_of_z, jnp.where(minus_zx < 0, -1, minus_zx // 8)), jnp.where(own_z == own_zx, 1.0, 0.0)], 1
    )
    mask_high = jnp.concatenate(
        [one_hot(rows_of_z, jnp.where(plus_zx < 0, -1, plus_zx // 8)), jnp.where(own_z + 7 == own_zx, 1.0, 0.0)], 1
    )
    at_low = jnp.where((own_zx >= 0) & (own_zx % 8 == 0), 1.0, 0.0)
    at_high = jnp.where((own_zx >= 0) & (own_zx % 8 == 7), 1.0, 0.0)
    flag = sub_of(rows_of_z)
    flags = jnp.where(flag == 0, at_low, jnp.where(flag == 1, at_high, 0.0))
    copies[8].wait()
    copies[9].wait()
    for snap in range(64):
        for field in range(2):
            slot = (1 + field + 2 * snap) * 64
            wide_ref[pl.ds(slot, 64), :] = states_ref[field, snap].astype(F32).reshape(FLAT)
            low_ref[field * 64 + snap] = wide_ref[pl.ds(slot, 8, stride=8), :].astype(BF16)
            high_ref[field * 64 + snap] = wide_ref[pl.ds(slot + 7, 8, stride=8), :].astype(BF16)

    def select(ref, weights, mask):
        for first, count in [(16 * n, 16) for n in range(8)] + [(128, 3)]:
            rows = matmul(ref[pl.ds(first, count)].reshape(count * 8, 128), weights)
            for n in range(count):
                product = rows[n * 8 : n * 8 + 8] * mask
                for half in range(2):
                    product_ref[half, pl.ds((first + n) * 8, 8), :] = product[:, half * 128 : half * 128 + 128]
        halves = []
        for half in range(2):
            product_ref[half, pl.ds(131 * 8, 40), :] = jnp.zeros((40, 128), F32)
            total = product_ref[half, pl.ds(0, 136, stride=8), :]
            for z in range(1, 8):
                total = total + product_ref[half, pl.ds(z, 136, stride=8), :]
            halves.append(total)
        return halves

    def pack(rows):
        return jnp.concatenate([rows[:64] + turn(rows[64:128], 64), rows[128:136]], 0).astype(BF16)

    to_minus, own_low = select(low_ref, weights_ref[0], mask_low)
    to_plus, own_high = select(high_ref, weights_ref[1], mask_high)
    to_minus_ref[...] = pack(to_minus)
    to_plus_ref[...] = pack(to_plus)
    own_ref[pl.ds(0, 136), :] = own_low + own_high
    own_ref[pl.ds(136, 8), :] = flags


def edge_y_kernel(table_hbm, class_hbm, states_hbm, side_ref, perm_ref, states_ref, class_ref, table_ref, sem):
    copies = [
        pltpu.make_async_copy(table_hbm, table_ref, sem.at[0]),
        pltpu.make_async_copy(class_hbm, class_ref, sem.at[1]),
    ]
    for n in range(2):
        half = pl.ds(32 * n, 32)
        copies.append(pltpu.make_async_copy(states_hbm.at[:, half], states_ref.at[:, half], sem.at[2 + n]))
    for copy in copies:
        copy.start()
    copies[0].wait()
    copies[1].wait()
    perm = look_up(class_ref[...], table_ref)
    perm_ref[...] = perm
    first = jnp.broadcast_to(perm[:, :, 0:1], CUBE)
    last = jnp.broadcast_to(perm[:, :, 127:128], CUBE)
    for n, piece in enumerate(three_pieces(jnp.where(lane_of(CUBE) % 2 == 0, first, last))):
        side_ref[2 + n] = piece
    lane = lane_of(FLAT)
    acc = [jnp.zeros(FLAT, F32), jnp.zeros(FLAT, F32)]
    for snap in range(64):
        if snap % 32 == 0:
            copies[2 + snap // 32].wait()
        keep = (lane == 2 * snap) | (lane == (2 * snap + 127) % 128)
        for field in range(2):
            value = states_ref[field, snap].astype(F32).reshape(FLAT)
            acc[field] = jnp.where(keep, turn(value, 2 * snap), acc[field])
    for field in range(2):
        side_ref[field] = acc[field].reshape(CUBE).astype(BF16)


def set_up_faces(perm, tx_ref, ty_ref, tz_ref, shift_ref):
    row = lax.broadcasted_iota(jnp.int32, CUBE, 1)
    next_y = turn(perm.reshape(FLAT), 127).reshape(CUBE)
    tx_ref[...] = jnp.where(row == 7, 0.0, trans(perm, jnp.roll(perm, -1, 1)))
    ty_ref[...] = jnp.where(lane_of(CUBE) == 127, 0.0, trans(perm, next_y)).reshape(FLAT)
    tz_ref[...] = trans(perm[:-1], perm[1:])
    square = (128, 128)
    shift_ref[...] = jnp.where(sub_of(square) == lane_of(square) + 1, 1.0, 0.0).astype(BF16)


def flux_within(states_ref, snap, tx_ref, ty_ref, tz_ref, shift_ref):
    p = states_ref[0, snap].astype(F32)
    s = states_ref[1, snap].astype(F32)
    m = s * s
    fx = face(tx_ref[...], m, jnp.roll(m, -1, 1), p, jnp.roll(p, -1, 1))
    total = fx - jnp.roll(fx, 1, 1)
    p_next = matmul(states_ref[0, snap].reshape(FLAT), shift_ref[...])
    s_next = matmul(states_ref[1, snap].reshape(FLAT), shift_ref[...])
    fy = face(ty_ref[...], m.reshape(FLAT), s_next * s_next, p.reshape(FLAT), p_next)
    total = total + (fy - turn(fy, 1)).reshape(CUBE)
    fz = face(tz_ref[...], m[:-1], m[1:], p[:-1], p[1:])
    zero = jnp.zeros((1, 8, 128), F32)
    total = total + (jnp.concatenate([fz, zero], 0) - jnp.concatenate([zero, fz], 0))
    return total.reshape(FLAT)


def inner_kernel(perm_ref, states_ref, out_ref, tx_ref, ty_ref, tz_ref, shift_ref):
    faces = (tx_ref, ty_ref, tz_ref, shift_ref)
    set_up_faces(perm_ref[...], *faces)

    def group(number, carry):
        for k in range(16):
            snap = number * 16 + k
            span = pl.ds(pl.multiple_of(snap * 64, 64), 64)
            out_ref[span, :] = flux_within(states_ref, snap, *faces)
        return carry

    lax.fori_loop(0, 4, group, 0)


def sum_of_eights(picked_ref):
    total = picked_ref[pl.ds(0, 64, stride=8), :]
    for at in range(1, 8):
        total = total + picked_ref[pl.ds(at, 64, stride=8), :]
    return total


def perm_of(ref, at):
    high, middle, low = (ref[at + n].astype(F32) for n in range(3))
    return (high + middle) + low


def flux_across_y(side_ref, side_low_ref, side_high_ref):
    lane = lane_of(FLAT)

    def beyond(below, above):
        below, above = below.reshape(FLAT), above.reshape(FLAT)
        return jnp.where(lane % 2 == 0, turn(below, 1), turn(above, 127))

    t_side = trans(
        perm_of(side_ref, 2).reshape(FLAT), beyond(perm_of(side_low_ref, 2), perm_of(side_high_ref, 2))
    )

    def side_pair(which):
        here = side_ref[which].astype(F32).reshape(FLAT)
        return here, beyond(side_low_ref[which].astype(F32), side_high_ref[which].astype(F32))

    p_here, p_next = side_pair(0)
    s_here, s_next = side_pair(1)
    return face(t_side, s_here * s_here, s_next * s_next, p_here, p_next)


def sides_of(qy_ref, snap):
    lane = lane_of(FLAT)
    turned = turn(qy_ref[...], (128 - 2 * snap) % 128)
    return jnp.where((lane == 0) | (lane == 127), turned, 0.0)


def middle_kernel(
    inner_ref, cells_ref, hits_ref, side_ref, side_low_ref, side_high_ref, own_ref, from_minus_ref, from_plus_ref,
    mine_ref, send_ref, qy_ref, picked_ref,
):
    qy_ref[...] = flux_across_y(side_ref, side_low_ref, side_high_ref)
    for snap in range(64):
        flux = inner_ref[pl.ds(snap * 64, 64), :] + sides_of(qy_ref, snap)
        rows = matmul(two_pieces(flux), cells_ref[...]) * hits_ref[...]
        picked_ref[pl.ds(snap * 8, 8), :] = jnp.sum(rows.reshape(CUBE), 0)
    at_low, at_high = own_ref[pl.ds(136, 1), :], own_ref[pl.ds(137, 1), :]
    beside = from_minus_ref[...].astype(F32) * at_low + from_plus_ref[...].astype(F32) * at_high
    sat = from_minus_ref[:64].astype(F32) * turn(at_low, 64) + from_plus_ref[:64].astype(F32) * turn(at_high, 64)
    m_next, p_next = turn(sat, 64), beside[:64]
    p_own, m_own = own_ref[pl.ds(0, 64), :], own_ref[pl.ds(64, 64), :]
    k_next = (beside[64:65] + beside[65:66]) + beside[66:67]
    k_own = (own_ref[pl.ds(128, 1), :] + own_ref[pl.ds(129, 1), :]) + own_ref[pl.ds(130, 1), :]
    k_sum = jnp.where(at_low + at_high > 0.0, k_own + k_next, 1.0)
    q_x = face(k_own * k_next / k_sum, m_own * m_own, m_next * m_next, p_own, p_next)
    total = sum_of_eights(picked_ref) + q_x
    rows = jnp.transpose(jnp.concatenate([total, jnp.zeros(FLAT, F32)], 0))
    mine_ref[...] = rows[:32]
    send_ref[...] = rows[32:64]


def near_kernel(
    perm_ref, side_ref, side_low_ref, side_high_ref, states_hbm, out_ref,
    states_ref, tx_ref, ty_ref, tz_ref, shift_ref, qy_ref, sem,
):
    copies = []
    for n in range(2):
        half = pl.ds(32 * n, 32)
        copies.append(pltpu.make_async_copy(states_hbm.at[:, half], states_ref.at[:, half], sem.at[n]))
        copies[n].start()
    faces = (tx_ref, ty_ref, tz_ref, shift_ref)
    set_up_faces(perm_ref[...], *faces)
    qy_ref[...] = flux_across_y(side_ref, side_low_ref, side_high_ref)

    def group(number, carry):
        for k in range(16):
            snap = number * 16 + k
            span = pl.ds(pl.multiple_of(snap * 64, 64), 64)
            out_ref[span, :] = flux_within(states_ref, snap, *faces) + sides_of(qy_ref, snap)
        return carry

    for n in range(2):
        copies[n].wait()
        lax.fori_loop(2 * n, 2 * n + 2, group, 0)


def outer_kernel(within_ref, low_ref, high_ref, from_low_ref, from_high_ref, out_hbm, out_ref, edge_ref, sem):
    t_low = trans(perm_of(low_ref, 128), perm_of(from_low_ref, 128))
    t_high = trans(perm_of(high_ref, 128), perm_of(from_high_ref, 128))
    edge_ref[...] = jnp.zeros_like(edge_ref)

    def edge(own_ref, other_ref, t, snap):
        s_here, s_next = own_ref[64 + snap].astype(F32), other_ref[64 + snap].astype(F32)
        p_here, p_next = own_ref[snap].astype(F32), other_ref[snap].astype(F32)
        return face(t, s_here * s_here, s_next * s_next, p_here, p_next)

    def put(part):
        span = pl.ds(part * 32, 32)
        return pltpu.make_async_copy(out_ref.at[span], out_hbm.at[span], sem.at[part])

    def group(number, carry):
        for k in range(16):
            snap = number * 16 + k
            edge_ref[pl.ds(k * 64, 8, stride=8), :] = edge(low_ref, from_low_ref, t_low, snap)
            edge_ref[pl.ds(k * 64 + 7, 8, stride=8), :] = edge(high_ref, from_high_ref, t_high, snap)
        for k in range(16):
            snap = number * 16 + k
            flux = within_ref[pl.ds(pl.multiple_of(snap * 64, 64), 64), :] + edge_ref[pl.ds(k * 64, 64), :]
            out_ref[snap] = flux.reshape(CUBE).astype(BF16)
        return carry

    for part in range(2):
        lax.fori_loop(2 * part, 2 * part + 2, group, 0)
        put(part).start()
    for part in range(2):
        put(part).wait()


def tree_kernel(where_ref, pick_ref, mine_ref, other_ref, out_hbm, level_ref, kept_ref, out_ref, sem):
    def select(node, stack):
        got = matmul(pick_ref[node - 64], stack)
        kept_ref[pl.ds(node * KEPT, 64), :] = got
        level_ref[node - 64] = got.astype(BF16)

    def first_levels(low_ref, high_ref):
        for j in range(32):
            pair = [low_ref[2 * j], high_ref[2 * j], low_ref[2 * j + 1], high_ref[2 * j + 1]]
            select(64 + j, jnp.concatenate(pair, 0))
        for chip in range(64):
            kept_ref[pl.ds(chip * KEPT, 32), :] = low_ref[chip].astype(F32)
            kept_ref[pl.ds(chip * KEPT + 32, 32), :] = high_ref[chip].astype(F32)

    @pl.when(where_ref[0] % 2 == 0)
    def _():
        first_levels(mine_ref, other_ref)

    @pl.when(where_ref[0] % 2 == 1)
    def _():
        first_levels(other_ref, mine_ref)

    before, offset, count = 64, 96, 16
    while count >= 1:
        for j in range(count):
            select(offset + j, level_ref[pl.ds(before + 2 * j - 64, 2)].reshape(128, 128))
        before, offset, count = offset, offset + count, count // 2

    def put(at):
        span = pl.ds(at, 16)
        return pltpu.make_async_copy(out_ref.at[span], out_hbm.at[span], sem.at[at // 16])

    for slot in range(64):
        turned = jnp.transpose(kept_ref[pl.ds(slot, 128, stride=KEPT), :])
        out_ref[slot] = (turned[:64] + turned[64:])[:, :127]
        if slot % 16 == 15:
            put(slot - 15).start()
    for at in range(0, 64, 16):
        put(at).wait()


ROWS = jax.ShapeDtypeStruct((32, 128), F32)
SLOTS = (72, 128)
OWN = (144, 128)


def edge_x_call(*operands):
    edge, slots = jax.ShapeDtypeStruct(EDGE, BF16), jax.ShapeDtypeStruct(SLOTS, BF16)
    shapes = [
        edge, edge, slots, slots, jax.ShapeDtypeStruct(OWN, F32),
        jax.ShapeDtypeStruct((256, 128), BF16), jax.ShapeDtypeStruct(FLAT, F32),
    ]
    return pl.pallas_call(
        edge_x_kernel,
        in_specs=[SMEM] + [HBM] * 5,
        out_specs=[whole(one.shape) for one in shapes],
        out_shape=shapes,
        scratch_shapes=[
            pltpu.VMEM((2, 64, 8, 8, 128), BF16),
            pltpu.VMEM(CUBE, jnp.int32),
            pltpu.VMEM((3, 1, 64), jnp.int32),
            pltpu.VMEM((3, 1, 128), jnp.int32),
            pltpu.SMEM((8,), F32),
            pltpu.VMEM((129 * 64, 128), F32),
            pltpu.VMEM((2, 128, 256), BF16),
            pltpu.VMEM((2, 136 * 8, 128), F32),
            pltpu.SemaphoreType.DMA((10,)),
        ],
        compiler_params=LIMIT,
    )(*operands)


def middle_call(*operands):
    return pl.pallas_call(
        middle_kernel,
        in_specs=[whole((4096, 128)), whole((256, 128)), whole(FLAT)]
        + [whole(SIDE)] * 3 + [whole(OWN), whole(SLOTS), whole(SLOTS)],
        out_specs=[whole((32, 128)), whole((32, 128))],
        out_shape=[ROWS, ROWS],
        scratch_shapes=[pltpu.VMEM(FLAT, F32), pltpu.VMEM((512, 128), F32)],
        compiler_params=LIMIT,
    )(*operands)


FACES = [
    pltpu.VMEM(CUBE, F32), pltpu.VMEM(FLAT, F32), pltpu.VMEM((7, 8, 128), F32), pltpu.VMEM((128, 128), BF16)
]


def near_call(*operands):
    return pl.pallas_call(
        near_kernel,
        in_specs=[whole(CUBE)] + [whole(SIDE)] * 3 + [HBM],
        out_specs=whole((4096, 128)),
        out_shape=jax.ShapeDtypeStruct((4096, 128), F32),
        scratch_shapes=[pltpu.VMEM((2, 64, 8, 8, 128), BF16)]
        + FACES
        + [pltpu.VMEM(FLAT, F32), pltpu.SemaphoreType.DMA((2,))],
        compiler_params=LIMIT,
    )(*operands)


def outer_call(*operands):
    return pl.pallas_call(
        outer_kernel,
        in_specs=[whole((4096, 128))] + [whole(EDGE)] * 4,
        out_specs=HBM,
        out_shape=jax.ShapeDtypeStruct((64, 8, 8, 128), BF16),
        scratch_shapes=[
            pltpu.VMEM((64, 8, 8, 128), BF16),
            pltpu.VMEM((1024, 128), F32),
            pltpu.SemaphoreType.DMA((2,)),
        ],
        compiler_params=LIMIT,
    )(*operands)


def tree_call(*operands):
    return pl.pallas_call(
        tree_kernel,
        in_specs=[SMEM, whole((63, 64, 128)), whole((64, 32, 128)), whole((64, 32, 128))],
        out_specs=HBM,
        out_shape=jax.ShapeDtypeStruct((64, 64, 127), F32),
        scratch_shapes=[
            pltpu.VMEM((63, 64, 128), BF16),
            pltpu.VMEM((128 * KEPT, 128), F32),
            pltpu.VMEM((64, 64, 127), F32),
            pltpu.SemaphoreType.DMA((4,)),
        ],
        compiler_params=LIMIT,
    )(*operands)


def local(states, class_map, perm_table, candidates, merge_order):
    tile = lax.axis_index("gx") * lax.axis_size("gy") + lax.axis_index("gy")
    where = tile.reshape(1).astype(jnp.int32)
    states, class_map, perm_table, candidates, merge_rows = (
        pltpu.with_memory_space_constraint(value, pltpu.HBM)
        for value in (states, class_map, perm_table, candidates.reshape(128, 64), merge_order)
    )
    states_shape = (2, 64, 8, 8, 128)
    low, high, to_minus, to_plus, own, cells, hits = edge_x_call(
        where, perm_table, class_map, candidates, merge_rows, states
    )

    def shift(value, axis, by):
        count = lax.axis_size(axis)
        return lax.ppermute(value, axis, [(i, (i + by) % count) for i in range(count)])

    from_minus = shift(to_plus, "gx", 1)
    from_plus = shift(to_minus, "gx", -1)

    side, perm, near_states = pl.pallas_call(
        edge_y_kernel,
        in_specs=[HBM, HBM, HBM],
        out_specs=[whole(SIDE), whole(CUBE), whole(states_shape)],
        out_shape=[
            jax.ShapeDtypeStruct(SIDE, BF16),
            jax.ShapeDtypeStruct(CUBE, F32),
            jax.ShapeDtypeStruct(states_shape, BF16),
        ],
        scratch_shapes=[pltpu.VMEM(CUBE, jnp.int32), pltpu.SMEM((8,), F32), pltpu.SemaphoreType.DMA((4,))],
        compiler_params=LIMIT,
    )(perm_table, class_map, states)
    side_low = shift(side, "gy", 1)
    side_high = shift(side, "gy", -1)

    inner = pl.pallas_call(
        inner_kernel,
        in_specs=[whole(CUBE), whole(states_shape)],
        out_specs=whole((4096, 128)),
        out_shape=jax.ShapeDtypeStruct((4096, 128), F32),
        scratch_shapes=FACES,
        compiler_params=LIMIT,
    )(perm, near_states)
    mine_rows, send_rows = middle_call(
        inner, cells, hits, side, side_low, side_high, own, from_minus, from_plus
    )

    swap = [(i, i ^ 1) for i in range(8)]
    got_rows = lax.ppermute(send_rows, "gy", swap)
    merged = mine_rows[:, :64] + got_rows[:, :64]
    top = merged.astype(BF16)
    rest = (merged - lax.reduce_precision(merged, 8, 7)).astype(BF16)
    spread = jnp.broadcast_to(jnp.concatenate([top, rest], 1)[None], (64, 32, 128))
    peers = [[i * 8 + j * 2 + c for i in range(16) for j in range(4)] for c in range(2)]
    spread, low, high, perm = lax.optimization_barrier((spread, low, high, perm))
    mine = lax.all_to_all(spread, ("gx", "gy"), 0, 0, axis_index_groups=peers)

    from_low = shift(high, "gx", 1)
    from_high = shift(low, "gx", -1)
    within = near_call(perm, side, side_low, side_high, states)
    flux = outer_call(within, low, high, from_low, from_high)
    numbers = lax.broadcasted_iota(jnp.int32, (63, 64, 128), 2)
    picks = (merge_order[64:, :64, None] == numbers).astype(BF16)
    mine, flux, picks = lax.optimization_barrier((mine, flux, picks))
    other = lax.ppermute(mine, "gy", swap)
    kept = tree_call(where, picks, mine, other)
    return flux, jnp.transpose(kept, (2, 0, 1))


def solution(mesh):
    in_specs = (P(None, None, None, "gx", "gy"), P(None, "gx", "gy"), P(), P(), P())
    out_specs = (P(None, None, "gx", "gy"), P())
    return jax.shard_map(local, mesh=mesh, in_specs=in_specs, out_specs=out_specs, check_vma=False)
```

time: 47.6 us -> 53.8 us (1.13)
  blocking collectives: 18.2 us -> 0 us
  starting transfers between devices: 12.3 us -> 25.1 us
  waiting for transfers between devices: 3.06 us -> 10.2 us
  Pallas kernels: 12.2 us -> 15.8 us
  local copies, waits for them, and re-layouts: 0.08 us -> 0.87 us
    all_to_all x1 -> x0, blocking collectives: 18.2 us -> none  [local(): mine = lax.all_to_all(spread, ('gx', 'gy'), 0, 0, axis_index_groups=peers)]
    all_to_all x0 -> x1, starting transfers between devices: none -> 8.22 us  [local(): mine = lax.all_to_all(spread, ('gx', 'gy'), 0, 0, axis_index_groups=peers)]
    ppermute x4 -> x6, waiting for transfers between devices: 0.68 us -> 7.77 us  [shift(): lax.ppermute(value, axis, [(i, (i + by) % count) for i in range(count)])]
    ppermute x4 -> x6, starting transfers between devices: 9.08 us -> 13.7 us  [shift(): lax.ppermute(value, axis, [(i, (i + by) % count) for i in range(count)])]
    pallas_call x3 -> x4, Pallas kernels: 5.6 us -> 9.23 us  [the longest x1 3.61 us: near_call(): pl.pallas_call(near_kernel, in_specs=[whole(CUBE)] + [whole(SIDE)] * 3 +...]
    ppermute x1, starting transfers between devices: 2.04 us -> 1.08 us  [local(): other = lax.ppermute(mine, 'gy', swap)]
    ppermute x1, starting transfers between devices: 1.17 us -> 2.09 us  [local(): got_rows = lax.ppermute(send_rows, 'gy', swap)]
    broadcast_in_dim x1, local copies, waits for them, and re-layouts: 0.07 us -> 0.87 us  [local(): jnp.broadcast_to(jnp.concatenate([top, rest], 1)[None], (64, 32, 128))]
  transfers between devices with their start and end apart: 6 -> 9, of which waited for: 3 -> 3; matrix products, arithmetic and copies ran while one was open for 2% -> 2% of each run, Pallas kernels for 12% -> 18%
where the time goes in v6:
time: 53.8 us; the launch traced here: 53.6 us
  starting transfers between devices  25.1 us (47%)
  Pallas kernels  15.8 us (29%)
  waiting for transfers between devices  10.2 us (19%)
  other arithmetic  0.92 us (2%)
  local copies, waits for them, and re-layouts  0.87 us (2%)
  between operations  0.74 us (1%)
    ppermute x6, starting transfers between devices, shift(): lax.ppermute(value, axis, [(i, (i + by) % count) for i in range(count)])  13.7 us
    all_to_all x1, starting transfers between devices, local(): mine = lax.all_to_all(spread, ('gx', 'gy'), 0, 0, axis_index_groups=peers)  8.22 us
    ppermute x6, waiting for transfers between devices, shift(): lax.ppermute(value, axis, [(i, (i + by) % count) for i in range(count)])  7.77 us
    pallas_call x1, Pallas kernels, near_call(): pl.pallas_call(near_kernel, in_specs=[whole(CUBE)] + [whole(SIDE)] * 3 +...  3.61 us
    pallas_call x1, Pallas kernels, tree_call(): pl.pallas_call(tree_kernel, in_specs=[SMEM, whole((63, 64, 128)), whole((...  3.39 us
    pallas_call x1, Pallas kernels, edge_x_call(): pl.pallas_call(edge_x_kernel, in_specs=[SMEM] + [HBM] * 5, out_specs=[who...  2.47 us
    pallas_call x1, Pallas kernels, local(): pl.pallas_call(inner_kernel, in_specs=[whole(CUBE), whole(states_shape)],...  2.24 us
    ppermute x1, starting transfers between devices, local(): got_rows = lax.ppermute(send_rows, 'gy', swap)  2.09 us
  transfers between devices with their start and end apart: 9, of which 3 were waited for; matrix products, arithmetic and copies ran while one was open for 2% of the time, Pallas kernels for 18%

profile of v6, /device:TPU:1, one launch (start us, length us, event | category | flops | bytes accessed | tf_op | source)
XLA Modules:
  0.0 53.6 jit_solution(2668041037095150125)
XLA Ops:
  0.6 2.0 %shard_map.68 = (bf16[5,8,8,128]{3,2,1,0:T(8,128)(2,1)S(1)}, f32[8,8,128]{2,1,0:T(8,128)S(1)}, bf16[2,64,8,8,128]{4,3,2,1,0:T(8,128)(2,1)S(1)}) custom-call(f32[8]{0:T(128)} %table_hbm.3, s32[8,8,128]{2,1,0:T(8,128)} %class_hbm.3, bf16[2,64,8,8,128]{4,3,2,1,0:T(8,128)(2,1)} %states_hbm.5), custom_call_target="tpu_custom_call" | custom-call | tf_op jit(solution)/shard_map/pallas_call | solution.py:512
  2.6 2.7 %collective-permute-start = (bf16[5,8,8,128]{3,2,1,0:T(8,128)(2,1)S(1)}, bf16[5,8,8,128]{3,2,1,0:T(8,128)(2,1)S(1)}, u32[]{:S(2)}, u32[]{:S(2)}) collective-permute-start(bf16[5,8,8,128]{3,2,1,0:T(8,128)(2,1)S(1)} %get-tuple-element.25.side_ref), channel_id=1, source_target_pairs={{0,1},{1,2},{2,3},{3,4},{4,5},{5,6},{6,7},{7,0},{8,9},{9,10},{10,1... | collective-permute-start | bytes 245768 | tf_op jit(solution)/shard_map/ppermute | solution.py:507
  5.3 0.0 collective-permute-start.1
  5.3 2.5 %shard_map.70 = (bf16[131,8,128]{2,1,0:T(8,128)(2,1)S(1)}, bf16[131,8,128]{2,1,0:T(8,128)(2,1)S(1)}, bf16[72,128]{1,0:T(8,128)(2,1)S(1)}, bf16[72,128]{1,0:T(8,1...) custom-call(s32[1]{0:T(128)} %bitcast.where_ref, f32[8]{0:T(128)} %table_hbm.3, ...), custom_call_target="tpu_custom_call" | custom-call | tf_op jit(solution)/shard_map/pallas_call | solution.py:412
  7.8 1.7 %collective-permute-start.2 = (bf16[72,128]{1,0:T(8,128)(2,1)S(1)}, bf16[72,128]{1,0:T(8,128)(2,1)S(1)}, u32[]{:S(2)}, u32[]{:S(2)}) collective-permute-start(bf16[72,128]{1,0:T(8,128)(2,1)S(1)} %get-tuple-element.27), channel_id=1, source_target_pairs={{0,8},{8,16},{16,24},{24,32},{32,40},{40,48},{48,56},{56,64},{64,7... | collective-permute-start | bytes 55304 | tf_op jit(solution)/shard_map/ppermute | solution.py:507
  9.5 4.4 %collective-permute-start.3 = (bf16[72,128]{1,0:T(8,128)(2,1)S(1)}, bf16[72,128]{1,0:T(8,128)(2,1)S(1)}, u32[]{:S(2)}, u32[]{:S(2)}) collective-permute-start(bf16[72,128]{1,0:T(8,128)(2,1)S(1)} %get-tuple-element.28), channel_id=1, source_target_pairs={{0,120},{8,0},{16,8},{24,16},{32,24},{40,32},{48,40},{56,48},{64,5... | collective-permute-start | bytes 55304 | tf_op jit(solution)/shard_map/ppermute | solution.py:507
  13.9 2.2 %shard_map.69.inner_ref = f32[4096,128]{1,0:T(8,128)S(1)} custom-call(f32[8,8,128]{2,1,0:T(8,128)S(1)} %get-tuple-element.34.perm_ref, bf16[2,64,8,8,128]{4,3,2,1,0:T(8,128)(2,1)S(1)} %get-tuple-element.22.states_ref), custom_call_target="tpu_custom_call" | custom-call | tf_op jit(solution)/shard_map/pallas_call | solution.py:527
  16.1 0.0 collective-permute-done.2.from_minus_ref
  16.1 0.0 collective-permute-done.3.from_plus_ref
  16.1 0.0 collective-permute-done.side_low_ref
  16.2 0.0 collective-permute-done.1.side_high_ref
  16.2 0.0 copy-start
  16.2 1.0 %shard_map.71 = (f32[32,128]{1,0:T(8,128)S(1)}, f32[32,128]{1,0:T(8,128)S(1)}) custom-call(f32[4096,128]{1,0:T(8,128)S(1)} %shard_map.69.inner_ref, bf16[256,128]{1,0:T(8,128)(2,1)S(1)} %get-tuple-element.23.cells_ref, f32[64,128]{1,0:T(8,128)S(1)} %get-tuple-element.24.hits_ref, bf16[5,8,8,128]{3,2,1,0:T(8,128)(2,1)S(1)} %get-tuple-element.25.side_ref, ...), custom_call_target="tpu_custom_call" | custom-call | tf_op jit(solution)/shard_map/pallas_call | solution.py:433
  17.1 2.1 %collective-permute-start.4 = (f32[32,128]{1,0:T(8,128)S(1)}, f32[32,128]{1,0:T(8,128)S(1)}, u32[]{:S(2)}, u32[]{:S(2)}) collective-permute-start(f32[32,128]{1,0:T(8,128)S(1)} %get-tuple-element.30), channel_id=1, source_target_pairs={{0,1},{1,0},{2,3},{3,2},{4,5},{5,4},{6,7},{7,6},{8,9},{9,8},{10,11... | collective-permute-start | bytes 49160 | tf_op jit(solution)/shard_map/ppermute | solution.py:540
  19.2 0.8 %collective-permute-done.4 = f32[32,128]{1,0:T(8,128)S(1)} collective-permute-done((f32[32,128]{1,0:T(8,128)S(1)}, f32[32,128]{1,0:T(8,128)S(1)}, u32[]{:S(2)}, u32[]{:S(2)}) %collective-permute-start.4) | collective-permute-done | bytes 16416 | tf_op jit(solution)/shard_map/ppermute | solution.py:540
  20.1 0.1 pad_maximum_fusion
  20.2 0.9 %broadcast_in_dim.2 = bf16[64,32,128]{2,1,0:T(8,128)(2,1)} broadcast(bf16[32,128]{1,0:T(8,128)(2,1)S(1)} %pad_maximum_fusion), dimensions={1,2} | broadcast | bytes 532480 | tf_op jit(solution)/shard_map/broadcast_in_dim | solution.py:544
  21.0 8.2 %all-to-all-start = ((bf16[64,32,128]{2,1,0:T(8,128)(2,1)}), bf16[64,32,128]{2,1,0:T(8,128)(2,1)S(1)}, u32[]{:S(2)}, u32[]{:S(2)}) async-start(bf16[64,32,128]{2,1,0:T(8,128)(2,1)} %broadcast_in_dim.2), calls=%async_computation | async-start | bytes 1048576 | tf_op jit(solution)/shard_map/all_to_all | solution.py:547
  29.3 1.1 %collective-permute-start.5 = (bf16[131,8,128]{2,1,0:T(8,128)(2,1)S(1)}, bf16[131,8,128]{2,1,0:T(8,128)(2,1)S(1)}, u32[]{:S(2)}, u32[]{:S(2)}) collective-permute-start(bf16[131,8,128]{2,1,0:T(8,128)(2,1)S(1)} %get-tuple-element.36.high_ref), channel_id=1, source_target_pairs={{0,8},{8,16},{16,24},{24,32},{32,40},{40,48},{48,56},{56,64},{64,7... | collective-permute-start | bytes 804872 | tf_op jit(solution)/shard_map/ppermute | solution.py:507
  30.4 3.8 %collective-permute-start.6 = (bf16[131,8,128]{2,1,0:T(8,128)(2,1)S(1)}, bf16[131,8,128]{2,1,0:T(8,128)(2,1)S(1)}, u32[]{:S(2)}, u32[]{:S(2)}) collective-permute-start(bf16[131,8,128]{2,1,0:T(8,128)(2,1)S(1)} %get-tuple-element.35.low_ref), channel_id=1, source_target_pairs={{0,120},{8,0},{16,8},{24,16},{32,24},{40,32},{48,40},{56,48},{64,5... | collective-permute-start | bytes 804872 | tf_op jit(solution)/shard_map/ppermute | solution.py:507
  34.1 0.0 copy-done
  34.1 0.8 %fusion.pick_ref = bf16[63,64,128]{2,1,0:T(8,128)(2,1)S(1)} fusion(s32[63,64]{1,0:T(8,128)S(1)} %slice.11), kind=kLoop, calls=%fused_computation.1 | loop fusion | flops 1032192 | bytes 1048320 | tf_op jit(solution)/shard_map/convert_element_type | solution.py:554
  35.0 3.6 %shard_map.72.within_ref = f32[4096,128]{1,0:T(8,128)S(1)} custom-call(f32[8,8,128]{2,1,0:T(8,128)S(1)} %get-tuple-element.34.perm_ref, bf16[5,8,8,128]{3,2,1,0:T(8,128)(2,1)S(1)} %get-tuple-element.25.side_ref, bf16[5,8,8,128]{3,2,1,0:T(8,128)(2,1)S(1)} %collective-permute-done.side_low_ref, ...), custom_call_target="tpu_custom_call" | custom-call | tf_op jit(solution)/shard_map/pallas_call | solution.py:450
  38.6 7.8 %collective-permute-done.5.from_low_ref = bf16[131,8,128]{2,1,0:T(8,128)(2,1)S(1)} collective-permute-done((bf16[131,8,128]{2,1,0:T(8,128)(2,1)S(1)}, bf16[131,8,128]{2,1,0:T(8,128)(2,1)S(1)}, u32[]{:S(2)}, u32[]{:S(2)}) %collective-permute-start.5) | collective-permute-done | bytes 268320 | tf_op jit(solution)/shard_map/ppermute | solution.py:507
  46.3 0.0 collective-permute-done.6.from_high_ref
  46.3 1.2 %shard_map.73 = bf16[64,8,8,128]{3,2,1,0:T(8,128)(2,1)} custom-call(f32[4096,128]{1,0:T(8,128)S(1)} %shard_map.72.within_ref, bf16[131,8,128]{2,1,0:T(8,128)(2,1)S(1)} %get-tuple-element.35.low_ref, bf16[131,8,128]{2,1,0:T(8,128)(2,1)S(1)} %get-tuple-element.36.high_ref, bf16[131,8,128]{2,1,0:T(8,128)(2,1)S(1)} %collective-permute-done.5.from_low_ref, ...), custom_call_target="tpu_custom_call" | custom-call | tf_op jit(solution)/shard_map/pallas_call | solution.py:463
  47.5 0.0 all-to-all-done.mine_ref
  47.6 1.1 %collective-permute-start.7 = (bf16[64,32,128]{2,1,0:T(8,128)(2,1)S(1)}, bf16[64,32,128]{2,1,0:T(8,128)(2,1)S(1)}, u32[]{:S(2)}, u32[]{:S(2)}) collective-permute-start(bf16[64,32,128]{2,1,0:T(8,128)(2,1)S(1)} %all-to-all-done.mine_ref), channel_id=1, source_target_pairs={{0,1},{1,0},{2,3},{3,2},{4,5},{5,4},{6,7},{7,6},{8,9},{9,8},{10,11... | collective-permute-start | bytes 1572872 | tf_op jit(solution)/shard_map/ppermute | solution.py:556
  48.6 1.5 %collective-permute-done.7.other_ref = bf16[64,32,128]{2,1,0:T(8,128)(2,1)S(1)} collective-permute-done((bf16[64,32,128]{2,1,0:T(8,128)(2,1)S(1)}, bf16[64,32,128]{2,1,0:T(8,128)(2,1)S(1)}, u32[]{:S(2)}, u32[]{:S(2)}) %collective-permute-start.7) | collective-permute-done | bytes 524320 | tf_op jit(solution)/shard_map/ppermute | solution.py:556
  50.2 3.4 %shard_map.74 = f32[64,64,127]{2,1,0:T(8,128)} custom-call(s32[1]{0:T(128)} %bitcast.where_ref, bf16[63,64,128]{2,1,0:T(8,128)(2,1)S(1)} %fusion.pick_ref, bf16[64,32,128]{2,1,0:T(8,128)(2,1)S(1)} %all-to-all-done.mine_ref, bf16[64,32,128]{2,1,0:T(8,128)(2,1)S(1)} %collective-permute-done.7.other_ref), custom_call_target="tpu_custom_call" | custom-call | tf_op jit(solution)/shard_map/pallas_call | solution.py:478
  (2 shorter events, 0.0 us)
Async XLA Ops:
  2.6 13.6 %collective-permute-start = (bf16[5,8,8,128]{3,2,1,0:T(8,128)(2,1)S(1)}, bf16[5,8,8,128]{3,2,1,0:T(8,128)(2,1)S(1)}, u32[]{:S(2)}, u32[]{:S(2)}) collective-permute-start(bf16[5,8,8,128]{3,2,1,0:T(8,128)(2,1)S(1)} %get-tuple-element.25.side_ref), channel_id=1, source_target_pairs={{0,1},{1,2},{2,3},{3,4},{4,5},{5,6},{6,7},{7,0},{8,9},{9,10},{10,1... | collective-permute-start | bytes 245768 | tf_op jit(solution)/shard_map/ppermute | solution.py:507
  5.3 10.9 %collective-permute-start.1 = (bf16[5,8,8,128]{3,2,1,0:T(8,128)(2,1)S(1)}, bf16[5,8,8,128]{3,2,1,0:T(8,128)(2,1)S(1)}, u32[]{:S(2)}, u32[]{:S(2)}) collective-permute-start(bf16[5,8,8,128]{3,2,1,0:T(8,128)(2,1)S(1)} %get-tuple-element.25.side_ref), channel_id=1, source_target_pairs={{0,7},{1,0},{2,1},{3,2},{4,3},{5,4},{6,5},{7,6},{8,15},{9,8},{10,9... | collective-permute-start | bytes 245768 | tf_op jit(solution)/shard_map/ppermute | solution.py:507
  7.8 8.4 %collective-permute-start.2 = (bf16[72,128]{1,0:T(8,128)(2,1)S(1)}, bf16[72,128]{1,0:T(8,128)(2,1)S(1)}, u32[]{:S(2)}, u32[]{:S(2)}) collective-permute-start(bf16[72,128]{1,0:T(8,128)(2,1)S(1)} %get-tuple-element.27), channel_id=1, source_target_pairs={{0,8},{8,16},{16,24},{24,32},{32,40},{40,48},{48,56},{56,64},{64,7... | collective-permute-start | bytes 55304 | tf_op jit(solution)/shard_map/ppermute | solution.py:507
  9.5 6.7 %collective-permute-start.3 = (bf16[72,128]{1,0:T(8,128)(2,1)S(1)}, bf16[72,128]{1,0:T(8,128)(2,1)S(1)}, u32[]{:S(2)}, u32[]{:S(2)}) collective-permute-start(bf16[72,128]{1,0:T(8,128)(2,1)S(1)} %get-tuple-element.28), channel_id=1, source_target_pairs={{0,120},{8,0},{16,8},{24,16},{32,24},{40,32},{48,40},{56,48},{64,5... | collective-permute-start | bytes 55304 | tf_op jit(solution)/shard_map/ppermute | solution.py:507
  16.2 18.0 %copy-start = (s32[127,128]{1,0:T(8,128)S(1)}, s32[127,128]{1,0:T(8,128)}, u32[]{:S(2)}) copy-start(s32[127,128]{1,0:T(8,128)} %order_hbm.1) | copy-start | bytes 195076
  17.1 2.9 %collective-permute-start.4 = (f32[32,128]{1,0:T(8,128)S(1)}, f32[32,128]{1,0:T(8,128)S(1)}, u32[]{:S(2)}, u32[]{:S(2)}) collective-permute-start(f32[32,128]{1,0:T(8,128)S(1)} %get-tuple-element.30), channel_id=1, source_target_pairs={{0,1},{1,0},{2,3},{3,2},{4,5},{5,4},{6,7},{7,6},{8,9},{9,8},{10,11... | collective-permute-start | bytes 49160 | tf_op jit(solution)/shard_map/ppermute | solution.py:540
  21.0 26.5 %all-to-all-start = ((bf16[64,32,128]{2,1,0:T(8,128)(2,1)}), bf16[64,32,128]{2,1,0:T(8,128)(2,1)S(1)}, u32[]{:S(2)}, u32[]{:S(2)}) async-start(bf16[64,32,128]{2,1,0:T(8,128)(2,1)} %broadcast_in_dim.2), calls=%async_computation | async-start | bytes 1048576 | tf_op jit(solution)/shard_map/all_to_all | solution.py:547
  29.3 17.1 %collective-permute-start.5 = (bf16[131,8,128]{2,1,0:T(8,128)(2,1)S(1)}, bf16[131,8,128]{2,1,0:T(8,128)(2,1)S(1)}, u32[]{:S(2)}, u32[]{:S(2)}) collective-permute-start(bf16[131,8,128]{2,1,0:T(8,128)(2,1)S(1)} %get-tuple-element.36.high_ref), channel_id=1, source_target_pairs={{0,8},{8,16},{16,24},{24,32},{32,40},{40,48},{48,56},{56,64},{64,7... | collective-permute-start | bytes 804872 | tf_op jit(solution)/shard_map/ppermute | solution.py:507
  30.4 16.0 %collective-permute-start.6 = (bf16[131,8,128]{2,1,0:T(8,128)(2,1)S(1)}, bf16[131,8,128]{2,1,0:T(8,128)(2,1)S(1)}, u32[]{:S(2)}, u32[]{:S(2)}) collective-permute-start(bf16[131,8,128]{2,1,0:T(8,128)(2,1)S(1)} %get-tuple-element.35.low_ref), channel_id=1, source_target_pairs={{0,120},{8,0},{16,8},{24,16},{32,24},{40,32},{48,40},{56,48},{64,5... | collective-permute-start | bytes 804872 | tf_op jit(solution)/shard_map/ppermute | solution.py:507
  47.6 2.6 %collective-permute-start.7 = (bf16[64,32,128]{2,1,0:T(8,128)(2,1)S(1)}, bf16[64,32,128]{2,1,0:T(8,128)(2,1)S(1)}, u32[]{:S(2)}, u32[]{:S(2)}) collective-permute-start(bf16[64,32,128]{2,1,0:T(8,128)(2,1)S(1)} %all-to-all-done.mine_ref), channel_id=1, source_target_pairs={{0,1},{1,0},{2,3},{3,2},{4,5},{5,4},{6,7},{7,6},{8,9},{9,8},{10,11... | collective-permute-start | bytes 1572872 | tf_op jit(solution)/shard_map/ppermute | solution.py:556

commit v7 on v6

--- a/solution.py
+++ b/solution.py
@@ -84,10 +84,10 @@
     return jnp.where(sub_of(shape) == at, 1.0, 0.0)
 
 
-def edge_x_kernel(
+def edge_kernel(
     where_ref, table_hbm, class_hbm, cand_hbm, order_hbm, states_hbm,
-    low_ref, high_ref, to_minus_ref, to_plus_ref, own_ref, cells_ref, hits_ref,
-    states_ref, class_ref, cand_ref, order_ref, table_ref, wide_ref, weights_ref, product_ref, sem,
+    low_ref, high_ref, to_minus_ref, to_plus_ref, own_ref, cells_ref, hits_ref, side_ref, perm_ref, states_ref,
+    class_ref, cand_ref, order_ref, table_ref, wide_ref, weights_ref, product_ref, sem,
 ):
     tile = where_ref[0]
     core = tile % 2
@@ -99,15 +99,20 @@
     for n, at in enumerate(tiles):
         copies.append(pltpu.make_async_copy(cand_hbm.at[pl.ds(at, 1)], cand_ref.at[n], sem.at[2 + n]))
         copies.append(pltpu.make_async_copy(order_hbm.at[pl.ds(at // 2, 1)], order_ref.at[n], sem.at[5 + n]))
-    for n, rows in enumerate((pl.ds(0, 2), pl.ds(6, 2))):
-        copies.append(
-            pltpu.make_async_copy(states_hbm.at[:, :, :, rows], states_ref.at[:, :, :, rows], sem.at[8 + n])
-        )
+    for n in range(2):
+        half = pl.ds(32 * n, 32)
+        copies.append(pltpu.make_async_copy(states_hbm.at[:, half], states_ref.at[:, half], sem.at[8 + n]))
     for copy in copies:
         copy.start()
     for copy in copies[:8]:
         copy.wait()
-    wide_ref[pl.ds(0, 64), :] = look_up(class_ref[...], table_ref).reshape(FLAT)
+    perm = look_up(class_ref[...], table_ref)
+    perm_ref[...] = perm
+    first = jnp.broadcast_to(perm[:, :, 0:1], CUBE)
+    last = jnp.broadcast_to(perm[:, :, 127:128], CUBE)
+    for n, piece in enumerate(three_pieces(jnp.where(lane_of(CUBE) % 2 == 0, first, last))):
+        side_ref[2 + n] = piece
+    wide_ref[pl.ds(0, 64), :] = perm.reshape(FLAT)
     for ref, at in ((low_ref, 0), (high_ref, 7)):
         for n, piece in enumerate(three_pieces(wide_ref[pl.ds(at, 8, stride=8), :])):
             ref[128 + n] = piece
@@ -131,14 +136,22 @@
     at_high = jnp.where((own_zx >= 0) & (own_zx % 8 == 7), 1.0, 0.0)
     flag = sub_of(rows_of_z)
     flags = jnp.where(flag == 0, at_low, jnp.where(flag == 1, at_high, 0.0))
-    copies[8].wait()
-    copies[9].wait()
+    lane = lane_of(FLAT)
+    acc = [jnp.zeros(FLAT, F32), jnp.zeros(FLAT, F32)]
     for snap in range(64):
+        if snap % 32 == 0:
+            copies[8 + snap // 32].wait()
+        keep = (lane == 2 * snap) | (lane == (2 * snap + 127) % 128)
         for field in range(2):
             slot = (1 + field + 2 * snap) * 64
-            wide_ref[pl.ds(slot, 64), :] = states_ref[field, snap].astype(F32).reshape(FLAT)
+            value = states_ref[field, snap].astype(F32).reshape(FLAT)
+            acc[field] = jnp.where(keep, turn(value, 2 * snap), acc[field])
+            wide_ref[pl.ds(slot, 64), :] = value
             low_ref[field * 64 + snap] = wide_ref[pl.ds(slot, 8, stride=8), :].astype(BF16)
             high_ref[field * 64 + snap] = wide_ref[pl.ds(slot + 7, 8, stride=8), :].astype(BF16)
+
+    for field in range(2):
+        side_ref[field] = acc[field].reshape(CUBE).astype(BF16)
 
     def select(ref, weights, mask):
         for first, count in [(16 * n, 16) for n in range(8)] + [(128, 3)]:
@@ -165,37 +178,6 @@
     to_plus_ref[...] = pack(to_plus)
     own_ref[pl.ds(0, 136), :] = own_low + own_high
     own_ref[pl.ds(136, 8), :] = flags
-
-
-def edge_y_kernel(table_hbm, class_hbm, states_hbm, side_ref, perm_ref, states_ref, class_ref, table_ref, sem):
-    copies = [
-        pltpu.make_async_copy(table_hbm, table_ref, sem.at[0]),
-        pltpu.make_async_copy(class_hbm, class_ref, sem.at[1]),
-    ]
-    for n in range(2):
-        half = pl.ds(32 * n, 32)
-        copies.append(pltpu.make_async_copy(states_hbm.at[:, half], states_ref.at[:, half], sem.at[2 + n]))
-    for copy in copies:
-        copy.start()
-    copies[0].wait()
-    copies[1].wait()
-    perm = look_up(class_ref[...], table_ref)
-    perm_ref[...] = perm
-    first = jnp.broadcast_to(perm[:, :, 0:1], CUBE)
-    last = jnp.broadcast_to(perm[:, :, 127:128], CUBE)
-    for n, piece in enumerate(three_pieces(jnp.where(lane_of(CUBE) % 2 == 0, first, last))):
-        side_ref[2 + n] = piece
-    lane = lane_of(FLAT)
-    acc = [jnp.zeros(FLAT, F32), jnp.zeros(FLAT, F32)]
-    for snap in range(64):
-        if snap % 32 == 0:
-            copies[2 + snap // 32].wait()
-        keep = (lane == 2 * snap) | (lane == (2 * snap + 127) % 128)
-        for field in range(2):
-            value = states_ref[field, snap].astype(F32).reshape(FLAT)
-            acc[field] = jnp.where(keep, turn(value, 2 * snap), acc[field])
-    for field in range(2):
-        side_ref[field] = acc[field].reshape(CUBE).astype(BF16)
 
 
 def set_up_faces(perm, tx_ref, ty_ref, tz_ref, shift_ref):
@@ -403,19 +385,20 @@
 OWN = (144, 128)
 
 
-def edge_x_call(*operands):
+def edge_call(*operands):
     edge, slots = jax.ShapeDtypeStruct(EDGE, BF16), jax.ShapeDtypeStruct(SLOTS, BF16)
     shapes = [
         edge, edge, slots, slots, jax.ShapeDtypeStruct(OWN, F32),
         jax.ShapeDtypeStruct((256, 128), BF16), jax.ShapeDtypeStruct(FLAT, F32),
+        jax.ShapeDtypeStruct(SIDE, BF16), jax.ShapeDtypeStruct(CUBE, F32),
+        jax.ShapeDtypeStruct((2, 64, 8, 8, 128), BF16),
     ]
     return pl.pallas_call(
-        edge_x_kernel,
+        edge_kernel,
         in_specs=[SMEM] + [HBM] * 5,
         out_specs=[whole(one.shape) for one in shapes],
         out_shape=shapes,
         scratch_shapes=[
-            pltpu.VMEM((2, 64, 8, 8, 128), BF16),
             pltpu.VMEM(CUBE, jnp.int32),
             pltpu.VMEM((3, 1, 64), jnp.int32),
             pltpu.VMEM((3, 1, 128), jnp.int32),
@@ -497,8 +480,7 @@
         pltpu.with_memory_space_constraint(value, pltpu.HBM)
         for value in (states, class_map, perm_table, candidates.reshape(128, 64), merge_order)
     )
-    states_shape = (2, 64, 8, 8, 128)
-    low, high, to_minus, to_plus, own, cells, hits = edge_x_call(
+    low, high, to_minus, to_plus, own, cells, hits, side, perm, near_states = edge_call(
         where, perm_table, class_map, candidates, merge_rows, states
     )
 
@@ -509,24 +491,12 @@
     from_minus = shift(to_plus, "gx", 1)
     from_plus = shift(to_minus, "gx", -1)
 
-    side, perm, near_states = pl.pallas_call(
-        edge_y_kernel,
-        in_specs=[HBM, HBM, HBM],
-        out_specs=[whole(SIDE), whole(CUBE), whole(states_shape)],
-        out_shape=[
-            jax.ShapeDtypeStruct(SIDE, BF16),
-            jax.ShapeDtypeStruct(CUBE, F32),
-            jax.ShapeDtypeStruct(states_shape, BF16),
-        ],
-        scratch_shapes=[pltpu.VMEM(CUBE, jnp.int32), pltpu.SMEM((8,), F32), pltpu.SemaphoreType.DMA((4,))],
-        compiler_params=LIMIT,
-    )(perm_table, class_map, states)
     side_low = shift(side, "gy", 1)
     side_high = shift(side, "gy", -1)
 
     inner = pl.pallas_call(
         inner_kernel,
-        in_specs=[whole(CUBE), whole(states_shape)],
+        in_specs=[whole(CUBE), whole((2, 64, 8, 8, 128))],
         out_specs=whole((4096, 128)),
         out_shape=jax.ShapeDtypeStruct((4096, 128), F32),
         scratch_shapes=FACES,
@@ -543,15 +513,16 @@
     rest = (merged - lax.reduce_precision(merged, 8, 7)).astype(BF16)
     spread = jnp.broadcast_to(jnp.concatenate([top, rest], 1)[None], (64, 32, 128))
     peers = [[i * 8 + j * 2 + c for i in range(16) for j in range(4)] for c in range(2)]
-    spread, low, high, perm = lax.optimization_barrier((spread, low, high, perm))
+    spread, perm = lax.optimization_barrier((spread, perm))
     mine = lax.all_to_all(spread, ("gx", "gy"), 0, 0, axis_index_groups=peers)
 
     from_low = shift(high, "gx", 1)
     from_high = shift(low, "gx", -1)
     within = near_call(perm, side, side_low, side_high, states)
     flux = outer_call(within, low, high, from_low, from_high)
+    flux, orders = lax.optimization_barrier((flux, merge_order))
     numbers = lax.broadcasted_iota(jnp.int32, (63, 64, 128), 2)
-    picks = (merge_order[64:, :64, None] == numbers).astype(BF16)
+    picks = (orders[64:, :64, None] == numbers).astype(BF16)
     mine, flux, picks = lax.optimization_barrier((mine, flux, picks))
     other = lax.ppermute(mine, "gy", swap)
     kept = tree_call(where, picks, mine, other)

time: 53.8 us -> 50 us (0.929)
  waiting for transfers between devices: 10.2 us -> 7.28 us
  Pallas kernels: 15.8 us -> 14.3 us
    ppermute x6, waiting for transfers between devices: 7.77 us -> 0.02 us  [shift(): lax.ppermute(value, axis, [(i, (i + by) % count) for i in range(count)])]
    all_to_all x1, waiting for transfers between devices: 0.01 us -> 5.73 us  [local(): mine = lax.all_to_all(spread, ('gx', 'gy'), 0, 0, axis_index_groups=peers)]
    pallas_call x3 -> x2, Pallas kernels: 6.67 us -> 5.11 us  [the longest x1 2.87 us: edge_call(): pl.pallas_call(edge_kernel, in_specs=[SMEM] + [HBM] * 5, out_specs=[whole...]
    ppermute x1, starting transfers between devices: 1.08 us -> 2.6 us  [local(): other = lax.ppermute(mine, 'gy', swap)]
    ppermute x1, waiting for transfers between devices: 0.84 us -> 0.01 us  [local(): got_rows = lax.ppermute(send_rows, 'gy', swap)]
  transfers between devices with their start and end apart: 9 -> 9, of which waited for: 3 -> 2; matrix products, arithmetic and copies ran while one was open for 2% -> 4% of each run, Pallas kernels for 18% -> 14%
where the time goes in v7:
time: 50 us; the launch traced here: 49.8 us
  starting transfers between devices  25.6 us (51%)
  Pallas kernels  14.3 us (29%)
  waiting for transfers between devices  7.28 us (15%)
  other arithmetic  0.94 us (2%)
  local copies, waits for them, and re-layouts  0.88 us (2%)
  between operations  0.77 us (2%)
    ppermute x6, starting transfers between devices, shift(): lax.ppermute(value, axis, [(i, (i + by) % count) for i in range(count)])  13.2 us
    all_to_all x1, starting transfers between devices, local(): mine = lax.all_to_all(spread, ('gx', 'gy'), 0, 0, axis_index_groups=peers)  8.26 us
    all_to_all x1, waiting for transfers between devices, local(): mine = lax.all_to_all(spread, ('gx', 'gy'), 0, 0, axis_index_groups=peers)  5.73 us
    pallas_call x1, Pallas kernels, near_call(): pl.pallas_call(near_kernel, in_specs=[whole(CUBE)] + [whole(SIDE)] * 3 +...  3.6 us
    pallas_call x1, Pallas kernels, tree_call(): pl.pallas_call(tree_kernel, in_specs=[SMEM, whole((63, 64, 128)), whole((...  3.39 us
    pallas_call x1, Pallas kernels, edge_call(): pl.pallas_call(edge_kernel, in_specs=[SMEM] + [HBM] * 5, out_specs=[whole...  2.87 us
    ppermute x1, starting transfers between devices, local(): other = lax.ppermute(mine, 'gy', swap)  2.6 us
    pallas_call x1, Pallas kernels, local(): pl.pallas_call(inner_kernel, in_specs=[whole(CUBE), whole((2, 64, 8, 8, 1...  2.24 us
  transfers between devices with their start and end apart: 9, of which 2 were waited for; matrix products, arithmetic and copies ran while one was open for 4% of the time, Pallas kernels for 14%

profile of v7, /device:TPU:1, one launch (start us, length us, event | category | flops | bytes accessed | tf_op | source)
XLA Modules:
  0.0 49.8 jit_solution(5136908510117699472)
XLA Ops:
  0.6 2.9 %shard_map.68 = (bf16[131,8,128]{2,1,0:T(8,128)(2,1)S(1)}, bf16[131,8,128]{2,1,0:T(8,128)(2,1)S(1)}, bf16[72,128]{1,0:T(8,128)(2,1)S(1)}, bf16[72,128]{1,0:T(8,1...) custom-call(s32[1]{0:T(128)} %bitcast.where_ref, ...), custom_call_target="tpu_custom_call" | custom-call | tf_op jit(solution)/shard_map/pallas_call | solution.py:396
  3.5 1.4 %collective-permute-start.1 = (bf16[5,8,8,128]{3,2,1,0:T(8,128)(2,1)S(1)}, bf16[5,8,8,128]{3,2,1,0:T(8,128)(2,1)S(1)}, u32[]{:S(2)}, u32[]{:S(2)}) collective-permute-start(bf16[5,8,8,128]{3,2,1,0:T(8,128)(2,1)S(1)} %get-tuple-element.25.side_ref), channel_id=1, source_target_pairs={{0,7},{1,0},{2,1},{3,2},{4,3},{5,4},{6,5},{7,6},{8,15},{9,8},{10,9... | collective-permute-start | bytes 245768 | tf_op jit(solution)/shard_map/ppermute | solution.py:489
  4.9 1.3 %collective-permute-start = (bf16[5,8,8,128]{3,2,1,0:T(8,128)(2,1)S(1)}, bf16[5,8,8,128]{3,2,1,0:T(8,128)(2,1)S(1)}, u32[]{:S(2)}, u32[]{:S(2)}) collective-permute-start(bf16[5,8,8,128]{3,2,1,0:T(8,128)(2,1)S(1)} %get-tuple-element.25.side_ref), channel_id=1, source_target_pairs={{0,1},{1,2},{2,3},{3,4},{4,5},{5,6},{6,7},{7,0},{8,9},{9,10},{10,1... | collective-permute-start | bytes 245768 | tf_op jit(solution)/shard_map/ppermute | solution.py:489
  6.2 1.6 %collective-permute-start.2 = (bf16[72,128]{1,0:T(8,128)(2,1)S(1)}, bf16[72,128]{1,0:T(8,128)(2,1)S(1)}, u32[]{:S(2)}, u32[]{:S(2)}) collective-permute-start(bf16[72,128]{1,0:T(8,128)(2,1)S(1)} %get-tuple-element.27), channel_id=1, source_target_pairs={{0,8},{8,16},{16,24},{24,32},{32,40},{40,48},{48,56},{56,64},{64,7... | collective-permute-start | bytes 55304 | tf_op jit(solution)/shard_map/ppermute | solution.py:489
  7.9 4.3 %collective-permute-start.3 = (bf16[72,128]{1,0:T(8,128)(2,1)S(1)}, bf16[72,128]{1,0:T(8,128)(2,1)S(1)}, u32[]{:S(2)}, u32[]{:S(2)}) collective-permute-start(bf16[72,128]{1,0:T(8,128)(2,1)S(1)} %get-tuple-element.28), channel_id=1, source_target_pairs={{0,120},{8,0},{16,8},{24,16},{32,24},{40,32},{48,40},{56,48},{64,5... | collective-permute-start | bytes 55304 | tf_op jit(solution)/shard_map/ppermute | solution.py:489
  12.2 2.2 %shard_map.69.inner_ref = f32[4096,128]{1,0:T(8,128)S(1)} custom-call(f32[8,8,128]{2,1,0:T(8,128)S(1)} %get-tuple-element.32.perm_ref, bf16[2,64,8,8,128]{4,3,2,1,0:T(8,128)(2,1)S(1)} %get-tuple-element.22.states_ref), custom_call_target="tpu_custom_call" | custom-call | tf_op jit(solution)/shard_map/pallas_call | solution.py:497
  14.4 0.0 collective-permute-done.2.from_minus_ref
  14.5 0.0 collective-permute-done.3.from_plus_ref
  14.5 0.0 collective-permute-done.1.side_high_ref
  14.5 0.0 collective-permute-done.side_low_ref
  14.5 1.0 %shard_map.70 = (f32[32,128]{1,0:T(8,128)S(1)}, f32[32,128]{1,0:T(8,128)S(1)}) custom-call(f32[4096,128]{1,0:T(8,128)S(1)} %shard_map.69.inner_ref, bf16[256,128]{1,0:T(8,128)(2,1)S(1)} %get-tuple-element.23.cells_ref, f32[64,128]{1,0:T(8,128)S(1)} %get-tuple-element.24.hits_ref, bf16[5,8,8,128]{3,2,1,0:T(8,128)(2,1)S(1)} %get-tuple-element.25.side_ref, ...), custom_call_target="tpu_custom_call" | custom-call | tf_op jit(solution)/shard_map/pallas_call | solution.py:416
  15.5 1.6 %collective-permute-start.4 = (f32[32,128]{1,0:T(8,128)S(1)}, f32[32,128]{1,0:T(8,128)S(1)}, u32[]{:S(2)}, u32[]{:S(2)}) collective-permute-start(f32[32,128]{1,0:T(8,128)S(1)} %get-tuple-element.30), channel_id=1, source_target_pairs={{0,1},{1,0},{2,3},{3,2},{4,5},{5,4},{6,7},{7,6},{8,9},{9,8},{10,11... | collective-permute-start | bytes 49160 | tf_op jit(solution)/shard_map/ppermute | solution.py:510
  17.0 4.5 %collective-permute-start.6 = (bf16[131,8,128]{2,1,0:T(8,128)(2,1)S(1)}, bf16[131,8,128]{2,1,0:T(8,128)(2,1)S(1)}, u32[]{:S(2)}, u32[]{:S(2)}) collective-permute-start(bf16[131,8,128]{2,1,0:T(8,128)(2,1)S(1)} %get-tuple-element.33.low_ref), channel_id=1, source_target_pairs={{0,120},{8,0},{16,8},{24,16},{32,24},{40,32},{48,40},{56,48},{64,5... | collective-permute-start | bytes 804872 | tf_op jit(solution)/shard_map/ppermute | solution.py:489
  21.6 0.0 collective-permute-start.5
  21.6 0.0 collective-permute-done.4
  21.6 0.1 pad_maximum_fusion
  21.7 0.9 %broadcast_in_dim.2 = bf16[64,32,128]{2,1,0:T(8,128)(2,1)} broadcast(bf16[32,128]{1,0:T(8,128)(2,1)S(1)} %pad_maximum_fusion), dimensions={1,2} | broadcast | bytes 532480 | tf_op jit(solution)/shard_map/broadcast_in_dim | solution.py:514
  22.5 8.3 %all-to-all-start = ((bf16[64,32,128]{2,1,0:T(8,128)(2,1)}), bf16[64,32,128]{2,1,0:T(8,128)(2,1)S(1)}, u32[]{:S(2)}, u32[]{:S(2)}) async-start(bf16[64,32,128]{2,1,0:T(8,128)(2,1)} %broadcast_in_dim.2), calls=%async_computation | async-start | bytes 1048576 | tf_op jit(solution)/shard_map/all_to_all | solution.py:517
  30.8 3.6 %shard_map.71.within_ref = f32[4096,128]{1,0:T(8,128)S(1)} custom-call(f32[8,8,128]{2,1,0:T(8,128)S(1)} %get-tuple-element.32.perm_ref, bf16[5,8,8,128]{3,2,1,0:T(8,128)(2,1)S(1)} %get-tuple-element.25.side_ref, bf16[5,8,8,128]{3,2,1,0:T(8,128)(2,1)S(1)} %collective-permute-done.side_low_ref, ...), custom_call_target="tpu_custom_call" | custom-call | tf_op jit(solution)/shard_map/pallas_call | solution.py:433
  34.4 0.0 copy-start
  34.4 0.0 collective-permute-done.6.from_high_ref
  34.4 0.0 collective-permute-done.5.from_low_ref
  34.4 1.2 %shard_map.72 = bf16[64,8,8,128]{3,2,1,0:T(8,128)(2,1)} custom-call(f32[4096,128]{1,0:T(8,128)S(1)} %shard_map.71.within_ref, bf16[131,8,128]{2,1,0:T(8,128)(2,1)S(1)} %get-tuple-element.33.low_ref, bf16[131,8,128]{2,1,0:T(8,128)(2,1)S(1)} %get-tuple-element.34.high_ref, bf16[131,8,128]{2,1,0:T(8,128)(2,1)S(1)} %collective-permute-done.5.from_low_ref, ...), custom_call_target="tpu_custom_call" | custom-call | tf_op jit(solution)/shard_map/pallas_call | solution.py:446
  35.6 0.0 copy-done
  35.7 0.8 %fusion.pick_ref = bf16[63,64,128]{2,1,0:T(8,128)(2,1)S(1)} fusion(s32[63,64]{1,0:T(8,128)S(1)} %slice.11), kind=kLoop, calls=%fused_computation.1 | loop fusion | flops 1032192 | bytes 1048320 | tf_op jit(solution)/shard_map/convert_element_type | solution.py:525
  36.5 5.7 %all-to-all-done.mine_ref = bf16[64,32,128]{2,1,0:T(8,128)(2,1)S(1)} async-done(((bf16[64,32,128]{2,1,0:T(8,128)(2,1)}), bf16[64,32,128]{2,1,0:T(8,128)(2,1)S(1)}, u32[]{:S(2)}, u32[]{:S(2)}) %all-to-all-start) | async-done | bytes 524320 | tf_op jit(solution)/shard_map/all_to_all | solution.py:517
  42.2 2.6 %collective-permute-start.7 = (bf16[64,32,128]{2,1,0:T(8,128)(2,1)S(1)}, bf16[64,32,128]{2,1,0:T(8,128)(2,1)S(1)}, u32[]{:S(2)}, u32[]{:S(2)}) collective-permute-start(bf16[64,32,128]{2,1,0:T(8,128)(2,1)S(1)} %all-to-all-done.mine_ref), channel_id=1, source_target_pairs={{0,1},{1,0},{2,3},{3,2},{4,5},{5,4},{6,7},{7,6},{8,9},{9,8},{10,11... | collective-permute-start | bytes 1572872 | tf_op jit(solution)/shard_map/ppermute | solution.py:527
  44.8 1.5 %collective-permute-done.7.other_ref = bf16[64,32,128]{2,1,0:T(8,128)(2,1)S(1)} collective-permute-done((bf16[64,32,128]{2,1,0:T(8,128)(2,1)S(1)}, bf16[64,32,128]{2,1,0:T(8,128)(2,1)S(1)}, u32[]{:S(2)}, u32[]{:S(2)}) %collective-permute-start.7) | collective-permute-done | bytes 524320 | tf_op jit(solution)/shard_map/ppermute | solution.py:527
  46.4 3.4 %shard_map.73 = f32[64,64,127]{2,1,0:T(8,128)} custom-call(s32[1]{0:T(128)} %bitcast.where_ref, bf16[63,64,128]{2,1,0:T(8,128)(2,1)S(1)} %fusion.pick_ref, bf16[64,32,128]{2,1,0:T(8,128)(2,1)S(1)} %all-to-all-done.mine_ref, bf16[64,32,128]{2,1,0:T(8,128)(2,1)S(1)} %collective-permute-done.7.other_ref), custom_call_target="tpu_custom_call" | custom-call | tf_op jit(solution)/shard_map/pallas_call | solution.py:461
  (2 shorter events, 0.0 us)
Async XLA Ops:
  3.5 11.0 %collective-permute-start.1 = (bf16[5,8,8,128]{3,2,1,0:T(8,128)(2,1)S(1)}, bf16[5,8,8,128]{3,2,1,0:T(8,128)(2,1)S(1)}, u32[]{:S(2)}, u32[]{:S(2)}) collective-permute-start(bf16[5,8,8,128]{3,2,1,0:T(8,128)(2,1)S(1)} %get-tuple-element.25.side_ref), channel_id=1, source_target_pairs={{0,7},{1,0},{2,1},{3,2},{4,3},{5,4},{6,5},{7,6},{8,15},{9,8},{10,9... | collective-permute-start | bytes 245768 | tf_op jit(solution)/shard_map/ppermute | solution.py:489
  4.9 9.5 %collective-permute-start = (bf16[5,8,8,128]{3,2,1,0:T(8,128)(2,1)S(1)}, bf16[5,8,8,128]{3,2,1,0:T(8,128)(2,1)S(1)}, u32[]{:S(2)}, u32[]{:S(2)}) collective-permute-start(bf16[5,8,8,128]{3,2,1,0:T(8,128)(2,1)S(1)} %get-tuple-element.25.side_ref), channel_id=1, source_target_pairs={{0,1},{1,2},{2,3},{3,4},{4,5},{5,6},{6,7},{7,0},{8,9},{9,10},{10,1... | collective-permute-start | bytes 245768 | tf_op jit(solution)/shard_map/ppermute | solution.py:489
  6.2 8.2 %collective-permute-start.2 = (bf16[72,128]{1,0:T(8,128)(2,1)S(1)}, bf16[72,128]{1,0:T(8,128)(2,1)S(1)}, u32[]{:S(2)}, u32[]{:S(2)}) collective-permute-start(bf16[72,128]{1,0:T(8,128)(2,1)S(1)} %get-tuple-element.27), channel_id=1, source_target_pairs={{0,8},{8,16},{16,24},{24,32},{32,40},{40,48},{48,56},{56,64},{64,7... | collective-permute-start | bytes 55304 | tf_op jit(solution)/shard_map/ppermute | solution.py:489
  7.9 6.6 %collective-permute-start.3 = (bf16[72,128]{1,0:T(8,128)(2,1)S(1)}, bf16[72,128]{1,0:T(8,128)(2,1)S(1)}, u32[]{:S(2)}, u32[]{:S(2)}) collective-permute-start(bf16[72,128]{1,0:T(8,128)(2,1)S(1)} %get-tuple-element.28), channel_id=1, source_target_pairs={{0,120},{8,0},{16,8},{24,16},{32,24},{40,32},{48,40},{56,48},{64,5... | collective-permute-start | bytes 55304 | tf_op jit(solution)/shard_map/ppermute | solution.py:489
  15.5 6.1 %collective-permute-start.4 = (f32[32,128]{1,0:T(8,128)S(1)}, f32[32,128]{1,0:T(8,128)S(1)}, u32[]{:S(2)}, u32[]{:S(2)}) collective-permute-start(f32[32,128]{1,0:T(8,128)S(1)} %get-tuple-element.30), channel_id=1, source_target_pairs={{0,1},{1,0},{2,3},{3,2},{4,5},{5,4},{6,7},{7,6},{8,9},{9,8},{10,11... | collective-permute-start | bytes 49160 | tf_op jit(solution)/shard_map/ppermute | solution.py:510
  17.0 17.4 %collective-permute-start.6 = (bf16[131,8,128]{2,1,0:T(8,128)(2,1)S(1)}, bf16[131,8,128]{2,1,0:T(8,128)(2,1)S(1)}, u32[]{:S(2)}, u32[]{:S(2)}) collective-permute-start(bf16[131,8,128]{2,1,0:T(8,128)(2,1)S(1)} %get-tuple-element.33.low_ref), channel_id=1, source_target_pairs={{0,120},{8,0},{16,8},{24,16},{32,24},{40,32},{48,40},{56,48},{64,5... | collective-permute-start | bytes 804872 | tf_op jit(solution)/shard_map/ppermute | solution.py:489
  21.6 12.9 %collective-permute-start.5 = (bf16[131,8,128]{2,1,0:T(8,128)(2,1)S(1)}, bf16[131,8,128]{2,1,0:T(8,128)(2,1)S(1)}, u32[]{:S(2)}, u32[]{:S(2)}) collective-permute-start(bf16[131,8,128]{2,1,0:T(8,128)(2,1)S(1)} %get-tuple-element.34.high_ref), channel_id=1, source_target_pairs={{0,8},{8,16},{16,24},{24,32},{32,40},{40,48},{48,56},{56,64},{64,7... | collective-permute-start | bytes 804872 | tf_op jit(solution)/shard_map/ppermute | solution.py:489
  22.5 19.7 %all-to-all-start = ((bf16[64,32,128]{2,1,0:T(8,128)(2,1)}), bf16[64,32,128]{2,1,0:T(8,128)(2,1)S(1)}, u32[]{:S(2)}, u32[]{:S(2)}) async-start(bf16[64,32,128]{2,1,0:T(8,128)(2,1)} %broadcast_in_dim.2), calls=%async_computation | async-start | bytes 1048576 | tf_op jit(solution)/shard_map/all_to_all | solution.py:517
  34.4 1.2 %copy-start = (s32[127,128]{1,0:T(8,128)S(1)}, s32[127,128]{1,0:T(8,128)}, u32[]{:S(2)}) copy-start(s32[127,128]{1,0:T(8,128)} %order_hbm.1) | copy-start | bytes 195076
  42.2 4.1 %collective-permute-start.7 = (bf16[64,32,128]{2,1,0:T(8,128)(2,1)S(1)}, bf16[64,32,128]{2,1,0:T(8,128)(2,1)S(1)}, u32[]{:S(2)}, u32[]{:S(2)}) collective-permute-start(bf16[64,32,128]{2,1,0:T(8,128)(2,1)S(1)} %all-to-all-done.mine_ref), channel_id=1, source_target_pairs={{0,1},{1,0},{2,3},{3,2},{4,5},{5,4},{6,7},{7,6},{8,9},{9,8},{10,11... | collective-permute-start | bytes 1572872 | tf_op jit(solution)/shard_map/ppermute | solution.py:527

commit v8 on v5

--- a/solution.py
+++ b/solution.py
@@ -230,43 +230,21 @@
     rows_ref[...] = sum_of_eights(picked_ref)
 
 
-def outer_kernel(
-    within_ref, rows_ref, cells_ref, hits_ref, low_ref, high_ref, from_low_ref, from_high_ref,
-    out_hbm, mine_ref, send_ref, out_ref, edge_ref, qx_ref, picked_ref, sem,
+def outer_rows_kernel(
+    rows_ref, cells_ref, hits_ref, low_ref, high_ref, from_low_ref, from_high_ref,
+    mine_ref, send_ref, qx_ref, picked_ref,
 ):
     t_low = trans(perm_of(low_ref, 128), perm_of(from_low_ref, 128))
     t_high = trans(perm_of(high_ref, 128), perm_of(from_high_ref, 128))
-    edge_ref[...] = jnp.zeros_like(edge_ref)
 
     def edge(own_ref, other_ref, t, snap):
         s_here, s_next = own_ref[64 + snap].astype(F32), other_ref[64 + snap].astype(F32)
         p_here, p_next = own_ref[snap].astype(F32), other_ref[snap].astype(F32)
         return face(t, s_here * s_here, s_next * s_next, p_here, p_next)
 
-    def put(part):
-        span = pl.ds(part * 32, 32)
-        return pltpu.make_async_copy(out_ref.at[span], out_hbm.at[span], sem.at[part])
-
-    def group(number, carry):
-        for k in range(16):
-            snap = number * 16 + k
-            q_low = edge(low_ref, from_low_ref, t_low, snap)
-            q_high = edge(high_ref, from_high_ref, t_high, snap)
-            at = pl.multiple_of(snap * 16, 16)
-            qx_ref[pl.ds(at, 8), :] = q_low
-            qx_ref[pl.ds(at + 8, 8), :] = q_high
-            edge_ref[pl.ds(k * 64, 8, stride=8), :] = q_low
-            edge_ref[pl.ds(k * 64 + 7, 8, stride=8), :] = q_high
-        for k in range(16):
-            snap = number * 16 + k
-            flux = within_ref[pl.ds(pl.multiple_of(snap * 64, 64), 64), :] + edge_ref[pl.ds(k * 64, 64), :]
-            out_ref[snap] = flux.reshape(CUBE).astype(BF16)
-        return carry
-
-    for part in range(2):
-        lax.fori_loop(2 * part, 2 * part + 2, group, 0)
-        put(part).start()
-
+    for snap in range(64):
+        qx_ref[pl.ds(snap * 16, 8), :] = edge(low_ref, from_low_ref, t_low, snap)
+        qx_ref[pl.ds(snap * 16 + 8, 8), :] = edge(high_ref, from_high_ref, t_high, snap)
     hit_low, hit_high = hits_ref[pl.ds(0, 8, stride=8), :], hits_ref[pl.ds(7, 8, stride=8), :]
     for part in range(4):
         rows = matmul(two_pieces(qx_ref[pl.ds(part * 256, 256), :]), cells_ref[...])
@@ -278,6 +256,29 @@
     rows = jnp.transpose(jnp.concatenate([total, jnp.zeros(FLAT, F32)], 0))
     mine_ref[...] = rows[:32]
     send_ref[...] = rows[32:64]
+
+
+def outer_flux_kernel(within_ref, qx_ref, out_hbm, out_ref, edge_ref, sem):
+    edge_ref[...] = jnp.zeros_like(edge_ref)
+
+    def put(part):
+        span = pl.ds(part * 32, 32)
+        return pltpu.make_async_copy(out_ref.at[span], out_hbm.at[span], sem.at[part])
+
+    def group(number, carry):
+        for k in range(16):
+            at = pl.multiple_of((number * 16 + k) * 16, 16)
+            edge_ref[pl.ds(k * 64, 8, stride=8), :] = qx_ref[pl.ds(at, 8), :]
+            edge_ref[pl.ds(k * 64 + 7, 8, stride=8), :] = qx_ref[pl.ds(at + 8, 8), :]
+        for k in range(16):
+            snap = number * 16 + k
+            flux = within_ref[pl.ds(pl.multiple_of(snap * 64, 64), 64), :] + edge_ref[pl.ds(k * 64, 64), :]
+            out_ref[snap] = flux.reshape(CUBE).astype(BF16)
+        return carry
+
+    for part in range(2):
+        lax.fori_loop(2 * part, 2 * part + 2, group, 0)
+        put(part).start()
     for part in range(2):
         put(part).wait()
 
@@ -334,21 +335,27 @@
     )(*operands)
 
 
-def outer_call(*operands):
+def outer_rows_call(*operands):
+    rows = jax.ShapeDtypeStruct((32, 128), F32)
     return pl.pallas_call(
-        outer_kernel,
-        in_specs=[whole((4096, 128)), whole(FLAT), whole((256, 128)), whole(FLAT)] + [whole(EDGE)] * 4,
-        out_specs=[HBM, whole((32, 128)), whole((32, 128))],
-        out_shape=[
-            jax.ShapeDtypeStruct((64, 8, 8, 128), BF16),
-            jax.ShapeDtypeStruct((32, 128), F32),
-            jax.ShapeDtypeStruct((32, 128), F32),
-        ],
+        outer_rows_kernel,
+        in_specs=[whole(FLAT), whole((256, 128)), whole(FLAT)] + [whole(EDGE)] * 4,
+        out_specs=[whole((32, 128)), whole((32, 128)), whole((1024, 128))],
+        out_shape=[rows, rows, jax.ShapeDtypeStruct((1024, 128), F32)],
+        scratch_shapes=[pltpu.VMEM((512, 128), F32)],
+        compiler_params=LIMIT,
+    )(*operands)
+
+
+def outer_flux_call(*operands):
+    return pl.pallas_call(
+        outer_flux_kernel,
+        in_specs=[whole((4096, 128)), whole((1024, 128))],
+        out_specs=HBM,
+        out_shape=jax.ShapeDtypeStruct((64, 8, 8, 128), BF16),
         scratch_shapes=[
             pltpu.VMEM((64, 8, 8, 128), BF16),
             pltpu.VMEM((1024, 128), F32),
-            pltpu.VMEM((1024, 128), F32),
-            pltpu.VMEM((512, 128), F32),
             pltpu.SemaphoreType.DMA((2,)),
         ],
         compiler_params=LIMIT,
@@ -439,10 +446,12 @@
     inner, picks = lax.optimization_barrier((inner, picks))
 
     within, part_rows = middle_call(inner, cells, hits, side, side_low, side_high)
-    flux, mine_rows, send_rows = outer_call(within, part_rows, cells, hits, low, high, from_low, from_high)
+    mine_rows, send_rows, q_x = outer_rows_call(part_rows, cells, hits, low, high, from_low, from_high)
 
     swap = [(i, i ^ 1) for i in range(8)]
     got_rows = lax.ppermute(send_rows, "gy", swap)
+    flux = outer_flux_call(within, q_x)
+    flux, got_rows = lax.optimization_barrier((flux, got_rows))
     merged = mine_rows[:, :64] + got_rows[:, :64]
     top = merged.astype(BF16)
     rest = (merged - lax.reduce_precision(merged, 8, 7)).astype(BF16)

time: 47.6 us -> 47.2 us (level)
  waiting for transfers between devices: 3.06 us -> 2.22 us
    ppermute x1, waiting for transfers between devices: 0.84 us -> 0.01 us  [local(): got_rows = lax.ppermute(send_rows, 'gy', swap)]
    pallas_call x1 -> x2, Pallas kernels: 1.2 us -> 1.62 us  [the longest x1 1.16 us: outer_flux_call(): pl.pallas_call(outer_flux_kernel, in_specs=[whole((4096, 128)), whole((10...]
  transfers between devices with their start and end apart: 6 -> 6, of which waited for: 3 -> 2; matrix products, arithmetic and copies ran while one was open for 2% -> 2% of each run, Pallas kernels for 12% -> 15%
where the time goes in v8:
time: 47.2 us; the launch traced here: 47 us
  blocking collectives  18.4 us (39%)
  Pallas kernels  12.6 us (27%)
  starting transfers between devices  12.1 us (26%)
  waiting for transfers between devices  2.22 us (5%)
  other arithmetic  0.94 us (2%)
  between operations  0.73 us (2%)
    all_to_all x1, blocking collectives, local(): mine = lax.all_to_all(spread, ('gx', 'gy'), 0, 0, axis_index_groups=peers)  18.4 us
    ppermute x4, starting transfers between devices, shift(): lax.ppermute(value, axis, [(i, (i + by) % count) for i in range(count)])  9.08 us
    pallas_call x1, Pallas kernels, tree_call(): pl.pallas_call(tree_kernel, in_specs=[SMEM, whole((63, 64, 128)), whole((...  3.39 us
    pallas_call x1, Pallas kernels, local(): pl.pallas_call(edge_y_kernel, in_specs=[SMEM] + [HBM] * 5, out_specs=[who...  2.69 us
    pallas_call x1, Pallas kernels, local(): pl.pallas_call(inner_kernel, in_specs=[whole(CUBE), whole(states_shape)],...  2.3 us
    ppermute x1, starting transfers between devices, local(): other = lax.ppermute(mine, 'gy', swap)  1.83 us
    pallas_call x1, Pallas kernels, local(): pl.pallas_call(edge_x_kernel, in_specs=[HBM, HBM, HBM], out_specs=[whole(...  1.71 us
    ppermute x1, waiting for transfers between devices, local(): other = lax.ppermute(mine, 'gy', swap)  1.54 us
  transfers between devices with their start and end apart: 6, of which 2 were waited for; matrix products, arithmetic and copies ran while one was open for 2% of the time, Pallas kernels for 15%

profile of v8, /device:TPU:1, one launch (start us, length us, event | category | flops | bytes accessed | tf_op | source)
XLA Modules:
  0.0 47.0 jit_solution(10648372493250992952)
XLA Ops:
  0.6 0.0 copy-start
  0.6 1.7 %shard_map.71 = (bf16[131,8,128]{2,1,0:T(8,128)(2,1)S(1)}, bf16[131,8,128]{2,1,0:T(8,128)(2,1)S(1)}) custom-call(f32[8]{0:T(128)} %table_hbm.3, s32[8,8,128]{2,1,0:T(8,128)} %class_hbm.3, bf16[2,64,8,8,128]{4,3,2,1,0:T(8,128)(2,1)} %states_hbm.3), custom_call_target="tpu_custom_call" | custom-call | tf_op jit(solution)/shard_map/pallas_call | solution.py:390
  2.4 2.5 %collective-permute-start.2 = (bf16[131,8,128]{2,1,0:T(8,128)(2,1)S(1)}, bf16[131,8,128]{2,1,0:T(8,128)(2,1)S(1)}, u32[]{:S(2)}, u32[]{:S(2)}) collective-permute-start(bf16[131,8,128]{2,1,0:T(8,128)(2,1)S(1)} %get-tuple-element.27.high_ref), channel_id=1, source_target_pairs={{0,8},{8,16},{16,24},{24,32},{32,40},{40,48},{48,56},{56,64},{64,7... | collective-permute-start | bytes 804872 | tf_op jit(solution)/shard_map/ppermute | solution.py:403
  4.9 4.4 %collective-permute-start.3 = (bf16[131,8,128]{2,1,0:T(8,128)(2,1)S(1)}, bf16[131,8,128]{2,1,0:T(8,128)(2,1)S(1)}, u32[]{:S(2)}, u32[]{:S(2)}) collective-permute-start(bf16[131,8,128]{2,1,0:T(8,128)(2,1)S(1)} %get-tuple-element.26.low_ref), channel_id=1, source_target_pairs={{0,120},{8,0},{16,8},{24,16},{32,24},{40,32},{48,40},{56,48},{64,5... | collective-permute-start | bytes 804872 | tf_op jit(solution)/shard_map/ppermute | solution.py:403
  9.3 2.7 %shard_map.68 = (bf16[5,8,8,128]{3,2,1,0:T(8,128)(2,1)S(1)}, f32[8,8,128]{2,1,0:T(8,128)S(1)}, bf16[2,64,8,8,128]{4,3,2,1,0:T(8,128)(2,1)S(1)}, bf16[256,128]{1,0:T(8,128)(2,1)S(1)}, f32[64,128]{1,0:T(8,128)S(1)}) custom-call(s32[1]{0:T(128)} %bitcast.where_ref, f32[8]{0:T(128)} %table_hbm.3, s32[8,8,128]{2,1,0:T(8,128)} %class_hbm.3, s32[128,64]{1,0:T(8,128)} %bitcast.4, ...), custom_call_target="tpu_custom_call" | custom-call | tf_op jit(solution)/shard_map/pallas_call | solution.py:408
  12.0 2.1 %collective-permute-start = (bf16[5,8,8,128]{3,2,1,0:T(8,128)(2,1)S(1)}, bf16[5,8,8,128]{3,2,1,0:T(8,128)(2,1)S(1)}, u32[]{:S(2)}, u32[]{:S(2)}) collective-permute-start(bf16[5,8,8,128]{3,2,1,0:T(8,128)(2,1)S(1)} %get-tuple-element.23.side_ref), channel_id=1, source_target_pairs={{0,1},{1,2},{2,3},{3,4},{4,5},{5,6},{6,7},{7,0},{8,9},{9,10},{10,1... | collective-permute-start | bytes 245768 | tf_op jit(solution)/shard_map/ppermute | solution.py:403
  14.1 0.0 collective-permute-start.1
  14.1 0.0 copy-done
  14.2 0.8 %fusion.pick_ref = bf16[63,64,128]{2,1,0:T(8,128)(2,1)S(1)} fusion(s32[63,64]{1,0:T(8,128)S(1)} %slice.9), kind=kLoop, calls=%fused_computation.1 | loop fusion | flops 1032192 | bytes 1048320 | tf_op jit(solution)/shard_map/convert_element_type | solution.py:445
  15.0 2.3 %shard_map.69.inner_ref = f32[4096,128]{1,0:T(8,128)S(1)} custom-call(f32[8,8,128]{2,1,0:T(8,128)S(1)} %get-tuple-element.18.perm_ref, bf16[2,64,8,8,128]{4,3,2,1,0:T(8,128)(2,1)S(1)} %get-tuple-element.19.states_ref), custom_call_target="tpu_custom_call" | custom-call | tf_op jit(solution)/shard_map/pallas_call | solution.py:431
  17.3 0.0 collective-permute-done.side_low_ref
  17.3 0.7 %collective-permute-done.1.side_high_ref = bf16[5,8,8,128]{3,2,1,0:T(8,128)(2,1)S(1)} collective-permute-done((bf16[5,8,8,128]{3,2,1,0:T(8,128)(2,1)S(1)}, bf16[5,8,8,128]{3,2,1,0:T(8,128)(2,1)S(1)}, u32[]{:S(2)}, u32[]{:S(2)}) %collective-permute-start.1) | collective-permute-done | bytes 81952 | tf_op jit(solution)/shard_map/ppermute | solution.py:403
  18.0 0.9 %shard_map.70 = (f32[4096,128]{1,0:T(8,128)S(1)}, f32[64,128]{1,0:T(8,128)S(1)}) custom-call(f32[4096,128]{1,0:T(8,128)S(1)} %shard_map.69.inner_ref, bf16[256,128]{1,0:T(8,128)(2,1)S(1)} %get-tuple-element.21.cells_ref, f32[64,128]{1,0:T(8,128)S(1)} %get-tuple-element.22.hits_ref, bf16[5,8,8,128]{3,2,1,0:T(8,128)(2,1)S(1)} %get-tuple-element.23.side_ref, ...), custom_call_target="tpu_custom_call" | custom-call | tf_op jit(solution)/shard_map/pallas_call | solution.py:328
  18.9 0.0 collective-permute-done.2.from_low_ref
  18.9 0.0 collective-permute-done.3.from_high_ref
  18.9 0.5 shard_map.72
  19.4 1.1 %collective-permute-start.4 = (f32[32,128]{1,0:T(8,128)S(1)}, f32[32,128]{1,0:T(8,128)S(1)}, u32[]{:S(2)}, u32[]{:S(2)}) collective-permute-start(f32[32,128]{1,0:T(8,128)S(1)} %get-tuple-element.29), channel_id=1, source_target_pairs={{0,1},{1,0},{2,3},{3,2},{4,5},{5,4},{6,7},{7,6},{8,9},{9,8},{10,11... | collective-permute-start | bytes 49160 | tf_op jit(solution)/shard_map/ppermute | solution.py:452
  20.6 1.2 %shard_map.73 = bf16[64,8,8,128]{3,2,1,0:T(8,128)(2,1)} custom-call(f32[4096,128]{1,0:T(8,128)S(1)} %get-tuple-element.24.within_ref, f32[1024,128]{1,0:T(8,128)S(1)} %get-tuple-element.28.qx_ref), custom_call_target="tpu_custom_call" | custom-call | tf_op jit(solution)/shard_map/pallas_call | solution.py:351
  21.7 0.0 collective-permute-done.4
  21.7 0.1 pad_maximum_fusion
  21.8 0.1 broadcast_in_dim.2
  21.9 18.4 %all_to_all.5.mine_ref = bf16[64,32,128]{2,1,0:T(8,128)(2,1)S(1)} all-to-all(bf16[64,32,128]{2,1,0:T(8,128)(2,1)S(1)} %broadcast_in_dim.2), channel_id=1, replica_groups={{0,2,4,6,8,10,12,14,16,18,20,22,24,26,28,30,32,34,36,38,40,42,44,46,48,..., dimensions={0} | all-to-all | bytes 1048576 | tf_op jit(solution)/shard_map/all_to_all | solution.py:460
  40.3 1.8 %collective-permute-start.5 = (bf16[64,32,128]{2,1,0:T(8,128)(2,1)S(1)}, bf16[64,32,128]{2,1,0:T(8,128)(2,1)S(1)}, u32[]{:S(2)}, u32[]{:S(2)}) collective-permute-start(bf16[64,32,128]{2,1,0:T(8,128)(2,1)S(1)} %all_to_all.5.mine_ref), channel_id=1, source_target_pairs={{0,1},{1,0},{2,3},{3,2},{4,5},{5,4},{6,7},{7,6},{8,9},{9,8},{10,11... | collective-permute-start | bytes 1572872 | tf_op jit(solution)/shard_map/ppermute | solution.py:461
  42.1 1.5 %collective-permute-done.5.other_ref = bf16[64,32,128]{2,1,0:T(8,128)(2,1)S(1)} collective-permute-done((bf16[64,32,128]{2,1,0:T(8,128)(2,1)S(1)}, bf16[64,32,128]{2,1,0:T(8,128)(2,1)S(1)}, u32[]{:S(2)}, u32[]{:S(2)}) %collective-permute-start.5) | collective-permute-done | bytes 524320 | tf_op jit(solution)/shard_map/ppermute | solution.py:461
  43.6 3.4 %shard_map.74 = f32[64,64,127]{2,1,0:T(8,128)} custom-call(s32[1]{0:T(128)} %bitcast.where_ref, bf16[63,64,128]{2,1,0:T(8,128)(2,1)S(1)} %fusion.pick_ref, bf16[64,32,128]{2,1,0:T(8,128)(2,1)S(1)} %all_to_all.5.mine_ref, bf16[64,32,128]{2,1,0:T(8,128)(2,1)S(1)} %collective-permute-done.5.other_ref), custom_call_target="tpu_custom_call" | custom-call | tf_op jit(solution)/shard_map/pallas_call | solution.py:366
  (2 shorter events, 0.0 us)
Async XLA Ops:
  0.6 13.5 %copy-start = (s32[127,128]{1,0:T(8,128)S(1)}, s32[127,128]{1,0:T(8,128)}, u32[]{:S(2)}) copy-start(s32[127,128]{1,0:T(8,128)} %order_hbm.1) | copy-start | bytes 195076
  2.4 16.6 %collective-permute-start.2 = (bf16[131,8,128]{2,1,0:T(8,128)(2,1)S(1)}, bf16[131,8,128]{2,1,0:T(8,128)(2,1)S(1)}, u32[]{:S(2)}, u32[]{:S(2)}) collective-permute-start(bf16[131,8,128]{2,1,0:T(8,128)(2,1)S(1)} %get-tuple-element.27.high_ref), channel_id=1, source_target_pairs={{0,8},{8,16},{16,24},{24,32},{32,40},{40,48},{48,56},{56,64},{64,7... | collective-permute-start | bytes 804872 | tf_op jit(solution)/shard_map/ppermute | solution.py:403
  4.9 14.0 %collective-permute-start.3 = (bf16[131,8,128]{2,1,0:T(8,128)(2,1)S(1)}, bf16[131,8,128]{2,1,0:T(8,128)(2,1)S(1)}, u32[]{:S(2)}, u32[]{:S(2)}) collective-permute-start(bf16[131,8,128]{2,1,0:T(8,128)(2,1)S(1)} %get-tuple-element.26.low_ref), channel_id=1, source_target_pairs={{0,120},{8,0},{16,8},{24,16},{32,24},{40,32},{48,40},{56,48},{64,5... | collective-permute-start | bytes 804872 | tf_op jit(solution)/shard_map/ppermute | solution.py:403
  12.0 5.3 %collective-permute-start = (bf16[5,8,8,128]{3,2,1,0:T(8,128)(2,1)S(1)}, bf16[5,8,8,128]{3,2,1,0:T(8,128)(2,1)S(1)}, u32[]{:S(2)}, u32[]{:S(2)}) collective-permute-start(bf16[5,8,8,128]{3,2,1,0:T(8,128)(2,1)S(1)} %get-tuple-element.23.side_ref), channel_id=1, source_target_pairs={{0,1},{1,2},{2,3},{3,4},{4,5},{5,6},{6,7},{7,0},{8,9},{9,10},{10,1... | collective-permute-start | bytes 245768 | tf_op jit(solution)/shard_map/ppermute | solution.py:403
  14.1 3.9 %collective-permute-start.1 = (bf16[5,8,8,128]{3,2,1,0:T(8,128)(2,1)S(1)}, bf16[5,8,8,128]{3,2,1,0:T(8,128)(2,1)S(1)}, u32[]{:S(2)}, u32[]{:S(2)}) collective-permute-start(bf16[5,8,8,128]{3,2,1,0:T(8,128)(2,1)S(1)} %get-tuple-element.23.side_ref), channel_id=1, source_target_pairs={{0,7},{1,0},{2,1},{3,2},{4,3},{5,4},{6,5},{7,6},{8,15},{9,8},{10,9... | collective-permute-start | bytes 245768 | tf_op jit(solution)/shard_map/ppermute | solution.py:403
  19.4 2.3 %collective-permute-start.4 = (f32[32,128]{1,0:T(8,128)S(1)}, f32[32,128]{1,0:T(8,128)S(1)}, u32[]{:S(2)}, u32[]{:S(2)}) collective-permute-start(f32[32,128]{1,0:T(8,128)S(1)} %get-tuple-element.29), channel_id=1, source_target_pairs={{0,1},{1,0},{2,3},{3,2},{4,5},{5,4},{6,7},{7,6},{8,9},{9,8},{10,11... | collective-permute-start | bytes 49160 | tf_op jit(solution)/shard_map/ppermute | solution.py:452
  40.3 3.4 %collective-permute-start.5 = (bf16[64,32,128]{2,1,0:T(8,128)(2,1)S(1)}, bf16[64,32,128]{2,1,0:T(8,128)(2,1)S(1)}, u32[]{:S(2)}, u32[]{:S(2)}) collective-permute-start(bf16[64,32,128]{2,1,0:T(8,128)(2,1)S(1)} %all_to_all.5.mine_ref), channel_id=1, source_target_pairs={{0,1},{1,0},{2,3},{3,2},{4,5},{5,4},{6,7},{7,6},{8,9},{9,8},{10,11... | collective-permute-start | bytes 1572872 | tf_op jit(solution)/shard_map/ppermute | solution.py:461
